TPU v7x, 256 devices: a whole 4x4x8 slice. The times are simulated.
256 devices in a mesh: branch: 2 (over core), prow: 16 (over x, z_lo), pcol: 8 (over z_hi, y).
Axes of the slice: x: 4, y: 4, z: 8 (z_hi: 2, z_lo: 4; z = z_hi * 4 + z_lo), core: 2. Of those that a mesh axis runs over, the one named last changes fastest.
Arguments:
- pair_rep: float32 [256, 256, 128], P(('branch', 'prow'), 'pcol'), may hold values from -6 to 6
- alignment: float32 [32, 256, 256], P('pcol', ('branch', 'prow')), may hold values from -6 to 6
- residue_mask: int32 [256], replicated, may hold values 0 or 1
- row_mask: int32 [32, 256], P('pcol', ('branch', 'prow')), may hold values 0 or 1
- attention_in: float32 [256, 1024], replicated, may hold values from -0.375 to 0.375
- pair_bias_w: float32 [128, 8], replicated, may hold values from -40 to 40
- attention_out: float32 [256, 256], replicated, may hold values from -0.375 to 0.375
- outer_in: float32 [256, 64], replicated, may hold values from -0.375 to 0.375
- outer_out: float32 [1024, 128], replicated, may hold values from -0.1875 to 0.1875
- triangle_in: float32 [128, 512], replicated, may hold values from -0.5 to 0.5
- triangle_gate: float32 [128, 128], replicated, may hold values from -0.5 to 0.5
- triangle_out: float32 [128, 128], replicated, may hold values from -0.5 to 0.5
- transit_in: float32 [128, 512], replicated, may hold values from -0.5 to 0.5
- transit_out: float32 [512, 128], replicated, may hold values from -0.25 to 0.25
Outputs:
- new_alignment: float32 [32, 256, 256], P('pcol', ('branch', 'prow'))
- new_pair: float32 [256, 256, 128], P(('branch', 'prow'), 'pcol')
All inputs are finite; a program needn't handle non-finite values. No bound on the sum of `row_mask` on one device may be relied on, other than what follows from the above.
Results may differ from a plain program's by a relative error of at most 0.0003.
Values sent between devices are 32-bit elements; how exact they have to be, the bound alone decides.
No kernel may reach another device: no remote copies, remote signals or barrier semaphores. Data moves between devices by JAX's collectives and lax.ppermute only.
A program may use at most 64 MiB of HBM per device.

v0:
```python
import jax
import jax.numpy as jnp
from jax import lax
from jax.sharding import PartitionSpec as P

highest = lax.Precision.HIGHEST
epsilon = 1e-05


def layer_norm(values):
    center = values - jnp.mean(values, axis=-1, keepdims=True)
    spread = jnp.mean(center * center, axis=-1, keepdims=True)
    return center * lax.rsqrt(spread + epsilon)


def matmul(left_side, right_side):
    return jnp.dot(left_side, right_side, precision=highest, preferred_element_type=jnp.float32)


def outer_block(left_rows, right_cols, outer_out):
    product = jnp.einsum("sip,sjq->ijpq", left_rows, right_cols, precision=highest)
    row_total, col_total, left_width, right_width = product.shape
    return matmul(product.reshape(row_total, col_total, left_width * right_width), outer_out)


def shards(
    pair_rep,
    alignment,
    residue_mask,
    row_mask,
    attention_in,
    pair_bias_w,
    attention_out,
    outer_in,
    outer_out,
    triangle_in,
    triangle_gate,
    triangle_out,
    transit_in,
    transit_out,
):
    row_count, col_count, _ = pair_rep.shape
    seq_count = alignment.shape[0]
    head_count = pair_bias_w.shape[1]
    att_width = attention_out.shape[0]
    head_depth = att_width // head_count
    outer_width = outer_in.shape[1] // 2
    inner_width = triangle_out.shape[0]
    row_start = lax.axis_index(("branch", "prow")) * row_count
    col_start = lax.axis_index("pcol") * col_count
    pair_norm = layer_norm(pair_rep)
    bias_tile = jnp.einsum("ijc,ch->hij", pair_norm, pair_bias_w, precision=highest)
    bias_rows = lax.all_gather(bias_tile, "pcol", axis=2, tiled=True)
    normed = layer_norm(alignment)
    mask_float = row_mask.astype(jnp.float32)
    key_bias = 1000000000.0 * (mask_float - 1.0)
    queries = matmul(normed, attention_in[:, :att_width]) * head_depth ** (-0.5)
    queries = queries.reshape(seq_count, row_count, head_count, head_depth)
    gate_logits = matmul(normed, attention_in[:, 3 * att_width :])
    key_value_w = attention_in[:, att_width : 3 * att_width]
    key_value_local = matmul(normed, key_value_w)
    widen = lambda sent_block: sent_block
    running_max = jnp.full((seq_count, head_count, row_count), -1e30, jnp.float32)
    make_sent_block = lax.all_gather(key_value_local, ("branch", "prow"), axis=1, tiled=True)
    block_bias = lax.all_gather(key_bias, ("branch", "prow"), axis=1, tiled=True)
    key_value = widen(make_sent_block)
    key_count = block_bias.shape[1]
    key_block = key_value[..., :att_width].reshape(seq_count, key_count, head_count, head_depth)
    value_block = key_value[..., att_width:].reshape(seq_count, key_count, head_count, head_depth)
    scores = jnp.einsum("sihd,sjhd->shij", queries, key_block, precision=highest)
    scores = scores + bias_rows[None] + block_bias[:, None, None, :]
    block_max = jnp.maximum(running_max, jnp.max(scores, axis=-1))
    weights = jnp.exp(scores - block_max[..., None])
    running_sum = jnp.sum(weights, axis=-1)
    accumulated = jnp.einsum("shij,sjhd->shid", weights, value_block, precision=highest)
    final_state = (block_max, running_sum, accumulated)
    _, running_sum, accumulated = final_state
    mixed = accumulated / running_sum[..., None]
    mixed = jnp.transpose(mixed, (0, 2, 1, 3)).reshape(seq_count, row_count, att_width)
    new_alignment = alignment + matmul(mixed * jax.nn.sigmoid(gate_logits), attention_out)
    factors = matmul(layer_norm(new_alignment), outer_in) * mask_float[..., None]
    left_outer = factors[..., :outer_width]
    right_outer = factors[..., outer_width:]
    right_all, mask_all = (
        lax.all_gather(right_outer, ("branch", "prow"), axis=1, tiled=True),
        lax.all_gather(mask_float, ("branch", "prow"), axis=1, tiled=True),
    )
    res_count = right_all.shape[1]
    block_count = res_count // col_count
    right_blocks = jnp.transpose(
        right_all.reshape(seq_count, block_count, col_count, outer_width), (1, 0, 2, 3)
    )
    outer_part = lax.map(
        lambda right_cols: outer_block(left_outer, right_cols, outer_out), right_blocks
    )
    count_part = jnp.einsum(
        "si,sbj->bij",
        mask_float,
        mask_all.reshape(seq_count, block_count, col_count),
        precision=highest,
    )
    outer_tile, count_tile = (
        lax.psum_scatter(outer_part, "pcol", scatter_dimension=0, tiled=True),
        lax.psum_scatter(count_part, "pcol", scatter_dimension=0, tiled=True),
    )
    outer_sum = outer_tile[0]
    count_sum = count_tile[0]
    outer_mean = outer_sum / (1.0 + count_sum)[..., None]
    pair_one = pair_rep + outer_mean
    tri_norm = layer_norm(pair_one)
    res_float = residue_mask.astype(jnp.float32)
    row_valid = lax.dynamic_slice_in_dim(res_float, row_start, row_count)
    col_valid = lax.dynamic_slice_in_dim(res_float, col_start, col_count)
    pair_valid = (row_valid[:, None] * col_valid[None, :])[..., None]
    edges = matmul(tri_norm, triangle_in)
    left_edge = (
        jax.nn.sigmoid(edges[..., :inner_width])
        * edges[..., inner_width : 2 * inner_width]
        * pair_valid
    )
    right_edge = (
        jax.nn.sigmoid(edges[..., 2 * inner_width : 3 * inner_width])
        * edges[..., 3 * inner_width :]
        * pair_valid
    )
    cross_part = jnp.einsum(
        "ikc,jkc->ijc",
        left_edge,
        lax.all_gather(right_edge, ("branch", "prow"), axis=0, tiled=True),
        precision=highest,
    )
    crossed = lax.psum_scatter(cross_part, "pcol", scatter_dimension=1, tiled=True)
    triangle = matmul(layer_norm(crossed), triangle_out) * jax.nn.sigmoid(
        matmul(tri_norm, triangle_gate)
    )
    pair_mid = pair_one + triangle
    hidden_units = jax.nn.relu(matmul(layer_norm(pair_mid), transit_in))
    new_pair = pair_mid + matmul(hidden_units, transit_out)
    return (new_alignment, new_pair)


def solution(mesh):
    return jax.shard_map(
        shards,
        mesh=mesh,
        in_specs=(
            P(("branch", "prow"), "pcol", None),
            P("pcol", ("branch", "prow"), None),
            P(),
            P("pcol", ("branch", "prow")),
            P(),
            P(),
            P(),
            P(),
            P(),
            P(),
            P(),
            P(),
            P(),
            P(),
        ),
        out_specs=(P("pcol", ("branch", "prow"), None), P(("branch", "prow"), "pcol", None)),
        check_vma=False,
    )
```

profile of v0, /device:TPU:2, one launch (start us, length us, event | category | flops | bytes accessed | tf_op | source)
XLA Modules:
  0.0 662.0 jit_solution(16955762189528096668)
XLA Ops:
  16.4 48.7 %all_gather.19 = f32[8,8,256]{1,0,2:T(8,128)S(1)} all-gather(f32[8,8,32]{1,0,2:T(8,128)S(1)} %copy.82), channel_id=1, replica_groups=mesh['branch'=2,'prow'=16,'pcol'=8] {'pcol'}, dimensions={2}, use_global_device_ids=true | all-gather | bytes 73728 | tf_op jit(solution)/shard_map/all_gather | solution.py:53
  65.5 67.1 %all-gather = f32[32,8,4]{1,2,0:T(4,128)S(1)} all-gather(f32[1,8,4]{1,2,0:T(4,128)S(1)} %multiply_bitcast_fusion), channel_id=1, replica_groups=mesh['branch'=2,'prow'=16,'pcol'=8] {'branch','prow'}, dimensions={0}, use_global_device_ids=true | all-gather | bytes 4224 | tf_op jit(solution)/shard_map/all_gather | solution.py:65
  142.6 69.7 %all_gather.21 = f32[4,256,32]{2,1,0:T(8,128)S(1)} all-gather(f32[4,8,32]{2,1,0:T(8,128)S(1)} %get-tuple-element.72), channel_id=1, replica_groups=mesh['branch'=2,'prow'=16,'pcol'=8] {'branch','prow'}, dimensions={1}, use_global_device_ids=true | all-gather | bytes 135168 | tf_op jit(solution)/shard_map/all_gather | solution.py:85
  212.7 128.6 %while.10 = (s32[]{:T(128)}, f32[8,8,32,128]{3,2,1,0:T(8,128)}, f32[8,4,32,32]{3,1,2,0:T(4,128)S(1)}, f32[4,8,32]{2,0,1:T(4,128)S(1)}, f32[1024,128]{1,0:T(8,128)S(1)}, /*index=5*/s32[]{:T(128)}) while((s32[]{:T(128)}, f32[8,8,32,128]{3,2,1,0:T(8,128)}, f32[8,4,32,32]{3,1,2,0:T(4,128)S(1)}, f32[4,8,32]{2,0,1:T(4,128)S(1)}, ...), condition=%wide.region_9.10_spmd, body=%wide.region_8.9_spmd.sunk | while | flops 415236096 | bytes 7029321 | solution.py:93
  212.7 5.1 convolution_bitcast_fusion.7
  217.8 5.6 copy.113
  223.4 3.7 reshape.165
  228.8 5.0 convolution_bitcast_fusion.7
  233.8 5.6 copy.113
  239.5 3.7 reshape.165
  244.9 5.0 convolution_bitcast_fusion.7
  249.9 5.6 copy.113
  260.9 5.0 convolution_bitcast_fusion.7
  266.0 5.6 copy.113
  271.6 3.7 reshape.165
  277.0 5.0 convolution_bitcast_fusion.7
  282.0 5.6 copy.113
  287.7 3.7 reshape.165
  293.1 5.0 convolution_bitcast_fusion.7
  298.1 5.6 copy.113
  303.7 3.7 reshape.165
  309.1 5.0 convolution_bitcast_fusion.7
  314.2 5.6 copy.113
  319.8 3.7 reshape.165
  325.2 5.0 convolution_bitcast_fusion.7
  330.2 5.6 copy.113
  341.4 69.0 %all-gather.1 = f32[32,8,4]{1,2,0:T(4,128)S(1)} all-gather(f32[1,8,4]{1,2,0:T(4,128)S(1)} %get-tuple-element.74), channel_id=1, replica_groups=mesh['branch'=2,'prow'=16,'pcol'=8] {'branch','prow'}, dimensions={0}, use_global_device_ids=true | all-gather | bytes 4224 | tf_op jit(solution)/shard_map/all_gather | solution.py:86
  411.5 54.2 %all-reduce = f32[8,8,32]{2,1,0:T(8,128)S(1)} all-reduce(f32[8,8,32]{2,1,0:T(8,128)S(1)} %convolution_bitcast_fusion.4), channel_id=3, replica_groups=mesh['branch'=2,'prow'=16,'pcol'=8] {'pcol'}, use_global_device_ids=true, to_apply=%region_11.12.clone | all-reduce | flops 2048 | bytes 16384
  469.7 59.8 %all-gather.7.cloned.1.call-done = f32[256,32,128]{2,1,0:T(8,128)} async-done(((f32[8,32,128]{2,1,0:T(8,128)}), f32[256,32,128]{2,1,0:T(8,128)}) %all-gather.7.cloned.1.call-update) | async-done | bytes 4194320 | tf_op jit(solution)/shard_map/all_gather | solution.py:129
  529.5 14.4 %copy.91 = f32[256,32,128]{1,0,2:T(8,128)} copy(f32[256,32,128]{2,1,0:T(8,128)} %all-gather.7.cloned.1.call-done) | data formatting | bytes 8388608 | tf_op jit(solution)/shard_map/all_gather | solution.py:129
  543.9 17.5 %convolution_bitcast_fusion.2 = f32[8,256,128]{1,0,2:T(8,128)S(1)} fusion(f32[256,32,128]{1,0,2:T(8,128)} %copy.91, f32[8,32,128]{1,0,2:T(8,128)S(1)} %copy.92), kind=kOutput, calls=%fused_computation.8 | convolution fusion | flops 100663296 | bytes 5373952 | tf_op jit(solution)/shard_map/ikc,jkc->ijc/dot_general | solution.py:126
  563.3 86.3 %reduce-scatter.5.cloned.1.call-done = f32[8,32,128]{2,0,1:T(8,128)} async-done(((f32[8,256,128]{2,0,1:T(8,128)}), f32[8,32,128]{2,0,1:T(8,128)}) %reduce-scatter.5.cloned.1.call-update) | async-done | bytes 131088 | tf_op jit(solution)/shard_map/reduce_scatter | solution.py:132
  (117 shorter events, 53.2 us)
Async XLA Ops:
  7.2 460.6 %copy-start = (f32[128,512]{1,0:T(8,128)S(1)}, f32[128,512]{1,0:T(8,128)}, u32[]{:S(2)}) copy-start(f32[128,512]{1,0:T(8,128)} %param.25) | copy-start | bytes 786436
  7.2 58.3 %copy-start.8 = (s32[4,8]{1,0:T(4,128)S(1)}, s32[4,8]{1,0:T(4,128)}, u32[]{:S(2)}) copy-start(s32[4,8]{1,0:T(4,128)} %param.19) | copy-start | bytes 388
  7.2 125.5 %all-gather.5.cloned.1.call-start = ((), (), s32[]{:S(2)}) async-start(), calls=%async_computation.2 | async-start | bytes 2162688 | tf_op jit(solution)/shard_map/all_gather | solution.py:64
  11.2 455.3 %reduce-scatter.3.cloned.1.call-start = ((), (), s32[]{:S(2)}) async-start(), calls=%async_computation.3 | async-start | bytes 1179648 | tf_op jit(solution)/shard_map/reduce_scatter | solution.py:103
  135.5 4.1 copy-start.3
  135.5 6.8 %copy-start.10 = (f32[256,64]{0,1:T(8,128)S(1)}, f32[256,64]{0,1:T(8,128)}, u32[]{:S(2)}) copy-start(f32[256,64]{0,1:T(8,128)} %param.23) | copy-start | bytes 196612
  137.1 75.6 %copy-start.1 = (f32[1024,128]{1,0:T(8,128)S(1)}, f32[1024,128]{1,0:T(8,128)}, u32[]{:S(2)}) copy-start(f32[1024,128]{1,0:T(8,128)} %param.24) | copy-start | bytes 1572868
  142.1 70.6 %copy-start.6 = (f32[4,8,256]{2,1,0:T(8,128)}, f32[4,8,256]{2,1,0:T(8,128)S(1)}, u32[]{:S(2)}) copy-start(f32[4,8,256]{2,1,0:T(8,128)S(1)} %get-tuple-element.78) | copy-start | bytes 98308
  212.7 197.9 %copy-start.9 = (s32[256]{0:T(256)S(1)}, s32[256]{0:T(256)}, u32[]{:S(2)}) copy-start(s32[256]{0:T(256)} %param.18) | copy-start | bytes 3076
  212.7 198.0 %copy-start.12 = (u32[256]{0:T(256)S(1)}, u32[256]{0:T(256)}, u32[]{:S(2)}) copy-start(u32[256]{0:T(256)} %constant.77) | copy-start | bytes 3076
  212.7 253.8 %copy-start.2 = (f32[8,32,128]{2,1,0:T(8,128)S(1)}, f32[8,32,128]{2,1,0:T(8,128)}, u32[]{:S(2)}) copy-start(f32[8,32,128]{2,1,0:T(8,128)} %param.16) | copy-start | bytes 393220
  341.3 188.2 %all-gather.7.cloned.1.call-start = ((), (), s32[]{:S(2)}) async-start(), calls=%async_computation.4 | async-start | bytes 4325376 | tf_op jit(solution)/shard_map/all_gather | solution.py:129
  469.2 180.4 %reduce-scatter.5.cloned.1.call-start = ((), (), s32[]{:S(2)}) async-start(), calls=%async_computation.5 | async-start | bytes 1179648 | tf_op jit(solution)/shard_map/reduce_scatter | solution.py:132
  543.9 19.1 %copy-start.11 = (f32[128,128]{1,0:T(8,128)S(1)}, f32[128,128]{1,0:T(8,128)}, u32[]{:S(2)}) copy-start(f32[128,128]{1,0:T(8,128)} %param.26) | copy-start | bytes 196612
  561.4 91.6 %copy-start.7 = (f32[128,128]{1,0:T(8,128)S(1)}, f32[128,128]{1,0:T(8,128)}, u32[]{:S(2)}) copy-start(f32[128,128]{1,0:T(8,128)} %param.27) | copy-start | bytes 196612
  561.4 92.2 %copy-start.4 = (f32[128,512]{1,0:T(8,128)S(1)}, f32[128,512]{1,0:T(8,128)}, u32[]{:S(2)}) copy-start(f32[128,512]{1,0:T(8,128)} %param.28) | copy-start | bytes 786436
  561.4 92.8 %copy-start.5 = (f32[512,128]{1,0:T(8,128)S(1)}, f32[512,128]{1,0:T(8,128)}, u32[]{:S(2)}) copy-start(f32[512,128]{1,0:T(8,128)} %param.29) | copy-start | bytes 786436
Sparse Core Ops, SparseCore 0:
  11.3 65.9 all-gather.4
  341.4 93.1 reduce-scatter.2
  469.3 60.1 all-gather.6
  563.1 86.4 reduce-scatter.4
where the time goes:
time: 664 us; the launch traced here: 662 us
  blocking collectives  309 us (47%)
  waiting for transfers between devices  146 us (22%)
  local copies, waits for them, and re-layouts  98.2 us (15%)
  matrix products  83.8 us (13%)
  between operations  14.2 us (2%)
  other arithmetic  10.4 us (2%)
    reduce_scatter x1, waiting for transfers between devices, shards(): lax.psum_scatter(cross_part, 'pcol', scatter_dimension=1, tiled=True)  86.3 us
    all_gather x1, blocking collectives, shards(): lax.all_gather(right_outer, ('branch', 'prow'), axis=1, tiled=True)  69.7 us
    all_gather x1, blocking collectives, shards(): lax.all_gather(mask_float, ('branch', 'prow'), axis=1, tiled=True)  69 us
    all_gather x1, blocking collectives, shards(): lax.all_gather(key_bias, ('branch', 'prow'), axis=1, tiled=True)  67.1 us
    all_gather x1, waiting for transfers between devices, shards(): lax.all_gather(right_edge, ('branch', 'prow'), axis=0, tiled=True)  59.8 us
    unnamed x1, blocking collectives  54.2 us
    all_gather x1, blocking collectives, shards(): bias_rows = lax.all_gather(bias_tile, 'pcol', axis=2, tiled=True)  48.7 us
    transpose x8, local copies, waits for them, and re-layouts, outer_block(): jnp.einsum('sip,sjq->ijpq', left_rows, right_cols, precision=highest)  45.1 us
  transfers between devices with their start and end apart: 4, of which 2 were waited for; matrix products, arithmetic and copies ran while one was open for 1% of the time, Pallas kernels for 0%

commit v1 on v0

v1 whole, which is shorter than its diff:
```python
import functools

import jax
import jax.numpy as jnp
from jax import lax
from jax.experimental import pallas as pl
from jax.experimental.pallas import tpu as pltpu
from jax.sharding import PartitionSpec as P

highest = lax.Precision.HIGHEST
epsilon = 1e-05
f32 = jnp.float32
bf16 = jnp.bfloat16

ROWS = ("branch", "prow")
CHIPS = ("prow", "pcol")
NN = (((1,), (0,)), ((), ()))
NT = (((1,), (1,)), ((), ()))


def layer_norm(values, axis=-1):
    center = values - jnp.mean(values, axis=axis, keepdims=True)
    spread = jnp.mean(center * center, axis=axis, keepdims=True)
    return center * lax.rsqrt(spread + epsilon)


def split(value):
    high = value.astype(bf16)
    low = (value - high.astype(f32)).astype(bf16)
    return high, low


def dot3(left, right, dims=NN):
    left_high, left_low = split(left)
    right_high, right_low = split(right)
    one = functools.partial(lax.dot_general, dimension_numbers=dims, preferred_element_type=f32)
    return one(left_high, right_high) + (one(left_high, right_low) + one(left_low, right_high))


def dot6(left, right, dims=NN):
    return lax.dot_general(left, right, dims, precision=highest, preferred_element_type=f32)


def iota(shape, axis):
    return lax.broadcasted_iota(jnp.int32, shape, axis)


def call(kernel, out_shapes, scratch=(), scalars=0, name=None):
    vmem = pl.BlockSpec(memory_space=pltpu.VMEM)
    smem = pl.BlockSpec(memory_space=pltpu.SMEM)

    def run(*args):
        return pl.pallas_call(
            kernel,
            out_shape=[jax.ShapeDtypeStruct(shape, f32) for shape in out_shapes],
            in_specs=[smem] * scalars + [vmem] * (len(args) - scalars),
            out_specs=[vmem] * len(out_shapes),
            scratch_shapes=list(scratch),
            name=name,
        )(*args)

    return run


def send_kernel(place, pair, align, mask, bias_w, x_send, bias_send):
    pair_norm = layer_norm(pair[...])
    bias = dot6(bias_w[...].T, pair_norm, NT)
    for peer in range(bias_send.shape[0]):
        bias_send[peer] = bias
    normed = layer_norm(align[...])
    lane = iota((8, 256), 1)
    spread = ((lane % 8 == iota((8, 256), 0)) & (lane // 8 == place[0])).astype(f32)
    mask_tile = lax.dot_general(mask[...], spread, NN, preferred_element_type=f32)
    for peer in range(x_send.shape[0]):
        x_send[peer, 0:32] = normed
        x_send[peer, 32:40] = mask_tile


def query_kernel(align, proj, query_out, gate_out):
    normed = layer_norm(align[...])
    query = dot6(normed, proj[:, 0:256]) * 32 ** (-0.5)
    gate_out[...] = jax.nn.sigmoid(dot3(normed, proj[:, 768:1024]))
    own_head = iota((32, 8, 256), 1) == iota((32, 8, 256), 2) // 32
    wide = jnp.where(own_head, jnp.broadcast_to(query[:, None, :], (32, 8, 256)), 0.0)
    query_out[...] = dot6(wide.reshape(256, 256), proj[:, 256:512], NT)


def attend_kernel(
    x_all, bias_all, query, gate, align, mask, mask_col, value_w, out_w, outer_w, new_align, right_send, left_mask, bias_s, mix_s
):
    lane = iota((8, 128), 1)
    chunk = lane // 32
    for i in range(8):
        half, place = divmod(i, 4)
        for group in range(2):
            tile = jnp.zeros((8, 128), f32)
            for c in range(4):
                source = bias_all[group * 4 + c, :, half * 128 : half * 128 + 128]
                shift = ((c - place) * 32) % 128
                if shift:
                    source = pltpu.roll(source, shift, 1)
                tile = jnp.where(chunk == c, source, tile)
            bias_s[i * 8 : i * 8 + 8, group * 128 : group * 128 + 128] = tile
    keys = x_all[0, 32:40, :]
    for r in range(1, 32):
        keys = keys + x_all[r, 32:40, :]
    key_bias = 1000000000.0 * (keys - 1.0)
    for s in range(4):
        x_row = x_all[:, s * 8 : s * 8 + 8, :].reshape(256, 256)
        scores = dot6(query[s * 64 : s * 64 + 64, :], x_row, NT)
        scores = (scores + bias_s[...]) + key_bias[s : s + 1, :]
        weights = jnp.exp(scores - jnp.max(scores, axis=-1, keepdims=True))
        total = jnp.sum(weights, axis=-1, keepdims=True)
        mix_s[s * 64 : s * 64 + 64, :] = dot3(weights, x_row) / total
    values = dot3(mix_s[...], value_w[...]).reshape(32, 8, 256)
    own_head = iota((32, 8, 256), 1) == iota((32, 8, 256), 2) // 32
    mixed = jnp.sum(jnp.where(own_head, values, 0.0), axis=1)
    updated = align[...] + dot3(mixed * gate[...], out_w[...])
    new_align[...] = updated
    factors = dot3(layer_norm(updated), outer_w[...]) * mask_col[...]
    wide_lane = iota((64, 256), 1)
    expand = (iota((64, 256), 0) == wide_lane % 32 + 32 * (wide_lane // 128)).astype(f32)
    wide = dot6(factors, expand)
    left = jnp.zeros((8, 128), f32)
    right = jnp.zeros((8, 128), f32)
    for s in range(4):
        left = jnp.where(chunk == s, wide[s * 8 : s * 8 + 8, 0:128], left)
        right = jnp.where(chunk == s, wide[s * 8 : s * 8 + 8, 128:256], right)
    for peer in range(32):
        right_send[peer] = right
    own = lax.dot_general(mask[...], (lane == iota((8, 128), 0) + 32).astype(f32), NN, preferred_element_type=f32)
    for c in range(8):
        tile = keys[:, (c // 4) * 128 : (c // 4) * 128 + 128]
        shift = (-(c % 4) * 32) % 128
        if shift:
            tile = pltpu.roll(tile, shift, 1)
        left_mask[c, 0:8] = left
        left_mask[c, 8:16] = jnp.where(chunk == 0, tile, own)


def outer_kernel(factors, pair, valid, outer_w, tri_w, pair_one, edge_send, right_s, left_s, sum_s):
    lane = iota((8, 128), 1)
    expand_lane = iota((128, 512), 1)
    expand = (iota((128, 512), 0) == (expand_lane // 128) * 32 + expand_lane % 32).astype(bf16)
    masks = []
    for c in range(8):
        high, low = split(factors[c, 0:32, :])
        wide = lax.dot_general(high, expand, NN, preferred_element_type=f32) + lax.dot_general(low, expand, NN, preferred_element_type=f32)
        left = factors[c, 32:40, :]
        masks.append(factors[c, 40:48, :])
        for s in range(4):
            right_s[c * 4 + s] = wide[:, s * 128 : s * 128 + 128]
            for group in range(8):
                index = s * 32 + group * 4 + lane // 32
                left_s[c * 4 + s, :, group * 128 : group * 128 + 128] = jnp.take_along_axis(left, index, axis=1)

    def one_row(i, carry):
        total = [jnp.zeros((32, 128), f32) for _ in range(8)]
        for s in range(32):
            right = right_s[s]
            row = left_s[s, pl.ds(i, 1), :]
            for group in range(8):
                total[group] = total[group] + right * row[:, group * 128 : group * 128 + 128]
        for group in range(8):
            sum_s[pl.ds(i * 32, 32), group * 128 : group * 128 + 128] = total[group]
        return carry

    lax.fori_loop(0, 8, one_row, 0)
    outer = dot3(sum_s[...], outer_w[...])
    mask_all = jnp.concatenate(masks, axis=0).astype(bf16)
    counts = lax.dot_general(mask_all.T, mask_all, NN, preferred_element_type=f32)
    count = jnp.concatenate([counts[0:32, 32 + i : 33 + i] for i in range(8)], axis=0)
    one = pair[...] + outer / (1.0 + count)
    pair_one[...] = one
    edges = dot3(tri_w[...].T, layer_norm(one), NT)
    left_edge = jax.nn.sigmoid(edges[0:128]) * edges[128:256] * valid[...]
    right_edge = jax.nn.sigmoid(edges[256:384]) * edges[384:512] * valid[...]
    edge_send[:, 0, :] = left_edge[:, 0:128]
    edge_send[:, 1, :] = left_edge[:, 128:256]
    edge_send[:, 2, :] = right_edge[:, 0:128]
    edge_send[:, 3, :] = right_edge[:, 128:256]


def cross_kernel(place, own, other, cross_send, left_s, right_s):
    chunk = iota((16, 128), 1) // 32
    for c in range(8):
        for h in range(2):
            left = own[pl.ds(c * 4 + h, 16, stride=32), :]
            for m in range(4):
                start = (m * 2 + h) * 16
                left_s[start : start + 16, c * 128 : c * 128 + 128] = jnp.where(chunk == m, left, 0.0)
            for half, source in enumerate((own, other)):
                right = source[pl.ds(c * 4 + 2 + h, 16, stride=32), :]
                for m in range(4):
                    part = jnp.where(chunk == m, right, 0.0)
                    part = part + pltpu.roll(part, 32, 1)
                    part = part + pltpu.roll(part, 64, 1)
                    right_s[half, c, pl.ds(h * 4 + m, 16, stride=8), :] = part
    for half in range(2):
        crossed = dot3(left_s[...], jnp.concatenate([right_s[half, c] for c in range(8)], axis=1), NT)
        branch = place[0] if half == 0 else 1 - place[0]
        for c in range(4):
            for h in range(2):
                tile = jnp.zeros((16, 128), f32)
                for m in range(4):
                    part = crossed[(m * 2 + h) * 16 : (m * 2 + h) * 16 + 16, :]
                    shift = ((m - c) * 32) % 128
                    if shift:
                        part = pltpu.roll(part, shift, 1)
                    tile = jnp.where(chunk == m, part, tile)
                cross_send[pl.ds((branch * 4 + c) * 2 + h, 16, stride=16), :] = tile


def gate_kernel(pair_one, gate_w, gate_out):
    gate_out[...] = jax.nn.sigmoid(dot3(layer_norm(pair_one[...]), gate_w[...]))


def final_kernel(crossed, pair_one, gate, out_w, in_w, last_w, new_pair, triangle_s):
    for h in range(2):
        part = layer_norm(crossed[pl.ds(h, 128, stride=2), :], axis=0)
        triangle_s[h * 128 : h * 128 + 128, :] = dot3(part.T, out_w[...])
    middle = pair_one[...] + triangle_s[...] * gate[...]
    hidden = jnp.maximum(dot3(layer_norm(middle), in_w[...]), 0.0)
    new_pair[...] = middle + dot3(hidden, last_w[...])


def shards(
    pair_rep,
    alignment,
    residue_mask,
    row_mask,
    attention_in,
    pair_bias_w,
    attention_out,
    outer_in,
    outer_out,
    triangle_in,
    triangle_gate,
    triangle_out,
    transit_in,
    transit_out,
):
    branch = lax.axis_index("branch").astype(jnp.int32).reshape(1)
    row = lax.axis_index(ROWS).astype(jnp.int32)
    col = lax.axis_index("pcol").astype(jnp.int32)
    pair = pair_rep.reshape(256, 128)
    align = alignment.reshape(32, 256)
    mask_float = row_mask.astype(f32)
    mask = jnp.pad(mask_float, ((0, 4), (0, 0)))
    x_send, bias_send = call(send_kernel, [(16, 40, 256), (8, 8, 256)], scalars=1, name="send")(
        row.reshape(1), pair, align, mask, pair_bias_w
    )
    x_half = lax.all_to_all(x_send, "prow", 0, 0, tiled=True)
    bias_all = lax.all_to_all(bias_send, "pcol", 0, 0, tiled=True)
    query, gate = call(query_kernel, [(256, 256), (32, 256)], name="query")(align, attention_in)
    x_all = lax.all_gather(x_half, "branch", axis=0, tiled=True)
    new_align, right_send, left_mask = call(
        attend_kernel,
        [(32, 256), (32, 8, 128), (8, 16, 128)],
        scratch=[pltpu.VMEM((64, 256), f32), pltpu.VMEM((256, 256), f32)],
        name="attend",
    )(
        x_all,
        bias_all,
        query,
        gate,
        align,
        mask,
        mask_float.reshape(32, 1),
        attention_in[:, 512:768],
        attention_out,
        outer_in,
    )
    right_all = lax.all_to_all(right_send, ROWS, 0, 0, tiled=True)
    factor_send = jnp.concatenate([right_all.reshape(8, 32, 128), left_mask], axis=1)
    factors = lax.all_to_all(factor_send, "pcol", 0, 0, tiled=True)
    res_float = residue_mask.astype(f32)
    row_valid = lax.dynamic_slice_in_dim(res_float, row * 8, 8)
    col_valid = lax.dynamic_slice_in_dim(res_float, col * 32, 32)
    valid = (row_valid[:, None] * col_valid[None, :]).reshape(1, 256)
    pair_one, edge_send = call(
        outer_kernel,
        [(256, 128), (128, 4, 128)],
        scratch=[pltpu.VMEM((32, 32, 128), f32), pltpu.VMEM((32, 8, 1024), f32), pltpu.VMEM((256, 1024), f32)],
        name="outer",
    )(factors, pair, valid, outer_out, triangle_in)
    own_edges = lax.all_to_all(edge_send, CHIPS, 0, 0, tiled=True)
    (tri_gate,) = call(gate_kernel, [(256, 128)], name="gate")(pair_one, triangle_gate)
    other_edges = lax.ppermute(own_edges, "branch", [(0, 1), (1, 0)])
    (cross_send,) = call(
        cross_kernel,
        [(256, 128)],
        scratch=[pltpu.VMEM((128, 1024), f32), pltpu.VMEM((2, 8, 128, 128), f32)],
        scalars=1,
        name="cross",
    )(branch, own_edges.reshape(512, 128), other_edges.reshape(512, 128))
    crossed = lax.all_to_all(cross_send.reshape(128, 2, 128), CHIPS, 0, 0, tiled=True)
    (new_pair,) = call(final_kernel, [(256, 128)], scratch=[pltpu.VMEM((256, 128), f32)], name="final")(
        crossed.reshape(256, 128), pair_one, tri_gate, triangle_out, transit_in, transit_out
    )
    return (new_align.reshape(4, 8, 256), new_pair.reshape(8, 32, 128))


def solution(mesh):
    return jax.shard_map(
        shards,
        mesh=mesh,
        in_specs=(
            P(("branch", "prow"), "pcol", None),
            P("pcol", ("branch", "prow"), None),
            P(),
            P("pcol", ("branch", "prow")),
            P(),
            P(),
            P(),
            P(),
            P(),
            P(),
            P(),
            P(),
            P(),
            P(),
        ),
        out_specs=(P("pcol", ("branch", "prow"), None), P(("branch", "prow"), "pcol", None)),
        check_vma=False,
    )
```

time: 664 us -> 159 us (0.24)
  blocking collectives: 309 us -> 59.3 us
  waiting for transfers between devices: 146 us -> 24.9 us
  local copies, waits for them, and re-layouts: 98.2 us -> 8.56 us
  matrix products: 83.8 us -> 0 us
  Pallas kernels: 0 us -> 26.3 us
  starting transfers between devices: 0.34 us -> 21.7 us
  other arithmetic: 10.4 us -> 2.28 us
    all_gather x4 -> x0, blocking collectives: 255 us -> none  [the longest x1 69.7 us: shards(): lax.all_gather(right_outer, ('branch', 'prow'), axis=1, tiled=True)]
    reduce_scatter x2 -> x0, waiting for transfers between devices: 86.3 us -> none  [the longest x1 86.3 us: shards(): lax.psum_scatter(cross_part, 'pcol', scatter_dimension=1, tiled=True)]
    dot_general x31 -> x0, matrix products: 83.8 us -> none  [the longest x8 40.3 us: outer_block(): jnp.einsum('sip,sjq->ijpq', left_rows, right_cols, precision=highest)]
    all_gather x2 -> x1, waiting for transfers between devices: 59.9 us -> 0.01 us  [shards(): x_all = lax.all_gather(x_half, 'branch', axis=0, tiled=True)]
    all_to_all x0 -> x3, blocking collectives: none -> 59.3 us  [the longest x1 26.6 us: shards(): x_half = lax.all_to_all(x_send, 'prow', 0, 0, tiled=True)]
    unnamed x1 -> x0, blocking collectives: 54.2 us -> none
    transpose x9 -> x0, local copies, waits for them, and re-layouts: 46.5 us -> none  [the longest x8 45.1 us: outer_block(): jnp.einsum('sip,sjq->ijpq', left_rows, right_cols, precision=highest)]
    reshape x12 -> x1, local copies, waits for them, and re-layouts: 30.6 us -> 0.68 us  [shards(): mask_float.reshape(32, 1)]
  transfers between devices with their start and end apart: 4 -> 5, of which waited for: 2 -> 4; matrix products, arithmetic and copies ran while one was open for 1% -> 3% of each run, Pallas kernels for 0% -> 3%
where the time goes in v1:
time: 159 us; the launch traced here: 157 us
  blocking collectives  59.3 us (37%)
  Pallas kernels  26.3 us (17%)
  waiting for transfers between devices  24.9 us (16%)
  starting transfers between devices  21.7 us (14%)
  between operations  14.1 us (9%)
  local copies, waits for them, and re-layouts  8.56 us (5%)
  other arithmetic  2.28 us (1%)
    all_to_all x1, blocking collectives, shards(): x_half = lax.all_to_all(x_send, 'prow', 0, 0, tiled=True)  26.6 us
    pallas_call x7, Pallas kernels, run(): pl.pallas_call(kernel, out_shape=[jax.ShapeDtypeStruct(shape, f32) for sh...  26.3 us
    all_to_all x1, blocking collectives, shards(): own_edges = lax.all_to_all(edge_send, CHIPS, 0, 0, tiled=True)  19.3 us
    all_to_all x1, blocking collectives, shards(): right_all = lax.all_to_all(right_send, ROWS, 0, 0, tiled=True)  13.4 us
    all_to_all x1, waiting for transfers between devices, shards(): factors = lax.all_to_all(factor_send, 'pcol', 0, 0, tiled=True)  10 us
    all_to_all x1, waiting for transfers between devices, shards(): lax.all_to_all(cross_send.reshape(128, 2, 128), CHIPS, 0, 0, tiled=True)  9.01 us
    all_to_all x1, starting transfers between devices, shards(): bias_all = lax.all_to_all(bias_send, 'pcol', 0, 0, tiled=True)  8.41 us
    all_to_all x1, starting transfers between devices, shards(): lax.all_to_all(cross_send.reshape(128, 2, 128), CHIPS, 0, 0, tiled=True)  7.92 us
  transfers between devices with their start and end apart: 5, of which 4 were waited for; matrix products, arithmetic and copies ran while one was open for 3% of the time, Pallas kernels for 3%

profile of v1, /device:TPU:2, one launch (start us, length us, event | category | flops | bytes accessed | tf_op | source)
XLA Modules:
  0.0 157.1 jit_solution(4369907577144178563)
XLA Ops:
  7.2 0.7 convert_element_type.8
  7.9 1.4 copy.19.bias_w
  9.3 0.6 pad.4.mask
  9.9 2.2 %send.1 = (f32[16,40,256]{2,1,0:T(8,128)}, f32[8,8,256]{2,1,0:T(8,128)}) custom-call(s32[1]{0:T(128)} %bitcast.place, f32[256,128]{1,0:T(8,128)} %bitcast.12, f32[32,256]{1,0:T(8,128)} %bitcast.17, f32[8,8]{1,0:T(8,128)} %pad.4.mask, f32[128,8]{1,0:T(8,128)} %copy.19.bias_w), custom_call_target="tpu_custom_call" | custom-call | tf_op jit(solution)/shard_map/send/pallas_call | solution.py:53
  12.1 26.6 %all_to_all.30 = f32[16,40,256]{2,1,0:T(8,128)} all-to-all(f32[16,40,256]{2,1,0:T(8,128)} %get-tuple-element.11), channel_id=1, replica_groups=mesh['branch'=2,'prow'=16,'pcol'=8] {'prow'}, dimensions={0} | all-to-all | bytes 1310720 | tf_op jit(solution)/shard_map/all_to_all | solution.py:253
  38.8 8.4 %all-to-all-start.1 = ((f32[8,8,256]{2,1,0:T(8,128)}), f32[8,8,256]{2,1,0:T(8,128)S(1)}, u32[]{:S(2)}, u32[]{:S(2)}) async-start(f32[8,8,256]{2,1,0:T(8,128)} %get-tuple-element.12), calls=%async_computation.1 | async-start | bytes 131072 | tf_op jit(solution)/shard_map/all_to_all | solution.py:254
  47.2 0.7 reshape.77.mask_col
  47.9 2.8 %query.1 = (f32[256,256]{1,0:T(8,128)}, f32[32,256]{1,0:T(8,128)}) custom-call(f32[32,256]{1,0:T(8,128)} %bitcast.18, f32[256,1024]{1,0:T(8,128)} %proj.1), custom_call_target="tpu_custom_call" | custom-call | tf_op jit(solution)/shard_map/query/pallas_call | solution.py:53
  50.7 1.7 %slice.3.value_w = f32[256,256]{1,0:T(8,128)} slice(f32[256,1024]{1,0:T(8,128)} %proj.1), slice={[0:256], [512:768]} | slice | bytes 524288 | tf_op jit(solution)/shard_map/slice | solution.py:270
  52.3 0.8 copy.21.outer_w
  53.1 4.3 %all-to-all-done.1.bias_all = f32[8,8,256]{2,1,0:T(8,128)S(1)} async-done(((f32[8,8,256]{2,1,0:T(8,128)}), f32[8,8,256]{2,1,0:T(8,128)S(1)}, u32[]{:S(2)}, u32[]{:S(2)}) %all-to-all-start.1) | async-done | bytes 65568 | tf_op jit(solution)/shard_map/all_to_all | solution.py:254
  57.4 0.6 copy-done.3
  58.1 6.1 %attend.1 = (f32[32,256]{1,0:T(8,128)}, f32[32,8,128]{2,1,0:T(8,128)}, f32[8,16,128]{2,1,0:T(8,128)}) custom-call(f32[32,40,256]{2,1,0:T(8,128)} %all-gather.2.cloned.1.call-done.x_all, f32[8,8,256]{2,1,0:T(8,128)} %copy-done.3, f32[256,256]{1,0:T(8,128)} %get-tuple-element.13.query, f32[32,256]{1,0:T(8,128)} %get-tuple-element.14.gate, f32[32,256]{1,0:T(8,128)} %bitcast.19, ...), custom_call_target="tpu_custom_call" | custom-call | tf_op jit(solution)/shard_map/attend/pallas_call | solution.py:53
  64.2 13.4 %all_to_all.31 = f32[32,8,128]{2,1,0:T(8,128)S(1)} all-to-all(f32[32,8,128]{2,1,0:T(8,128)} %get-tuple-element.16), channel_id=1, replica_groups=mesh['branch'=2,'prow'=16,'pcol'=8] {'branch','prow'}, dimensions={0} | all-to-all | bytes 262144 | tf_op jit(solution)/shard_map/all_to_all | solution.py:274
  77.6 1.5 pad_maximum_fusion
  79.1 5.4 %all-to-all-start.3 = ((f32[8,48,128]{2,1,0:T(8,128)}), f32[8,48,128]{2,1,0:T(8,128)S(1)}, u32[]{:S(2)}, u32[]{:S(2)}) async-start(f32[8,48,128]{2,1,0:T(8,128)} %pad_maximum_fusion), calls=%async_computation.3 | async-start | bytes 393216 | tf_op jit(solution)/shard_map/all_to_all | solution.py:276
  84.5 0.1 dynamic_slice.6
  84.5 0.1 dynamic_slice.7
  84.6 0.1 broadcast_multiply_fusion
  84.7 0.6 mul.38.valid
  85.3 10.0 %all-to-all-done.3.factors = f32[8,48,128]{2,1,0:T(8,128)S(1)} async-done(((f32[8,48,128]{2,1,0:T(8,128)}), f32[8,48,128]{2,1,0:T(8,128)S(1)}, u32[]{:S(2)}, u32[]{:S(2)}) %all-to-all-start.3) | async-done | bytes 196640 | tf_op jit(solution)/shard_map/all_to_all | solution.py:276
  95.4 0.7 copy-done.1
  96.0 7.1 %outer.1 = (f32[256,128]{1,0:T(8,128)}, f32[128,4,128]{2,1,0:T(4,128)}) custom-call(f32[8,48,128]{2,1,0:T(8,128)} %copy-done.1, f32[256,128]{1,0:T(8,128)} %bitcast.13, f32[1,256]{1,0:T(1,128)} %mul.38.valid, f32[1024,128]{1,0:T(8,128)} %outer_w.2, f32[128,512]{1,0:T(8,128)} %tri_w.1), custom_call_target="tpu_custom_call" | custom-call | tf_op jit(solution)/shard_map/outer/pallas_call | solution.py:53
  103.1 19.3 %all_to_all.32 = f32[128,4,128]{2,1,0:T(4,128)S(1)} all-to-all(f32[128,4,128]{2,1,0:T(4,128)} %get-tuple-element.18), channel_id=1, replica_groups=mesh['branch'=2,'prow'=16,'pcol'=8] {'prow','pcol'}, dimensions={0} | all-to-all | bytes 524288 | tf_op jit(solution)/shard_map/all_to_all | solution.py:287
  122.4 1.5 collective-permute-done
  124.0 0.7 copy-done.4
  124.7 3.0 %cross.1 = f32[256,128]{1,0:T(8,128)} custom-call(s32[1]{0:T(128)} %bitcast.4.place, f32[512,128]{1,0:T(8,128)} %bitcast.11, f32[512,128]{1,0:T(8,128)} %bitcast.20), custom_call_target="tpu_custom_call" | custom-call | tf_op jit(solution)/shard_map/cross/pallas_call | solution.py:53
  127.7 7.9 %all-to-all-start.5 = ((f32[128,2,128]{2,1,0:T(2,128)}), f32[128,2,128]{2,1,0:T(2,128)S(1)}, u32[]{:S(2)}, u32[]{:S(2)}) async-start(f32[128,2,128]{2,1,0:T(2,128)} %bitcast.16), calls=%async_computation.5 | async-start | bytes 262144 | tf_op jit(solution)/shard_map/all_to_all | solution.py:297
  135.6 1.9 %gate.1 = f32[256,128]{1,0:T(8,128)} custom-call(f32[256,128]{1,0:T(8,128)} %get-tuple-element.19.pair_one, f32[128,128]{1,0:T(8,128)} %gate_w.1), custom_call_target="tpu_custom_call" | custom-call | tf_op jit(solution)/shard_map/gate/pallas_call | solution.py:53
  137.6 9.0 %all-to-all-done.5 = f32[128,2,128]{2,1,0:T(2,128)S(1)} async-done(((f32[128,2,128]{2,1,0:T(2,128)}), f32[128,2,128]{2,1,0:T(2,128)S(1)}, u32[]{:S(2)}, u32[]{:S(2)}) %all-to-all-start.5) | async-done | bytes 131104 | tf_op jit(solution)/shard_map/all_to_all | solution.py:297
  146.6 0.6 copy-done.2
  147.2 3.1 %final.1 = f32[256,128]{1,0:T(8,128)} custom-call(f32[256,128]{1,0:T(8,128)} %bitcast.14, f32[256,128]{1,0:T(8,128)} %get-tuple-element.19.pair_one, f32[256,128]{1,0:T(8,128)} %gate.1, f32[128,128]{1,0:T(8,128)} %out_w.3, f32[128,512]{1,0:T(8,128)} %in_w.1, f32[512,128]{1,0:T(8,128)} %last_w.1), custom_call_target="tpu_custom_call" | custom-call | tf_op jit(solution)/shard_map/final/pallas_call | solution.py:53
  (15 shorter events, 0.1 us)
Async XLA Ops:
  7.2 50.3 %all-gather.2.cloned.1.call-start = ((), (), s32[]{:S(2)}) async-start(), calls=%async_computation.6 | async-start | bytes 1966080 | tf_op jit(solution)/shard_map/all_gather | solution.py:256
  38.7 13.6 %copy-start.5 = (f32[256,64]{0,1:T(8,128)S(1)}, f32[256,64]{0,1:T(8,128)}, u32[]{:S(2)}) copy-start(f32[256,64]{0,1:T(8,128)} %param.21) | copy-start | bytes 196612
  38.8 18.7 %all-to-all-start.1 = ((f32[8,8,256]{2,1,0:T(8,128)}), f32[8,8,256]{2,1,0:T(8,128)S(1)}, u32[]{:S(2)}, u32[]{:S(2)}) async-start(f32[8,8,256]{2,1,0:T(8,128)} %get-tuple-element.12), calls=%async_computation.1 | async-start | bytes 131072 | tf_op jit(solution)/shard_map/all_to_all | solution.py:254
  57.4 0.6 copy-start.3
  58.1 26.4 %copy-start.6 = (s32[256]{0:T(256)S(1)}, s32[256]{0:T(256)}, u32[]{:S(2)}) copy-start(s32[256]{0:T(256)} %param.16) | copy-start | bytes 3076
  79.1 16.3 %all-to-all-start.3 = ((f32[8,48,128]{2,1,0:T(8,128)}), f32[8,48,128]{2,1,0:T(8,128)S(1)}, u32[]{:S(2)}, u32[]{:S(2)}) async-start(f32[8,48,128]{2,1,0:T(8,128)} %pad_maximum_fusion), calls=%async_computation.3 | async-start | bytes 393216 | tf_op jit(solution)/shard_map/all_to_all | solution.py:276
  95.4 0.7 copy-start.1
  122.4 1.5 copy-start
  122.4 1.5 collective-permute-start
  124.0 0.7 copy-start.4
  127.7 18.9 %all-to-all-start.5 = ((f32[128,2,128]{2,1,0:T(2,128)}), f32[128,2,128]{2,1,0:T(2,128)S(1)}, u32[]{:S(2)}, u32[]{:S(2)}) async-start(f32[128,2,128]{2,1,0:T(2,128)} %bitcast.16), calls=%async_computation.5 | async-start | bytes 262144 | tf_op jit(solution)/shard_map/all_to_all | solution.py:297
  146.6 0.6 copy-start.2
Sparse Core Ops, SparseCore 0:
  38.9 14.1 all-gather.1

commit v2 on v1

--- a/solution.py
+++ b/solution.py
@@ -7,6 +7,7 @@
 from jax.experimental.pallas import tpu as pltpu
 from jax.sharding import PartitionSpec as P
 
+
 highest = lax.Precision.HIGHEST
 epsilon = 1e-05
 f32 = jnp.float32
@@ -14,6 +15,7 @@
 
 ROWS = ("branch", "prow")
 CHIPS = ("prow", "pcol")
+
 NN = (((1,), (0,)), ((), ()))
 NT = (((1,), (1,)), ((), ()))
 
@@ -45,79 +47,111 @@
     return lax.broadcasted_iota(jnp.int32, shape, axis)
 
 
-def call(kernel, out_shapes, scratch=(), scalars=0, name=None):
+def call(kernel, out_shapes, scratch=(), scalars=0, far=0, kept=()):
     vmem = pl.BlockSpec(memory_space=pltpu.VMEM)
     smem = pl.BlockSpec(memory_space=pltpu.SMEM)
+    outs = [jax.ShapeDtypeStruct(shape, f32) if n in kept else pltpu.VMEM(shape, f32) for n, shape in enumerate(out_shapes)]
 
     def run(*args):
+        arrays = [pltpu.with_memory_space_constraint(arg, pltpu.VMEM) for arg in args[scalars + far :]]
         return pl.pallas_call(
             kernel,
-            out_shape=[jax.ShapeDtypeStruct(shape, f32) for shape in out_shapes],
-            in_specs=[smem] * scalars + [vmem] * (len(args) - scalars),
+            out_shape=outs,
+            in_specs=[smem] * scalars + [pl.BlockSpec(memory_space=pl.ANY)] * far + [vmem] * len(arrays),
             out_specs=[vmem] * len(out_shapes),
             scratch_shapes=list(scratch),
-            name=name,
-        )(*args)
+        )(*args[: scalars + far], *arrays)
 
     return run
 
 
 def send_kernel(place, pair, align, mask, bias_w, x_send, bias_send):
-    pair_norm = layer_norm(pair[...])
-    bias = dot6(bias_w[...].T, pair_norm, NT)
-    for peer in range(bias_send.shape[0]):
-        bias_send[peer] = bias
     normed = layer_norm(align[...])
-    lane = iota((8, 256), 1)
-    spread = ((lane % 8 == iota((8, 256), 0)) & (lane // 8 == place[0])).astype(f32)
-    mask_tile = lax.dot_general(mask[...], spread, NN, preferred_element_type=f32)
-    for peer in range(x_send.shape[0]):
-        x_send[peer, 0:32] = normed
-        x_send[peer, 32:40] = mask_tile
-
-
-def query_kernel(align, proj, query_out, gate_out):
-    normed = layer_norm(align[...])
-    query = dot6(normed, proj[:, 0:256]) * 32 ** (-0.5)
-    gate_out[...] = jax.nn.sigmoid(dot3(normed, proj[:, 768:1024]))
-    own_head = iota((32, 8, 256), 1) == iota((32, 8, 256), 2) // 32
-    wide = jnp.where(own_head, jnp.broadcast_to(query[:, None, :], (32, 8, 256)), 0.0)
-    query_out[...] = dot6(wide.reshape(256, 256), proj[:, 256:512], NT)
-
-
-def attend_kernel(
-    x_all, bias_all, query, gate, align, mask, mask_col, value_w, out_w, outer_w, new_align, right_send, left_mask, bias_s, mix_s
-):
     lane = iota((8, 128), 1)
-    chunk = lane // 32
+    spread = ((lane % 8 == iota((8, 128), 0)) & (lane // 8 == place[0])).astype(f32)
+    mask_rows = jnp.concatenate([mask[...].astype(f32), jnp.zeros((4, 8), f32)], axis=0)
+    mask_tile = lax.dot_general(mask_rows, spread, NN, preferred_element_type=f32)
+    x_send[0:32] = normed[:, 0:128]
+    x_send[32:64] = normed[:, 128:256]
+    x_send[64:72] = mask_tile
+    bias_send[...] = dot6(bias_w[...], layer_norm(pair[...]), NT)
+
+
+def query_kernel(place, proj, align, *refs):
+    pieces, (query_out, gate_out, bias_out, bias_s, proj_s, gate_s, sems) = refs[:4], refs[4:]
+    first = pltpu.make_async_copy(proj.at[:, pl.ds(0, 512)], proj_s, sems.at[0])
+    second = pltpu.make_async_copy(proj.at[:, pl.ds(768, 256)], gate_s, sems.at[1])
+    first.start()
+    second.start()
+    for step, piece in enumerate(pieces):
+        for high in range(2):
+            bias_s[place[1] ^ (step + 4 * high)] = piece[high]
+    chunk = iota((8, 128), 1) // 32
     for i in range(8):
-        half, place = divmod(i, 4)
-        for group in range(2):
+        half, spot = divmod(i, 4)
+        for group, branch in enumerate((place[0], 1 - place[0])):
             tile = jnp.zeros((8, 128), f32)
             for c in range(4):
-                source = bias_all[group * 4 + c, :, half * 128 : half * 128 + 128]
-                shift = ((c - place) * 32) % 128
+                source = bias_s[branch * 4 + c, :, half * 128 : half * 128 + 128]
+                shift = ((c - spot) * 32) % 128
                 if shift:
                     source = pltpu.roll(source, shift, 1)
                 tile = jnp.where(chunk == c, source, tile)
-            bias_s[i * 8 : i * 8 + 8, group * 128 : group * 128 + 128] = tile
-    keys = x_all[0, 32:40, :]
-    for r in range(1, 32):
-        keys = keys + x_all[r, 32:40, :]
-    key_bias = 1000000000.0 * (keys - 1.0)
+            bias_out[i * 8 : i * 8 + 8, group * 128 : group * 128 + 128] = tile
+    normed = layer_norm(align[...])
+    first.wait()
+    query = dot6(normed, proj_s[:, 0:256]) * 32 ** (-0.5)
+    own_head = iota((32, 8, 256), 1) == iota((32, 8, 256), 2) // 32
+    wide = jnp.where(own_head, jnp.broadcast_to(query[:, None, :], (32, 8, 256)), 0.0)
+    query_out[...] = dot6(wide.reshape(256, 256), proj_s[:, 256:512], NT)
+    second.wait()
+    gate_out[...] = jax.nn.sigmoid(dot3(normed, gate_s[...]))
+
+
+def attend_kernel(place, proj, out_w, bias_all, query, gate, align, mask, outer_w, *refs):
+    pieces, (new_align, right_send, left_mask, x_s, mix_s, value_s, out_s, sems) = refs[:8], refs[8:]
+    value_copy = pltpu.make_async_copy(proj.at[:, pl.ds(512, 256)], value_s, sems.at[0])
+    out_copy = pltpu.make_async_copy(out_w, out_s, sems.at[1])
+    value_copy.start()
+    out_copy.start()
+    for index, piece in enumerate(pieces):
+        swapped, step = divmod(index, 4)
+        for low in range(4):
+            x_s[swapped, place[1] ^ (step * 4 + low)] = piece[low]
+    x_own, x_other = x_s.at[0], x_s.at[1]
+    lane = iota((8, 128), 1)
+    chunk = lane // 32
+    keys_own, keys_other = x_own[0, 64:72, :], x_other[0, 64:72, :]
+    for r in range(1, 16):
+        keys_own = keys_own + x_own[r, 64:72, :]
+        keys_other = keys_other + x_other[r, 64:72, :]
+    key_bias = 1000000000.0 * (jnp.concatenate([keys_own, keys_other], axis=1) - 1.0)
+    keys = (jnp.where(place[0] == 0, keys_own, keys_other), jnp.where(place[0] == 0, keys_other, keys_own))
     for s in range(4):
-        x_row = x_all[:, s * 8 : s * 8 + 8, :].reshape(256, 256)
+        x_row = jnp.concatenate(
+            [
+                jnp.concatenate([half[:, t * 32 + s * 8 : t * 32 + s * 8 + 8, :].reshape(128, 128) for t in range(2)], axis=1)
+                for half in (x_own, x_other)
+            ],
+            axis=0,
+        )
         scores = dot6(query[s * 64 : s * 64 + 64, :], x_row, NT)
-        scores = (scores + bias_s[...]) + key_bias[s : s + 1, :]
+        scores = (scores + bias_all[...]) + key_bias[s : s + 1, :]
         weights = jnp.exp(scores - jnp.max(scores, axis=-1, keepdims=True))
         total = jnp.sum(weights, axis=-1, keepdims=True)
         mix_s[s * 64 : s * 64 + 64, :] = dot3(weights, x_row) / total
-    values = dot3(mix_s[...], value_w[...]).reshape(32, 8, 256)
+    value_copy.wait()
+    out_copy.wait()
+    values = dot3(mix_s[...], value_s[...]).reshape(32, 8, 256)
     own_head = iota((32, 8, 256), 1) == iota((32, 8, 256), 2) // 32
     mixed = jnp.sum(jnp.where(own_head, values, 0.0), axis=1)
-    updated = align[...] + dot3(mixed * gate[...], out_w[...])
+    updated = align[...] + dot3(mixed * gate[...], out_s[...])
     new_align[...] = updated
-    factors = dot3(layer_norm(updated), outer_w[...]) * mask_col[...]
+    mask_rows = jnp.concatenate([mask[...].astype(f32), jnp.zeros((4, 8), f32)], axis=0)
+    by_row = (iota((32, 8), 1) == iota((32, 8), 0) // 8).astype(f32)
+    mask_wide = lax.dot_general(by_row, mask_rows, NN, preferred_element_type=f32)
+    mask_col = jnp.sum(jnp.where(iota((32, 8), 1) == iota((32, 8), 0) % 8, mask_wide, 0.0), axis=1, keepdims=True)
+    factors = dot3(layer_norm(updated), outer_w[...], NT) * mask_col
     wide_lane = iota((64, 256), 1)
     expand = (iota((64, 256), 0) == wide_lane % 32 + 32 * (wide_lane // 128)).astype(f32)
     wide = dot6(factors, expand)
@@ -128,9 +162,9 @@
         right = jnp.where(chunk == s, wide[s * 8 : s * 8 + 8, 128:256], right)
     for peer in range(32):
         right_send[peer] = right
-    own = lax.dot_general(mask[...], (lane == iota((8, 128), 0) + 32).astype(f32), NN, preferred_element_type=f32)
+    own = lax.dot_general(mask_rows, (lane == iota((8, 128), 0) + 32).astype(f32), NN, preferred_element_type=f32)
     for c in range(8):
-        tile = keys[:, (c // 4) * 128 : (c // 4) * 128 + 128]
+        tile = keys[c // 4]
         shift = (-(c % 4) * 32) % 128
         if shift:
             tile = pltpu.roll(tile, shift, 1)
@@ -245,32 +279,47 @@
     col = lax.axis_index("pcol").astype(jnp.int32)
     pair = pair_rep.reshape(256, 128)
     align = alignment.reshape(32, 256)
-    mask_float = row_mask.astype(f32)
-    mask = jnp.pad(mask_float, ((0, 4), (0, 0)))
-    x_send, bias_send = call(send_kernel, [(16, 40, 256), (8, 8, 256)], scalars=1, name="send")(
-        row.reshape(1), pair, align, mask, pair_bias_w
+    place = jnp.stack([branch[0], col, row % 16])
+    x_send, bias_send = call(send_kernel, [(72, 128), (8, 256)], scalars=1)(
+        place[2:3], pair, align, row_mask, pair_bias_w.T
     )
-    x_half = lax.all_to_all(x_send, "prow", 0, 0, tiled=True)
-    bias_all = lax.all_to_all(bias_send, "pcol", 0, 0, tiled=True)
-    query, gate = call(query_kernel, [(256, 256), (32, 256)], name="query")(align, attention_in)
-    x_all = lax.all_gather(x_half, "branch", axis=0, tiled=True)
+
+    def swap(value, axis, size, step):
+        return lax.ppermute(value, axis, [(d, d ^ step) for d in range(size)])
+
+    x_stack = [x_send] + [swap(x_send, "prow", 16, step) for step in (3, 2, 1)][::-1]
+    bias_stack = [bias_send, swap(bias_send, "pcol", 8, 4)]
+    x_stack = jnp.stack(x_stack)
+    x_own = [x_stack] + [swap(x_stack, "prow", 16, 4 * step) for step in (1, 2, 3)]
+    bias_stack = jnp.stack(bias_stack)
+    bias_own = [bias_stack] + [swap(bias_stack, "pcol", 8, step) for step in (1, 2, 3)]
+    x_other = [swap(value, "branch", 2, 1) for value in x_own]
+    query, gate, bias_all = call(
+        query_kernel,
+        [(256, 256), (32, 256), (64, 256)],
+        scratch=[
+            pltpu.VMEM((8, 8, 256), f32),
+            pltpu.VMEM((256, 512), f32),
+            pltpu.VMEM((256, 256), f32),
+            pltpu.SemaphoreType.DMA((2,)),
+        ],
+        scalars=1,
+        far=1,
+    )(place, attention_in, align, *bias_own)
     new_align, right_send, left_mask = call(
         attend_kernel,
         [(32, 256), (32, 8, 128), (8, 16, 128)],
-        scratch=[pltpu.VMEM((64, 256), f32), pltpu.VMEM((256, 256), f32)],
-        name="attend",
-    )(
-        x_all,
-        bias_all,
-        query,
-        gate,
-        align,
-        mask,
-        mask_float.reshape(32, 1),
-        attention_in[:, 512:768],
-        attention_out,
-        outer_in,
-    )
+        scratch=[
+            pltpu.VMEM((2, 16, 72, 128), f32),
+            pltpu.VMEM((256, 256), f32),
+            pltpu.VMEM((256, 256), f32),
+            pltpu.VMEM((256, 256), f32),
+            pltpu.SemaphoreType.DMA((2,)),
+        ],
+        scalars=1,
+        far=2,
+        kept=(0,),
+    )(place[::2], attention_in, attention_out, bias_all, query, gate, align, row_mask, outer_in.T, *x_own, *x_other)
     right_all = lax.all_to_all(right_send, ROWS, 0, 0, tiled=True)
     factor_send = jnp.concatenate([right_all.reshape(8, 32, 128), left_mask], axis=1)
     factors = lax.all_to_all(factor_send, "pcol", 0, 0, tiled=True)
@@ -282,20 +331,15 @@
         outer_kernel,
         [(256, 128), (128, 4, 128)],
         scratch=[pltpu.VMEM((32, 32, 128), f32), pltpu.VMEM((32, 8, 1024), f32), pltpu.VMEM((256, 1024), f32)],
-        name="outer",
     )(factors, pair, valid, outer_out, triangle_in)
     own_edges = lax.all_to_all(edge_send, CHIPS, 0, 0, tiled=True)
-    (tri_gate,) = call(gate_kernel, [(256, 128)], name="gate")(pair_one, triangle_gate)
+    (tri_gate,) = call(gate_kernel, [(256, 128)])(pair_one, triangle_gate)
     other_edges = lax.ppermute(own_edges, "branch", [(0, 1), (1, 0)])
     (cross_send,) = call(
-        cross_kernel,
-        [(256, 128)],
-        scratch=[pltpu.VMEM((128, 1024), f32), pltpu.VMEM((2, 8, 128, 128), f32)],
-        scalars=1,
-        name="cross",
+        cross_kernel, [(256, 128)], scratch=[pltpu.VMEM((128, 1024), f32), pltpu.VMEM((2, 8, 128, 128), f32)], scalars=1
     )(branch, own_edges.reshape(512, 128), other_edges.reshape(512, 128))
     crossed = lax.all_to_all(cross_send.reshape(128, 2, 128), CHIPS, 0, 0, tiled=True)
-    (new_pair,) = call(final_kernel, [(256, 128)], scratch=[pltpu.VMEM((256, 128), f32)], name="final")(
+    (new_pair,) = call(final_kernel, [(256, 128)], scratch=[pltpu.VMEM((256, 128), f32)], kept=(0,))(
         crossed.reshape(256, 128), pair_one, tri_gate, triangle_out, transit_in, transit_out
     )
     return (new_align.reshape(4, 8, 256), new_pair.reshape(8, 32, 128))

time: 159 us -> 131 us (0.82)
  blocking collectives: 59.3 us -> 33.5 us
  starting transfers between devices: 21.7 us -> 36.5 us
  between operations: 14.1 us -> 0.82 us
  waiting for transfers between devices: 24.9 us -> 36.3 us
  Pallas kernels: 26.3 us -> 18.1 us
  local copies, waits for them, and re-layouts: 8.56 us -> 3.23 us
    all_to_all x1 -> x0, blocking collectives: 26.6 us -> none  [shards(): x_half = lax.all_to_all(x_send, 'prow', 0, 0, tiled=True)]
    ppermute x0 -> x14, starting transfers between devices: none -> 20.1 us  [swap(): return lax.ppermute(value, axis, [(d, d ^ step) for d in range(size)])]
    ppermute x0 -> x14, waiting for transfers between devices: none -> 14.3 us  [swap(): return lax.ppermute(value, axis, [(d, d ^ step) for d in range(size)])]
    all_to_all x1 -> x0, starting transfers between devices: 8.41 us -> none  [shards(): bias_all = lax.all_to_all(bias_send, 'pcol', 0, 0, tiled=True)]
    pallas_call x7, Pallas kernels: 26.3 us -> 18.1 us  [run(): pl.pallas_call(kernel, out_shape=outs, in_specs=[smem] * scalars + [pl.Bl...]
    all_to_all x1 -> x0, waiting for transfers between devices: 4.33 us -> none  [shards(): bias_all = lax.all_to_all(bias_send, 'pcol', 0, 0, tiled=True)]
    all_to_all x1, starting transfers between devices: 5.35 us -> 8.36 us  [shards(): factors = lax.all_to_all(factor_send, 'pcol', 0, 0, tiled=True)]
    unnamed x16 -> x28, local copies, waits for them, and re-layouts: 4.81 us -> 2.34 us
  transfers between devices with their start and end apart: 5 -> 17, of which waited for: 4 -> 10; matrix products, arithmetic and copies ran while one was open for 3% -> 1% of each run, Pallas kernels for 3% -> 2%
where the time goes in v2:
time: 131 us; the launch traced here: 129 us
  starting transfers between devices  36.5 us (28%)
  waiting for transfers between devices  36.3 us (28%)
  blocking collectives  33.5 us (26%)
  Pallas kernels  18.1 us (14%)
  local copies, waits for them, and re-layouts  3.23 us (2%)
    ppermute x14, starting transfers between devices, swap(): return lax.ppermute(value, axis, [(d, d ^ step) for d in range(size)])  20.1 us
    all_to_all x1, blocking collectives, shards(): own_edges = lax.all_to_all(edge_send, CHIPS, 0, 0, tiled=True)  19.1 us
    pallas_call x7, Pallas kernels, run(): pl.pallas_call(kernel, out_shape=outs, in_specs=[smem] * scalars + [pl.Bl...  18.1 us
    all_to_all x1, blocking collectives, shards(): right_all = lax.all_to_all(right_send, ROWS, 0, 0, tiled=True)  14.4 us
    ppermute x14, waiting for transfers between devices, swap(): return lax.ppermute(value, axis, [(d, d ^ step) for d in range(size)])  14.3 us
    all_to_all x1, waiting for transfers between devices, shards(): lax.all_to_all(cross_send.reshape(128, 2, 128), CHIPS, 0, 0, tiled=True)  10.6 us
    all_to_all x1, waiting for transfers between devices, shards(): factors = lax.all_to_all(factor_send, 'pcol', 0, 0, tiled=True)  9.93 us
    all_to_all x1, starting transfers between devices, shards(): factors = lax.all_to_all(factor_send, 'pcol', 0, 0, tiled=True)  8.36 us
  transfers between devices with their start and end apart: 17, of which 10 were waited for; matrix products, arithmetic and copies ran while one was open for 1% of the time, Pallas kernels for 2%

profile of v2, /device:TPU:2, one launch (start us, length us, event | category | flops | bytes accessed | tf_op | source)
XLA Modules:
  0.0 129.3 jit_solution(11238132236234378415)
XLA Ops:
  0.7 0.7 copy-done.3
  1.4 0.9 copy-done.1
  2.7 4.6 %collective-permute-start.6 = (f32[72,128]{1,0:T(8,128)S(1)}, f32[72,128]{1,0:T(8,128)S(1)}, u32[]{:S(2)}, u32[]{:S(2)}) collective-permute-start(f32[72,128]{1,0:T(8,128)S(1)} %get-tuple-element.16), channel_id=1, source_target_pairs={{0,24},{8,16},{16,8},{24,0},{32,56},{40,48},{48,40},{56,32},{64,88... | collective-permute-start | bytes 110600 | tf_op jit(solution)/shard_map/ppermute | solution.py:288
  7.3 0.7 collective-permute-start.4
  8.0 1.5 %collective-permute-done.6 = f32[72,128]{1,0:T(8,128)S(1)} collective-permute-done((f32[72,128]{1,0:T(8,128)S(1)}, f32[72,128]{1,0:T(8,128)S(1)}, u32[]{:S(2)}, u32[]{:S(2)}) %collective-permute-start.6) | collective-permute-done | bytes 36896 | tf_op jit(solution)/shard_map/ppermute | solution.py:288
  9.5 2.7 %collective-permute-done.5 = f32[72,128]{1,0:T(8,128)S(1)} collective-permute-done((f32[72,128]{1,0:T(8,128)S(1)}, f32[72,128]{1,0:T(8,128)S(1)}, u32[]{:S(2)}, u32[]{:S(2)}) %collective-permute-start.5) | collective-permute-done | bytes 36896 | tf_op jit(solution)/shard_map/ppermute | solution.py:288
  12.2 1.6 %collective-permute-start.9 = (f32[4,72,128]{2,1,0:T(8,128)S(1)}, f32[4,72,128]{2,1,0:T(8,128)S(1)}, u32[]{:S(2)}, u32[]{:S(2)}) collective-permute-start(f32[4,72,128]{2,1,0:T(8,128)S(1)} %pad_maximum_fusion.1.refs_0_), channel_id=1, source_target_pairs={{0,96},{8,104},{16,112},{24,120},{32,64},{40,72},{48,80},{56,88},{... | collective-permute-start | bytes 442376 | tf_op jit(solution)/shard_map/ppermute | solution.py:288
  13.8 1.1 collective-permute-start.8
  14.9 1.5 %collective-permute-start.7 = (f32[4,72,128]{2,1,0:T(8,128)S(1)}, f32[4,72,128]{2,1,0:T(8,128)S(1)}, u32[]{:S(2)}, u32[]{:S(2)}) collective-permute-start(f32[4,72,128]{2,1,0:T(8,128)S(1)} %pad_maximum_fusion.1.refs_0_), channel_id=1, source_target_pairs={{0,32},{8,40},{16,48},{24,56},{32,0},{40,8},{48,16},{56,24},{64,96... | collective-permute-start | bytes 442376 | tf_op jit(solution)/shard_map/ppermute | solution.py:288
  16.4 4.6 %collective-permute-start = (f32[8,256]{1,0:T(8,128)S(1)}, f32[8,256]{1,0:T(8,128)S(1)}, u32[]{:S(2)}, u32[]{:S(2)}) collective-permute-start(f32[8,256]{1,0:T(8,128)S(1)} %get-tuple-element.12), channel_id=1, source_target_pairs={{0,4},{1,5},{2,6},{3,7},{4,0},{5,1},{6,2},{7,3},{8,12},{9,13},{10,... | collective-permute-start | bytes 24584 | tf_op jit(solution)/shard_map/ppermute | solution.py:288
  21.0 0.5 collective-permute-start.13
  22.0 1.9 %collective-permute-done = f32[8,256]{1,0:T(8,128)S(1)} collective-permute-done((f32[8,256]{1,0:T(8,128)S(1)}, f32[8,256]{1,0:T(8,128)S(1)}, u32[]{:S(2)}, u32[]{:S(2)}) %collective-permute-start) | collective-permute-done | bytes 8224 | tf_op jit(solution)/shard_map/ppermute | solution.py:288
  23.9 3.0 %collective-permute-start.3 = (f32[2,8,256]{2,1,0:T(8,128)S(1)}, f32[2,8,256]{2,1,0:T(8,128)S(1)}, u32[]{:S(2)}, u32[]{:S(2)}) collective-permute-start(f32[2,8,256]{2,1,0:T(8,128)S(1)} %pad_maximum_fusion.2.refs_0_), channel_id=1, source_target_pairs={{0,3},{1,2},{2,1},{3,0},{4,7},{5,6},{6,5},{7,4},{8,11},{9,10},{10,... | collective-permute-start | bytes 49160 | tf_op jit(solution)/shard_map/ppermute | solution.py:288
  26.9 1.9 %collective-permute-done.3.refs_3_ = f32[2,8,256]{2,1,0:T(8,128)S(1)} collective-permute-done((f32[2,8,256]{2,1,0:T(8,128)S(1)}, f32[2,8,256]{2,1,0:T(8,128)S(1)}, u32[]{:S(2)}, u32[]{:S(2)}) %collective-permute-start.3) | collective-permute-done | bytes 16416 | tf_op jit(solution)/shard_map/ppermute | solution.py:288
  28.9 2.0 %collective-permute-start.2 = (f32[2,8,256]{2,1,0:T(8,128)S(1)}, f32[2,8,256]{2,1,0:T(8,128)S(1)}, u32[]{:S(2)}, u32[]{:S(2)}) collective-permute-start(f32[2,8,256]{2,1,0:T(8,128)S(1)} %pad_maximum_fusion.2.refs_0_), channel_id=1, source_target_pairs={{0,2},{1,3},{2,0},{3,1},{4,6},{5,7},{6,4},{7,5},{8,10},{9,11},{10,... | collective-permute-start | bytes 49160 | tf_op jit(solution)/shard_map/ppermute | solution.py:288
  30.9 3.3 %collective-permute-done.2.refs_2_ = f32[2,8,256]{2,1,0:T(8,128)S(1)} collective-permute-done((f32[2,8,256]{2,1,0:T(8,128)S(1)}, f32[2,8,256]{2,1,0:T(8,128)S(1)}, u32[]{:S(2)}, u32[]{:S(2)}) %collective-permute-start.2) | collective-permute-done | bytes 16416 | tf_op jit(solution)/shard_map/ppermute | solution.py:288
  34.6 0.7 slice.3.place
  35.2 2.6 %collective-permute-done.1.refs_1_ = f32[2,8,256]{2,1,0:T(8,128)S(1)} collective-permute-done((f32[2,8,256]{2,1,0:T(8,128)S(1)}, f32[2,8,256]{2,1,0:T(8,128)S(1)}, u32[]{:S(2)}, u32[]{:S(2)}) %collective-permute-start.1) | collective-permute-done | bytes 16416 | tf_op jit(solution)/shard_map/ppermute | solution.py:288
  37.9 2.8 %shard_map.150 = (f32[256,256]{1,0:T(8,128)S(1)}, f32[32,256]{1,0:T(8,128)S(1)}, f32[64,256]{1,0:T(8,128)S(1)}) custom-call(s32[3]{0:T(128)} %copy-done.12, f32[256,1024]{1,0:T(8,128)} %proj.3, f32[32,256]{1,0:T(8,128)S(1)} %bitcast.25, f32[2,8,256]{2,1,0:T(8,128)S(1)} %pad_maximum_fusion.2.refs_0_, f32[2,8,256]{2,1,0:T(8,128)S(1)} %collective-permute-done.1.refs_1_, ...), custom_call_target="tpu_custom_call" | custom-call | tf_op jit(solution)/shard_map/pallas_call | solution.py:57
  40.7 5.6 %shard_map.151 = (f32[32,256]{1,0:T(8,128)}, f32[32,8,128]{2,1,0:T(8,128)S(1)}, f32[8,16,128]{2,1,0:T(8,128)S(1)}) custom-call(s32[2]{0:T(128)} %slice.3.place, f32[256,1024]{1,0:T(8,128)} %proj.3, f32[256,256]{1,0:T(8,128)} %out_w.2, f32[64,256]{1,0:T(8,128)S(1)} %get-tuple-element.13.bias_all, f32[256,256]{1,0:T(8,128)S(1)} %get-tuple-element.14.query, ...), custom_call_target="tpu_custom_call" | custom-call | tf_op jit(solution)/shard_map/pallas_call | solution.py:57
  46.3 14.4 %all_to_all.20 = f32[32,8,128]{2,1,0:T(8,128)S(1)} all-to-all(f32[32,8,128]{2,1,0:T(8,128)S(1)} %get-tuple-element.18), channel_id=1, replica_groups=mesh['branch'=2,'prow'=16,'pcol'=8] {'branch','prow'}, dimensions={0} | all-to-all | bytes 262144 | tf_op jit(solution)/shard_map/all_to_all | solution.py:323
  60.7 0.7 pad_maximum_fusion
  61.4 8.4 %all-to-all-start.1 = ((f32[8,48,128]{2,1,0:T(8,128)}), f32[8,48,128]{2,1,0:T(8,128)S(1)}, u32[]{:S(2)}, u32[]{:S(2)}) async-start(f32[8,48,128]{2,1,0:T(8,128)} %pad_maximum_fusion), calls=%async_computation.1 | async-start | bytes 393216 | tf_op jit(solution)/shard_map/all_to_all | solution.py:325
  69.7 0.7 copy-done.13
  70.7 9.9 %all-to-all-done.1.factors = f32[8,48,128]{2,1,0:T(8,128)S(1)} async-done(((f32[8,48,128]{2,1,0:T(8,128)}), f32[8,48,128]{2,1,0:T(8,128)S(1)}, u32[]{:S(2)}, u32[]{:S(2)}) %all-to-all-start.1) | async-done | bytes 196640 | tf_op jit(solution)/shard_map/all_to_all | solution.py:325
  80.7 5.1 %shard_map.152 = (f32[256,128]{1,0:T(8,128)S(1)}, f32[128,4,128]{2,1,0:T(4,128)S(1)}) custom-call(f32[8,48,128]{2,1,0:T(8,128)S(1)} %all-to-all-done.1.factors, f32[256,128]{1,0:T(8,128)S(1)} %bitcast.22, f32[1,256]{1,0:T(1,128)S(1)} %mul.38.valid, f32[1024,128]{1,0:T(8,128)S(1)} %copy-done, f32[128,512]{1,0:T(8,128)S(1)} %copy-done.4), custom_call_target="tpu_custom_call" | custom-call | tf_op jit(solution)/shard_map/pallas_call | solution.py:57
  85.8 19.1 %all_to_all.21 = f32[128,4,128]{2,1,0:T(4,128)S(1)} all-to-all(f32[128,4,128]{2,1,0:T(4,128)S(1)} %get-tuple-element.20), channel_id=1, replica_groups=mesh['branch'=2,'prow'=16,'pcol'=8] {'prow','pcol'}, dimensions={0} | all-to-all | bytes 524288 | tf_op jit(solution)/shard_map/all_to_all | solution.py:335
  104.9 1.5 %collective-permute-done.14 = f32[128,4,128]{2,1,0:T(4,128)S(1)} collective-permute-done((f32[128,4,128]{2,1,0:T(4,128)S(1)}, f32[128,4,128]{2,1,0:T(4,128)S(1)}, u32[]{:S(2)}, u32[]{:S(2)}) %collective-permute-start.14) | collective-permute-done | bytes 262176 | tf_op jit(solution)/shard_map/ppermute | solution.py:337
  106.5 2.0 %shard_map.153 = f32[256,128]{1,0:T(8,128)} custom-call(s32[1]{0:T(128)} %bitcast.place, f32[512,128]{1,0:T(8,128)S(1)} %bitcast.20, f32[512,128]{1,0:T(8,128)S(1)} %bitcast.27), custom_call_target="tpu_custom_call" | custom-call | tf_op jit(solution)/shard_map/pallas_call | solution.py:57
  108.5 8.0 %all-to-all-start.3 = ((f32[128,2,128]{2,1,0:T(2,128)}), f32[128,2,128]{2,1,0:T(2,128)S(1)}, u32[]{:S(2)}, u32[]{:S(2)}) async-start(f32[128,2,128]{2,1,0:T(2,128)} %bitcast.17), calls=%async_computation.3 | async-start | bytes 262144 | tf_op jit(solution)/shard_map/all_to_all | solution.py:341
  116.9 10.6 %all-to-all-done.3 = f32[128,2,128]{2,1,0:T(2,128)S(1)} async-done(((f32[128,2,128]{2,1,0:T(2,128)}), f32[128,2,128]{2,1,0:T(2,128)S(1)}, u32[]{:S(2)}, u32[]{:S(2)}) %all-to-all-start.3) | async-done | bytes 131104 | tf_op jit(solution)/shard_map/all_to_all | solution.py:341
  127.5 1.8 %shard_map.155 = f32[256,128]{1,0:T(8,128)} custom-call(f32[256,128]{1,0:T(8,128)S(1)} %bitcast.23, f32[256,128]{1,0:T(8,128)S(1)} %get-tuple-element.21.pair_one, f32[256,128]{1,0:T(8,128)S(1)} %shard_map.154.gate, f32[128,128]{1,0:T(8,128)S(1)} %copy-done.9, f32[128,512]{1,0:T(8,128)S(1)} %copy-done.5, f32[512,128]{1,0:T(8,128)S(1)} %copy-done.6), custom_call_target="tpu_custom_call" | custom-call | tf_op jit(solution)/shard_map/pallas_call | solution.py:57
  (49 shorter events, 2.1 us)
Async XLA Ops:
  0.6 0.8 copy-start.3
  0.7 0.7 copy-start.11
  0.7 0.7 copy-start.10
  1.4 0.9 copy-start.1
  2.7 6.8 %collective-permute-start.6 = (f32[72,128]{1,0:T(8,128)S(1)}, f32[72,128]{1,0:T(8,128)S(1)}, u32[]{:S(2)}, u32[]{:S(2)}) collective-permute-start(f32[72,128]{1,0:T(8,128)S(1)} %get-tuple-element.16), channel_id=1, source_target_pairs={{0,24},{8,16},{16,8},{24,0},{32,56},{40,48},{48,40},{56,32},{64,88... | collective-permute-start | bytes 110600 | tf_op jit(solution)/shard_map/ppermute | solution.py:288
  7.3 4.9 %collective-permute-start.5 = (f32[72,128]{1,0:T(8,128)S(1)}, f32[72,128]{1,0:T(8,128)S(1)}, u32[]{:S(2)}, u32[]{:S(2)}) collective-permute-start(f32[72,128]{1,0:T(8,128)S(1)} %get-tuple-element.16), channel_id=1, source_target_pairs={{0,16},{8,24},{16,0},{24,8},{32,48},{40,56},{48,32},{56,40},{64,80... | collective-permute-start | bytes 110600 | tf_op jit(solution)/shard_map/ppermute | solution.py:288
  7.3 4.9 %collective-permute-start.4 = (f32[72,128]{1,0:T(8,128)S(1)}, f32[72,128]{1,0:T(8,128)S(1)}, u32[]{:S(2)}, u32[]{:S(2)}) collective-permute-start(f32[72,128]{1,0:T(8,128)S(1)} %get-tuple-element.16), channel_id=1, source_target_pairs={{0,8},{8,0},{16,24},{24,16},{32,40},{40,32},{48,56},{56,48},{64,72... | collective-permute-start | bytes 110600 | tf_op jit(solution)/shard_map/ppermute | solution.py:288
  12.2 8.8 %collective-permute-start.9 = (f32[4,72,128]{2,1,0:T(8,128)S(1)}, f32[4,72,128]{2,1,0:T(8,128)S(1)}, u32[]{:S(2)}, u32[]{:S(2)}) collective-permute-start(f32[4,72,128]{2,1,0:T(8,128)S(1)} %pad_maximum_fusion.1.refs_0_), channel_id=1, source_target_pairs={{0,96},{8,104},{16,112},{24,120},{32,64},{40,72},{48,80},{56,88},{... | collective-permute-start | bytes 442376 | tf_op jit(solution)/shard_map/ppermute | solution.py:288
  13.8 7.7 %collective-permute-start.8 = (f32[4,72,128]{2,1,0:T(8,128)S(1)}, f32[4,72,128]{2,1,0:T(8,128)S(1)}, u32[]{:S(2)}, u32[]{:S(2)}) collective-permute-start(f32[4,72,128]{2,1,0:T(8,128)S(1)} %pad_maximum_fusion.1.refs_0_), channel_id=1, source_target_pairs={{0,64},{8,72},{16,80},{24,88},{32,96},{40,104},{48,112},{56,120},{... | collective-permute-start | bytes 442376 | tf_op jit(solution)/shard_map/ppermute | solution.py:288
  14.9 7.0 %collective-permute-start.7 = (f32[4,72,128]{2,1,0:T(8,128)S(1)}, f32[4,72,128]{2,1,0:T(8,128)S(1)}, u32[]{:S(2)}, u32[]{:S(2)}) collective-permute-start(f32[4,72,128]{2,1,0:T(8,128)S(1)} %pad_maximum_fusion.1.refs_0_), channel_id=1, source_target_pairs={{0,32},{8,40},{16,48},{24,56},{32,0},{40,8},{48,16},{56,24},{64,96... | collective-permute-start | bytes 442376 | tf_op jit(solution)/shard_map/ppermute | solution.py:288
  16.4 7.6 %collective-permute-start = (f32[8,256]{1,0:T(8,128)S(1)}, f32[8,256]{1,0:T(8,128)S(1)}, u32[]{:S(2)}, u32[]{:S(2)}) collective-permute-start(f32[8,256]{1,0:T(8,128)S(1)} %get-tuple-element.12), channel_id=1, source_target_pairs={{0,4},{1,5},{2,6},{3,7},{4,0},{5,1},{6,2},{7,3},{8,12},{9,13},{10,... | collective-permute-start | bytes 24584 | tf_op jit(solution)/shard_map/ppermute | solution.py:288
  21.0 19.7 %collective-permute-start.10 = (f32[4,72,128]{2,1,0:T(8,128)S(1)}, f32[4,72,128]{2,1,0:T(8,128)S(1)}, u32[]{:S(2)}, u32[]{:S(2)}) collective-permute-start(f32[4,72,128]{2,1,0:T(8,128)S(1)} %pad_maximum_fusion.1.refs_0_), channel_id=1, source_target_pairs={{0,128},{128,0},{1,129},{129,1},{2,130},{130,2},{3,131},{131,3},{4... | collective-permute-start | bytes 442376 | tf_op jit(solution)/shard_map/ppermute | solution.py:288
  21.0 19.7 %collective-permute-start.13 = (f32[4,72,128]{2,1,0:T(8,128)S(1)}, f32[4,72,128]{2,1,0:T(8,128)S(1)}, u32[]{:S(2)}, u32[]{:S(2)}) collective-permute-start(f32[4,72,128]{2,1,0:T(8,128)S(1)} %collective-permute-done.9.refs_3_), channel_id=1, source_target_pairs={{0,128},{128,0},{1,129},{129,1},{2,130},{130,2},{3,131},{131,3},{4... | collective-permute-start | bytes 442376 | tf_op jit(solution)/shard_map/ppermute | solution.py:288
  21.5 19.2 %collective-permute-start.12 = (f32[4,72,128]{2,1,0:T(8,128)S(1)}, f32[4,72,128]{2,1,0:T(8,128)S(1)}, u32[]{:S(2)}, u32[]{:S(2)}) collective-permute-start(f32[4,72,128]{2,1,0:T(8,128)S(1)} %collective-permute-done.8.refs_2_), channel_id=1, source_target_pairs={{0,128},{128,0},{1,129},{129,1},{2,130},{130,2},{3,131},{131,3},{4... | collective-permute-start | bytes 442376 | tf_op jit(solution)/shard_map/ppermute | solution.py:288
  21.9 18.8 %collective-permute-start.11 = (f32[4,72,128]{2,1,0:T(8,128)S(1)}, f32[4,72,128]{2,1,0:T(8,128)S(1)}, u32[]{:S(2)}, u32[]{:S(2)}) collective-permute-start(f32[4,72,128]{2,1,0:T(8,128)S(1)} %collective-permute-done.7.refs_1_), channel_id=1, source_target_pairs={{0,128},{128,0},{1,129},{129,1},{2,130},{130,2},{3,131},{131,3},{4... | collective-permute-start | bytes 442376 | tf_op jit(solution)/shard_map/ppermute | solution.py:288
  23.9 4.9 %collective-permute-start.3 = (f32[2,8,256]{2,1,0:T(8,128)S(1)}, f32[2,8,256]{2,1,0:T(8,128)S(1)}, u32[]{:S(2)}, u32[]{:S(2)}) collective-permute-start(f32[2,8,256]{2,1,0:T(8,128)S(1)} %pad_maximum_fusion.2.refs_0_), channel_id=1, source_target_pairs={{0,3},{1,2},{2,1},{3,0},{4,7},{5,6},{6,5},{7,4},{8,11},{9,10},{10,... | collective-permute-start | bytes 49160 | tf_op jit(solution)/shard_map/ppermute | solution.py:288
  28.9 5.2 %collective-permute-start.2 = (f32[2,8,256]{2,1,0:T(8,128)S(1)}, f32[2,8,256]{2,1,0:T(8,128)S(1)}, u32[]{:S(2)}, u32[]{:S(2)}) collective-permute-start(f32[2,8,256]{2,1,0:T(8,128)S(1)} %pad_maximum_fusion.2.refs_0_), channel_id=1, source_target_pairs={{0,2},{1,3},{2,0},{3,1},{4,6},{5,7},{6,4},{7,5},{8,10},{9,11},{10,... | collective-permute-start | bytes 49160 | tf_op jit(solution)/shard_map/ppermute | solution.py:288
  34.1 3.7 %collective-permute-start.1 = (f32[2,8,256]{2,1,0:T(8,128)S(1)}, f32[2,8,256]{2,1,0:T(8,128)S(1)}, u32[]{:S(2)}, u32[]{:S(2)}) collective-permute-start(f32[2,8,256]{2,1,0:T(8,128)S(1)} %pad_maximum_fusion.2.refs_0_), channel_id=1, source_target_pairs={{0,1},{1,0},{2,3},{3,2},{4,5},{5,4},{6,7},{7,6},{8,9},{9,8},{10,11... | collective-permute-start | bytes 49160 | tf_op jit(solution)/shard_map/ppermute | solution.py:288
  34.6 0.7 copy-start.12
  35.2 5.5 %copy-start.7 = (f32[256,64]{0,1:T(8,128)S(1)}, f32[256,64]{0,1:T(8,128)}, u32[]{:S(2)}) copy-start(f32[256,64]{0,1:T(8,128)} %param.21) | copy-start | bytes 196612
  46.3 34.3 %copy-start = (f32[1024,128]{1,0:T(8,128)S(1)}, f32[1024,128]{1,0:T(8,128)}, u32[]{:S(2)}) copy-start(f32[1024,128]{1,0:T(8,128)} %outer_w.1) | copy-start | bytes 1572868
  61.4 19.3 %copy-start.2 = (f32[8,32,128]{2,1,0:T(8,128)S(1)}, f32[8,32,128]{2,1,0:T(8,128)}, u32[]{:S(2)}) copy-start(f32[8,32,128]{2,1,0:T(8,128)} %param.14) | copy-start | bytes 393220
  61.4 19.3 %copy-start.4 = (f32[128,512]{1,0:T(8,128)S(1)}, f32[128,512]{1,0:T(8,128)}, u32[]{:S(2)}) copy-start(f32[128,512]{1,0:T(8,128)} %tri_w.1) | copy-start | bytes 786436
  61.4 19.3 %all-to-all-start.1 = ((f32[8,48,128]{2,1,0:T(8,128)}), f32[8,48,128]{2,1,0:T(8,128)S(1)}, u32[]{:S(2)}, u32[]{:S(2)}) async-start(f32[8,48,128]{2,1,0:T(8,128)} %pad_maximum_fusion), calls=%async_computation.1 | async-start | bytes 393216 | tf_op jit(solution)/shard_map/all_to_all | solution.py:325
  69.7 0.7 copy-start.13
  104.9 1.5 %collective-permute-start.14 = (f32[128,4,128]{2,1,0:T(4,128)S(1)}, f32[128,4,128]{2,1,0:T(4,128)S(1)}, u32[]{:S(2)}, u32[]{:S(2)}) collective-permute-start(f32[128,4,128]{2,1,0:T(4,128)S(1)} %all_to_all.21), channel_id=1, source_target_pairs={{0,128},{128,0},{1,129},{129,1},{2,130},{130,2},{3,131},{131,3},{4... | collective-permute-start | bytes 786440 | tf_op jit(solution)/shard_map/ppermute | solution.py:337
  106.5 10.1 %copy-start.8 = (f32[128,128]{1,0:T(8,128)S(1)}, f32[128,128]{1,0:T(8,128)}, u32[]{:S(2)}) copy-start(f32[128,128]{1,0:T(8,128)} %gate_w.1) | copy-start | bytes 196612
  108.5 19.0 %copy-start.5 = (f32[128,512]{1,0:T(8,128)S(1)}, f32[128,512]{1,0:T(8,128)}, u32[]{:S(2)}) copy-start(f32[128,512]{1,0:T(8,128)} %in_w.1) | copy-start | bytes 786436
  108.5 19.0 %copy-start.6 = (f32[512,128]{1,0:T(8,128)S(1)}, f32[512,128]{1,0:T(8,128)}, u32[]{:S(2)}) copy-start(f32[512,128]{1,0:T(8,128)} %last_w.1) | copy-start | bytes 786436
  108.5 19.0 %all-to-all-start.3 = ((f32[128,2,128]{2,1,0:T(2,128)}), f32[128,2,128]{2,1,0:T(2,128)S(1)}, u32[]{:S(2)}, u32[]{:S(2)}) async-start(f32[128,2,128]{2,1,0:T(2,128)} %bitcast.17), calls=%async_computation.3 | async-start | bytes 262144 | tf_op jit(solution)/shard_map/all_to_all | solution.py:341
  116.5 10.9 %copy-start.9 = (f32[128,128]{1,0:T(8,128)S(1)}, f32[128,128]{1,0:T(8,128)}, u32[]{:S(2)}) copy-start(f32[128,128]{1,0:T(8,128)} %out_w.3) | copy-start | bytes 196612

commit v3 on v2

--- a/solution.py
+++ b/solution.py
@@ -1,5 +1,3 @@
-import functools
-
 import jax
 import jax.numpy as jnp
 from jax import lax
@@ -8,7 +6,6 @@
 from jax.sharding import PartitionSpec as P
 
 
-highest = lax.Precision.HIGHEST
 epsilon = 1e-05
 f32 = jnp.float32
 bf16 = jnp.bfloat16
@@ -32,15 +29,34 @@
     return high, low
 
 
+def stacked_dot(left_parts, right_parts, dims):
+    rows = left_parts[0].shape[0]
+    terms = []
+    for skip, right in enumerate(right_parts):
+        used = left_parts[: len(left_parts) - skip]
+        wide = used[0] if len(used) == 1 else jnp.concatenate(used, axis=0)
+        product = lax.dot_general(wide, right, dims, preferred_element_type=f32)
+        terms += [(skip + n, product[n * rows : (n + 1) * rows]) for n in range(len(used))]
+    terms.sort(key=lambda term: -term[0])
+    total = terms[0][1]
+    for _, term in terms[1:]:
+        total = total + term
+    return total
+
+
+def split3(value):
+    high, rest = value.astype(bf16), value
+    rest = rest - high.astype(f32)
+    middle = rest.astype(bf16)
+    return high, middle, (rest - middle.astype(f32)).astype(bf16)
+
+
 def dot3(left, right, dims=NN):
-    left_high, left_low = split(left)
-    right_high, right_low = split(right)
-    one = functools.partial(lax.dot_general, dimension_numbers=dims, preferred_element_type=f32)
-    return one(left_high, right_high) + (one(left_high, right_low) + one(left_low, right_high))
+    return stacked_dot(split(left), split(right), dims)
 
 
 def dot6(left, right, dims=NN):
-    return lax.dot_general(left, right, dims, precision=highest, preferred_element_type=f32)
+    return stacked_dot(split3(left), split3(right), dims)
 
 
 def iota(shape, axis):
@@ -65,39 +81,25 @@
     return run
 
 
-def send_kernel(place, pair, align, mask, bias_w, x_send, bias_send):
+def send_kernel(low, align, mask, x_send):
     normed = layer_norm(align[...])
     lane = iota((8, 128), 1)
-    spread = ((lane % 8 == iota((8, 128), 0)) & (lane // 8 == place[0])).astype(f32)
+    spread = ((lane % 8 == iota((8, 128), 0)) & (lane // 8 == low[0])).astype(f32)
     mask_rows = jnp.concatenate([mask[...].astype(f32), jnp.zeros((4, 8), f32)], axis=0)
-    mask_tile = lax.dot_general(mask_rows, spread, NN, preferred_element_type=f32)
     x_send[0:32] = normed[:, 0:128]
     x_send[32:64] = normed[:, 128:256]
-    x_send[64:72] = mask_tile
+    x_send[64:72] = lax.dot_general(mask_rows, spread, NN, preferred_element_type=f32)
+
+
+def bias_kernel(pair, bias_w, bias_send):
     bias_send[...] = dot6(bias_w[...], layer_norm(pair[...]), NT)
 
 
-def query_kernel(place, proj, align, *refs):
-    pieces, (query_out, gate_out, bias_out, bias_s, proj_s, gate_s, sems) = refs[:4], refs[4:]
+def query_kernel(proj, align, query_out, gate_out, proj_s, gate_s, sems):
     first = pltpu.make_async_copy(proj.at[:, pl.ds(0, 512)], proj_s, sems.at[0])
     second = pltpu.make_async_copy(proj.at[:, pl.ds(768, 256)], gate_s, sems.at[1])
     first.start()
     second.start()
-    for step, piece in enumerate(pieces):
-        for high in range(2):
-            bias_s[place[1] ^ (step + 4 * high)] = piece[high]
-    chunk = iota((8, 128), 1) // 32
-    for i in range(8):
-        half, spot = divmod(i, 4)
-        for group, branch in enumerate((place[0], 1 - place[0])):
-            tile = jnp.zeros((8, 128), f32)
-            for c in range(4):
-                source = bias_s[branch * 4 + c, :, half * 128 : half * 128 + 128]
-                shift = ((c - spot) * 32) % 128
-                if shift:
-                    source = pltpu.roll(source, shift, 1)
-                tile = jnp.where(chunk == c, source, tile)
-            bias_out[i * 8 : i * 8 + 8, group * 128 : group * 128 + 128] = tile
     normed = layer_norm(align[...])
     first.wait()
     query = dot6(normed, proj_s[:, 0:256]) * 32 ** (-0.5)
@@ -108,16 +110,32 @@
     gate_out[...] = jax.nn.sigmoid(dot3(normed, gate_s[...]))
 
 
-def attend_kernel(place, proj, out_w, bias_all, query, gate, align, mask, outer_w, *refs):
-    pieces, (new_align, right_send, left_mask, x_s, mix_s, value_s, out_s, sems) = refs[:8], refs[8:]
+def attend_kernel(branch_of, col_of, low_of, proj, out_w, query, gate, align, mask, outer_w, *refs):
+    bias, pieces = refs[:4], refs[4:12]
+    new_align, right_send, left_mask, tiles_s, bias_s, x_s, mix_s, value_s, out_s, sems = refs[12:]
     value_copy = pltpu.make_async_copy(proj.at[:, pl.ds(512, 256)], value_s, sems.at[0])
     out_copy = pltpu.make_async_copy(out_w, out_s, sems.at[1])
     value_copy.start()
     out_copy.start()
+    for step, piece in enumerate(bias):
+        for high in range(2):
+            tiles_s[col_of[0] ^ (step + 4 * high)] = piece[high]
+    chunk = iota((8, 128), 1) // 32
+    for i in range(8):
+        half, spot = divmod(i, 4)
+        for group, branch in enumerate((branch_of[0], 1 - branch_of[0])):
+            tile = jnp.zeros((8, 128), f32)
+            for c in range(4):
+                source = tiles_s[branch * 4 + c, :, half * 128 : half * 128 + 128]
+                shift = ((c - spot) * 32) % 128
+                if shift:
+                    source = pltpu.roll(source, shift, 1)
+                tile = jnp.where(chunk == c, source, tile)
+            bias_s[i * 8 : i * 8 + 8, group * 128 : group * 128 + 128] = tile
     for index, piece in enumerate(pieces):
         swapped, step = divmod(index, 4)
         for low in range(4):
-            x_s[swapped, place[1] ^ (step * 4 + low)] = piece[low]
+            x_s[swapped, low_of[0] ^ (step * 4 + low)] = piece[low]
     x_own, x_other = x_s.at[0], x_s.at[1]
     lane = iota((8, 128), 1)
     chunk = lane // 32
@@ -126,7 +144,7 @@
         keys_own = keys_own + x_own[r, 64:72, :]
         keys_other = keys_other + x_other[r, 64:72, :]
     key_bias = 1000000000.0 * (jnp.concatenate([keys_own, keys_other], axis=1) - 1.0)
-    keys = (jnp.where(place[0] == 0, keys_own, keys_other), jnp.where(place[0] == 0, keys_other, keys_own))
+    keys = (jnp.where(branch_of[0] == 0, keys_own, keys_other), jnp.where(branch_of[0] == 0, keys_other, keys_own))
     for s in range(4):
         x_row = jnp.concatenate(
             [
@@ -136,7 +154,7 @@
             axis=0,
         )
         scores = dot6(query[s * 64 : s * 64 + 64, :], x_row, NT)
-        scores = (scores + bias_all[...]) + key_bias[s : s + 1, :]
+        scores = (scores + bias_s[...]) + key_bias[s : s + 1, :]
         weights = jnp.exp(scores - jnp.max(scores, axis=-1, keepdims=True))
         total = jnp.sum(weights, axis=-1, keepdims=True)
         mix_s[s * 64 : s * 64 + 64, :] = dot3(weights, x_row) / total
@@ -176,14 +194,16 @@
     lane = iota((8, 128), 1)
     expand_lane = iota((128, 512), 1)
     expand = (iota((128, 512), 0) == (expand_lane // 128) * 32 + expand_lane % 32).astype(bf16)
+    rights = factors[:, 0:32, :].reshape(256, 128)
+    both = jnp.concatenate(split(rights), axis=0)
+    wide = lax.dot_general(both, expand, NN, preferred_element_type=f32)
+    wide = (wide[0:256] + wide[256:512]).reshape(8, 32, 512)
     masks = []
     for c in range(8):
-        high, low = split(factors[c, 0:32, :])
-        wide = lax.dot_general(high, expand, NN, preferred_element_type=f32) + lax.dot_general(low, expand, NN, preferred_element_type=f32)
         left = factors[c, 32:40, :]
         masks.append(factors[c, 40:48, :])
         for s in range(4):
-            right_s[c * 4 + s] = wide[:, s * 128 : s * 128 + 128]
+            right_s[c * 4 + s] = wide[c, :, s * 128 : s * 128 + 128]
             for group in range(8):
                 index = s * 32 + group * 4 + lane // 32
                 left_s[c * 4 + s, :, group * 128 : group * 128 + 128] = jnp.take_along_axis(left, index, axis=1)
@@ -279,10 +299,10 @@
     col = lax.axis_index("pcol").astype(jnp.int32)
     pair = pair_rep.reshape(256, 128)
     align = alignment.reshape(32, 256)
-    place = jnp.stack([branch[0], col, row % 16])
-    x_send, bias_send = call(send_kernel, [(72, 128), (8, 256)], scalars=1)(
-        place[2:3], pair, align, row_mask, pair_bias_w.T
-    )
+    low = lax.axis_index("prow").astype(jnp.int32).reshape(1)
+    place = (branch, col.reshape(1), low)
+    (x_send,) = call(send_kernel, [(72, 128)], scalars=1)(low, align, row_mask)
+    (bias_send,) = call(bias_kernel, [(8, 256)])(pair, pair_bias_w.T)
 
     def swap(value, axis, size, step):
         return lax.ppermute(value, axis, [(d, d ^ step) for d in range(size)])
@@ -294,32 +314,28 @@
     bias_stack = jnp.stack(bias_stack)
     bias_own = [bias_stack] + [swap(bias_stack, "pcol", 8, step) for step in (1, 2, 3)]
     x_other = [swap(value, "branch", 2, 1) for value in x_own]
-    query, gate, bias_all = call(
+    query, gate = call(
         query_kernel,
-        [(256, 256), (32, 256), (64, 256)],
-        scratch=[
-            pltpu.VMEM((8, 8, 256), f32),
-            pltpu.VMEM((256, 512), f32),
-            pltpu.VMEM((256, 256), f32),
-            pltpu.SemaphoreType.DMA((2,)),
-        ],
-        scalars=1,
+        [(256, 256), (32, 256)],
+        scratch=[pltpu.VMEM((256, 512), f32), pltpu.VMEM((256, 256), f32), pltpu.SemaphoreType.DMA((2,))],
         far=1,
-    )(place, attention_in, align, *bias_own)
+    )(attention_in, align)
     new_align, right_send, left_mask = call(
         attend_kernel,
         [(32, 256), (32, 8, 128), (8, 16, 128)],
         scratch=[
+            pltpu.VMEM((8, 8, 256), f32),
+            pltpu.VMEM((64, 256), f32),
             pltpu.VMEM((2, 16, 72, 128), f32),
             pltpu.VMEM((256, 256), f32),
             pltpu.VMEM((256, 256), f32),
             pltpu.VMEM((256, 256), f32),
             pltpu.SemaphoreType.DMA((2,)),
         ],
-        scalars=1,
+        scalars=3,
         far=2,
         kept=(0,),
-    )(place[::2], attention_in, attention_out, bias_all, query, gate, align, row_mask, outer_in.T, *x_own, *x_other)
+    )(*place, attention_in, attention_out, query, gate, align, row_mask, outer_in.T, *bias_own, *x_own, *x_other)
     right_all = lax.all_to_all(right_send, ROWS, 0, 0, tiled=True)
     factor_send = jnp.concatenate([right_all.reshape(8, 32, 128), left_mask], axis=1)
     factors = lax.all_to_all(factor_send, "pcol", 0, 0, tiled=True)

time: 131 us -> 127 us (0.969)
  Pallas kernels: 18.1 us -> 14.9 us
  starting transfers between devices: 36.5 us -> 39.5 us
  waiting for transfers between devices: 36.3 us -> 34.4 us
    pallas_call x7 -> x8, Pallas kernels: 18.1 us -> 14.9 us  [run(): pl.pallas_call(kernel, out_shape=outs, in_specs=[smem] * scalars + [pl.Bl...]
    ppermute x14, waiting for transfers between devices: 14.3 us -> 12.4 us  [swap(): return lax.ppermute(value, axis, [(d, d ^ step) for d in range(size)])]
    ppermute x14, starting transfers between devices: 20.1 us -> 21.8 us  [swap(): return lax.ppermute(value, axis, [(d, d ^ step) for d in range(size)])]
  transfers between devices with their start and end apart: 17 -> 17, of which waited for: 10 -> 9; matrix products, arithmetic and copies ran while one was open for 1% -> 0% of each run, Pallas kernels for 2% -> 2%
where the time goes in v3:
time: 127 us; the launch traced here: 126 us
  starting transfers between devices  39.5 us (31%)
  waiting for transfers between devices  34.4 us (27%)
  blocking collectives  33 us (26%)
  Pallas kernels  14.9 us (12%)
  local copies, waits for them, and re-layouts  2.37 us (2%)
    ppermute x14, starting transfers between devices, swap(): return lax.ppermute(value, axis, [(d, d ^ step) for d in range(size)])  21.8 us
    all_to_all x1, blocking collectives, shards(): own_edges = lax.all_to_all(edge_send, CHIPS, 0, 0, tiled=True)  19.1 us
    pallas_call x8, Pallas kernels, run(): pl.pallas_call(kernel, out_shape=outs, in_specs=[smem] * scalars + [pl.Bl...  14.9 us
    all_to_all x1, blocking collectives, shards(): right_all = lax.all_to_all(right_send, ROWS, 0, 0, tiled=True)  13.8 us
    ppermute x14, waiting for transfers between devices, swap(): return lax.ppermute(value, axis, [(d, d ^ step) for d in range(size)])  12.4 us
    all_to_all x1, waiting for transfers between devices, shards(): lax.all_to_all(cross_send.reshape(128, 2, 128), CHIPS, 0, 0, tiled=True)  10.6 us
    all_to_all x1, waiting for transfers between devices, shards(): factors = lax.all_to_all(factor_send, 'pcol', 0, 0, tiled=True)  9.93 us
    all_to_all x1, starting transfers between devices, shards(): factors = lax.all_to_all(factor_send, 'pcol', 0, 0, tiled=True)  9.64 us
  transfers between devices with their start and end apart: 17, of which 9 were waited for; matrix products, arithmetic and copies ran while one was open for 0% of the time, Pallas kernels for 2%

profile of v3, /device:TPU:2, one launch (start us, length us, event | category | flops | bytes accessed | tf_op | source)
XLA Modules:
  0.0 125.7 jit_solution(8415718390700126875)
XLA Ops:
  0.6 0.7 copy-done.9
  1.3 0.8 copy-done.2
  2.2 2.0 %collective-permute-start.4 = (f32[72,128]{1,0:T(8,128)S(1)}, f32[72,128]{1,0:T(8,128)S(1)}, u32[]{:S(2)}, u32[]{:S(2)}) collective-permute-start(f32[72,128]{1,0:T(8,128)S(1)} %shard_map.151), channel_id=1, source_target_pairs={{0,8},{8,0},{16,24},{24,16},{32,40},{40,32},{48,56},{56,48},{64,72... | collective-permute-start | bytes 110600 | tf_op jit(solution)/shard_map/ppermute | solution.py:308
  4.3 3.3 %collective-permute-start.5 = (f32[72,128]{1,0:T(8,128)S(1)}, f32[72,128]{1,0:T(8,128)S(1)}, u32[]{:S(2)}, u32[]{:S(2)}) collective-permute-start(f32[72,128]{1,0:T(8,128)S(1)} %shard_map.151), channel_id=1, source_target_pairs={{0,16},{8,24},{16,0},{24,8},{32,48},{40,56},{48,32},{56,40},{64,80... | collective-permute-start | bytes 110600 | tf_op jit(solution)/shard_map/ppermute | solution.py:308
  7.5 2.6 %collective-permute-done.5 = f32[72,128]{1,0:T(8,128)S(1)} collective-permute-done((f32[72,128]{1,0:T(8,128)S(1)}, f32[72,128]{1,0:T(8,128)S(1)}, u32[]{:S(2)}, u32[]{:S(2)}) %collective-permute-start.5) | collective-permute-done | bytes 36896 | tf_op jit(solution)/shard_map/ppermute | solution.py:308
  10.2 3.1 %collective-permute-done.6 = f32[72,128]{1,0:T(8,128)S(1)} collective-permute-done((f32[72,128]{1,0:T(8,128)S(1)}, f32[72,128]{1,0:T(8,128)S(1)}, u32[]{:S(2)}, u32[]{:S(2)}) %collective-permute-start.6) | collective-permute-done | bytes 36896 | tf_op jit(solution)/shard_map/ppermute | solution.py:308
  13.3 0.6 collective-permute-start.7
  13.9 2.4 %collective-permute-start.8 = (f32[4,72,128]{2,1,0:T(8,128)S(1)}, f32[4,72,128]{2,1,0:T(8,128)S(1)}, u32[]{:S(2)}, u32[]{:S(2)}) collective-permute-start(f32[4,72,128]{2,1,0:T(8,128)S(1)} %pad_maximum_fusion.1.refs_4_), channel_id=1, source_target_pairs={{0,64},{8,72},{16,80},{24,88},{32,96},{40,104},{48,112},{56,120},{... | collective-permute-start | bytes 442376 | tf_op jit(solution)/shard_map/ppermute | solution.py:308
  16.3 0.5 collective-permute-start.9
  17.2 4.6 %collective-permute-start = (f32[8,256]{1,0:T(8,128)S(1)}, f32[8,256]{1,0:T(8,128)S(1)}, u32[]{:S(2)}, u32[]{:S(2)}) collective-permute-start(f32[8,256]{1,0:T(8,128)S(1)} %shard_map.150), channel_id=1, source_target_pairs={{0,4},{1,5},{2,6},{3,7},{4,0},{5,1},{6,2},{7,3},{8,12},{9,13},{10,... | collective-permute-start | bytes 24584 | tf_op jit(solution)/shard_map/ppermute | solution.py:308
  21.8 0.5 collective-permute-start.11
  22.4 0.6 collective-permute-done.9.refs_7_
  23.0 1.9 %collective-permute-done = f32[8,256]{1,0:T(8,128)S(1)} collective-permute-done((f32[8,256]{1,0:T(8,128)S(1)}, f32[8,256]{1,0:T(8,128)S(1)}, u32[]{:S(2)}, u32[]{:S(2)}) %collective-permute-start) | collective-permute-done | bytes 8224 | tf_op jit(solution)/shard_map/ppermute | solution.py:308
  24.9 1.6 %collective-permute-start.1 = (f32[2,8,256]{2,1,0:T(8,128)S(1)}, f32[2,8,256]{2,1,0:T(8,128)S(1)}, u32[]{:S(2)}, u32[]{:S(2)}) collective-permute-start(f32[2,8,256]{2,1,0:T(8,128)S(1)} %pad_maximum_fusion.2.refs_0_), channel_id=1, source_target_pairs={{0,1},{1,0},{2,3},{3,2},{4,5},{5,4},{6,7},{7,6},{8,9},{9,8},{10,11... | collective-permute-start | bytes 49160 | tf_op jit(solution)/shard_map/ppermute | solution.py:308
  26.4 2.2 %collective-permute-done.1.refs_1_ = f32[2,8,256]{2,1,0:T(8,128)S(1)} collective-permute-done((f32[2,8,256]{2,1,0:T(8,128)S(1)}, f32[2,8,256]{2,1,0:T(8,128)S(1)}, u32[]{:S(2)}, u32[]{:S(2)}) %collective-permute-start.1) | collective-permute-done | bytes 16416 | tf_op jit(solution)/shard_map/ppermute | solution.py:308
  28.6 3.2 %collective-permute-start.2 = (f32[2,8,256]{2,1,0:T(8,128)S(1)}, f32[2,8,256]{2,1,0:T(8,128)S(1)}, u32[]{:S(2)}, u32[]{:S(2)}) collective-permute-start(f32[2,8,256]{2,1,0:T(8,128)S(1)} %pad_maximum_fusion.2.refs_0_), channel_id=1, source_target_pairs={{0,2},{1,3},{2,0},{3,1},{4,6},{5,7},{6,4},{7,5},{8,10},{9,11},{10,... | collective-permute-start | bytes 49160 | tf_op jit(solution)/shard_map/ppermute | solution.py:308
  31.8 2.0 %collective-permute-done.2.refs_2_ = f32[2,8,256]{2,1,0:T(8,128)S(1)} collective-permute-done((f32[2,8,256]{2,1,0:T(8,128)S(1)}, f32[2,8,256]{2,1,0:T(8,128)S(1)}, u32[]{:S(2)}, u32[]{:S(2)}) %collective-permute-start.2) | collective-permute-done | bytes 16416 | tf_op jit(solution)/shard_map/ppermute | solution.py:308
  33.8 3.0 %collective-permute-start.3 = (f32[2,8,256]{2,1,0:T(8,128)S(1)}, f32[2,8,256]{2,1,0:T(8,128)S(1)}, u32[]{:S(2)}, u32[]{:S(2)}) collective-permute-start(f32[2,8,256]{2,1,0:T(8,128)S(1)} %pad_maximum_fusion.2.refs_0_), channel_id=1, source_target_pairs={{0,3},{1,2},{2,1},{3,0},{4,7},{5,6},{6,5},{7,4},{8,11},{9,10},{10,... | collective-permute-start | bytes 49160 | tf_op jit(solution)/shard_map/ppermute | solution.py:308
  36.9 1.9 %shard_map.149 = (f32[256,256]{1,0:T(8,128)S(1)}, f32[32,256]{1,0:T(8,128)S(1)}) custom-call(f32[256,1024]{1,0:T(8,128)} %proj.3, f32[32,256]{1,0:T(8,128)S(1)} %bitcast.25), custom_call_target="tpu_custom_call" | custom-call | tf_op jit(solution)/shard_map/pallas_call | solution.py:73
  38.9 3.3 %shard_map.152 = (f32[32,256]{1,0:T(8,128)}, f32[32,8,128]{2,1,0:T(8,128)S(1)}, f32[8,16,128]{2,1,0:T(8,128)S(1)}) custom-call(s32[1]{0:T(128)} %bitcast.branch_of.place, s32[1]{0:T(128)} %bitcast.1.col_of, s32[1]{0:T(128)} %bitcast.2.low.low_of, f32[256,1024]{1,0:T(8,128)} %proj.3, f32[256,256]{1,0:T(8,128)} %out_w.2, ...), custom_call_target="tpu_custom_call" | custom-call | tf_op jit(solution)/shard_map/pallas_call | solution.py:73
  42.2 13.8 %all_to_all.20 = f32[32,8,128]{2,1,0:T(8,128)S(1)} all-to-all(f32[32,8,128]{2,1,0:T(8,128)S(1)} %get-tuple-element.12), channel_id=1, replica_groups=mesh['branch'=2,'prow'=16,'pcol'=8] {'branch','prow'}, dimensions={0} | all-to-all | bytes 262144 | tf_op jit(solution)/shard_map/all_to_all | solution.py:339
  56.0 0.7 pad_maximum_fusion
  56.7 9.6 %all-to-all-start.1 = ((f32[8,48,128]{2,1,0:T(8,128)}), f32[8,48,128]{2,1,0:T(8,128)S(1)}, u32[]{:S(2)}, u32[]{:S(2)}) async-start(f32[8,48,128]{2,1,0:T(8,128)} %pad_maximum_fusion), calls=%async_computation.1 | async-start | bytes 393216 | tf_op jit(solution)/shard_map/all_to_all | solution.py:341
  66.3 0.7 copy-done.11
  67.3 9.9 %all-to-all-done.1.factors = f32[8,48,128]{2,1,0:T(8,128)S(1)} async-done(((f32[8,48,128]{2,1,0:T(8,128)}), f32[8,48,128]{2,1,0:T(8,128)S(1)}, u32[]{:S(2)}, u32[]{:S(2)}) %all-to-all-start.1) | async-done | bytes 196640 | tf_op jit(solution)/shard_map/all_to_all | solution.py:341
  77.2 5.1 %shard_map.153 = (f32[256,128]{1,0:T(8,128)S(1)}, f32[128,4,128]{2,1,0:T(4,128)S(1)}) custom-call(f32[8,48,128]{2,1,0:T(8,128)S(1)} %all-to-all-done.1.factors, f32[256,128]{1,0:T(8,128)S(1)} %bitcast.22, f32[1,256]{1,0:T(1,128)S(1)} %mul.38.valid, f32[1024,128]{1,0:T(8,128)S(1)} %copy-done, f32[128,512]{1,0:T(8,128)S(1)} %copy-done.3), custom_call_target="tpu_custom_call" | custom-call | tf_op jit(solution)/shard_map/pallas_call | solution.py:73
  82.3 19.1 %all_to_all.21 = f32[128,4,128]{2,1,0:T(4,128)S(1)} all-to-all(f32[128,4,128]{2,1,0:T(4,128)S(1)} %get-tuple-element.14), channel_id=1, replica_groups=mesh['branch'=2,'prow'=16,'pcol'=8] {'prow','pcol'}, dimensions={0} | all-to-all | bytes 524288 | tf_op jit(solution)/shard_map/all_to_all | solution.py:351
  101.5 1.5 %collective-permute-done.14 = f32[128,4,128]{2,1,0:T(4,128)S(1)} collective-permute-done((f32[128,4,128]{2,1,0:T(4,128)S(1)}, f32[128,4,128]{2,1,0:T(4,128)S(1)}, u32[]{:S(2)}, u32[]{:S(2)}) %collective-permute-start.14) | collective-permute-done | bytes 262176 | tf_op jit(solution)/shard_map/ppermute | solution.py:353
  103.0 1.9 %shard_map.154 = f32[256,128]{1,0:T(8,128)} custom-call(s32[1]{0:T(128)} %bitcast.branch_of.place, f32[512,128]{1,0:T(8,128)S(1)} %bitcast.20, f32[512,128]{1,0:T(8,128)S(1)} %bitcast.27), custom_call_target="tpu_custom_call" | custom-call | tf_op jit(solution)/shard_map/pallas_call | solution.py:73
  104.9 8.0 %all-to-all-start.3 = ((f32[128,2,128]{2,1,0:T(2,128)}), f32[128,2,128]{2,1,0:T(2,128)S(1)}, u32[]{:S(2)}, u32[]{:S(2)}) async-start(f32[128,2,128]{2,1,0:T(2,128)} %bitcast.17), calls=%async_computation.3 | async-start | bytes 262144 | tf_op jit(solution)/shard_map/all_to_all | solution.py:357
  113.4 10.6 %all-to-all-done.3 = f32[128,2,128]{2,1,0:T(2,128)S(1)} async-done(((f32[128,2,128]{2,1,0:T(2,128)}), f32[128,2,128]{2,1,0:T(2,128)S(1)}, u32[]{:S(2)}, u32[]{:S(2)}) %all-to-all-start.3) | async-done | bytes 131104 | tf_op jit(solution)/shard_map/all_to_all | solution.py:357
  123.9 1.8 %shard_map.156 = f32[256,128]{1,0:T(8,128)} custom-call(f32[256,128]{1,0:T(8,128)S(1)} %bitcast.23, f32[256,128]{1,0:T(8,128)S(1)} %get-tuple-element.15.pair_one, f32[256,128]{1,0:T(8,128)S(1)} %shard_map.155.gate, f32[128,128]{1,0:T(8,128)S(1)} %copy-done.7, f32[128,512]{1,0:T(8,128)S(1)} %copy-done.4, f32[512,128]{1,0:T(8,128)S(1)} %copy-done.5), custom_call_target="tpu_custom_call" | custom-call | tf_op jit(solution)/shard_map/pallas_call | solution.py:73
  (44 shorter events, 1.3 us)
Async XLA Ops:
  0.6 0.7 copy-start.9
  1.3 0.8 copy-start.2
  2.2 5.3 %collective-permute-start.4 = (f32[72,128]{1,0:T(8,128)S(1)}, f32[72,128]{1,0:T(8,128)S(1)}, u32[]{:S(2)}, u32[]{:S(2)}) collective-permute-start(f32[72,128]{1,0:T(8,128)S(1)} %shard_map.151), channel_id=1, source_target_pairs={{0,8},{8,0},{16,24},{24,16},{32,40},{40,32},{48,56},{56,48},{64,72... | collective-permute-start | bytes 110600 | tf_op jit(solution)/shard_map/ppermute | solution.py:308
  4.3 5.9 %collective-permute-start.5 = (f32[72,128]{1,0:T(8,128)S(1)}, f32[72,128]{1,0:T(8,128)S(1)}, u32[]{:S(2)}, u32[]{:S(2)}) collective-permute-start(f32[72,128]{1,0:T(8,128)S(1)} %shard_map.151), channel_id=1, source_target_pairs={{0,16},{8,24},{16,0},{24,8},{32,48},{40,56},{48,32},{56,40},{64,80... | collective-permute-start | bytes 110600 | tf_op jit(solution)/shard_map/ppermute | solution.py:308
  7.5 5.8 %collective-permute-start.6 = (f32[72,128]{1,0:T(8,128)S(1)}, f32[72,128]{1,0:T(8,128)S(1)}, u32[]{:S(2)}, u32[]{:S(2)}) collective-permute-start(f32[72,128]{1,0:T(8,128)S(1)} %shard_map.151), channel_id=1, source_target_pairs={{0,24},{8,16},{16,8},{24,0},{32,56},{40,48},{48,40},{56,32},{64,88... | collective-permute-start | bytes 110600 | tf_op jit(solution)/shard_map/ppermute | solution.py:308
  13.3 3.6 %copy-start.1 = (f32[8,32,128]{2,1,0:T(8,128)S(1)}, f32[8,32,128]{2,1,0:T(8,128)}, u32[]{:S(2)}) copy-start(f32[8,32,128]{2,1,0:T(8,128)} %param.14) | copy-start | bytes 393220
  13.3 3.6 %copy-start.10 = (f32[128,8]{0,1:T(8,128)S(1)}, f32[128,8]{0,1:T(8,128)}, u32[]{:S(2)}) copy-start(f32[128,8]{0,1:T(8,128)} %param.19) | copy-start | bytes 12292
  13.3 8.5 %collective-permute-start.7 = (f32[4,72,128]{2,1,0:T(8,128)S(1)}, f32[4,72,128]{2,1,0:T(8,128)S(1)}, u32[]{:S(2)}, u32[]{:S(2)}) collective-permute-start(f32[4,72,128]{2,1,0:T(8,128)S(1)} %pad_maximum_fusion.1.refs_4_), channel_id=1, source_target_pairs={{0,32},{8,40},{16,48},{24,56},{32,0},{40,8},{48,16},{56,24},{64,96... | collective-permute-start | bytes 442376 | tf_op jit(solution)/shard_map/ppermute | solution.py:308
  13.9 8.4 %collective-permute-start.8 = (f32[4,72,128]{2,1,0:T(8,128)S(1)}, f32[4,72,128]{2,1,0:T(8,128)S(1)}, u32[]{:S(2)}, u32[]{:S(2)}) collective-permute-start(f32[4,72,128]{2,1,0:T(8,128)S(1)} %pad_maximum_fusion.1.refs_4_), channel_id=1, source_target_pairs={{0,64},{8,72},{16,80},{24,88},{32,96},{40,104},{48,112},{56,120},{... | collective-permute-start | bytes 442376 | tf_op jit(solution)/shard_map/ppermute | solution.py:308
  16.3 6.6 %collective-permute-start.9 = (f32[4,72,128]{2,1,0:T(8,128)S(1)}, f32[4,72,128]{2,1,0:T(8,128)S(1)}, u32[]{:S(2)}, u32[]{:S(2)}) collective-permute-start(f32[4,72,128]{2,1,0:T(8,128)S(1)} %pad_maximum_fusion.1.refs_4_), channel_id=1, source_target_pairs={{0,96},{8,104},{16,112},{24,120},{32,64},{40,72},{48,80},{56,88},{... | collective-permute-start | bytes 442376 | tf_op jit(solution)/shard_map/ppermute | solution.py:308
  17.2 7.6 %collective-permute-start = (f32[8,256]{1,0:T(8,128)S(1)}, f32[8,256]{1,0:T(8,128)S(1)}, u32[]{:S(2)}, u32[]{:S(2)}) collective-permute-start(f32[8,256]{1,0:T(8,128)S(1)} %shard_map.150), channel_id=1, source_target_pairs={{0,4},{1,5},{2,6},{3,7},{4,0},{5,1},{6,2},{7,3},{8,12},{9,13},{10,... | collective-permute-start | bytes 24584 | tf_op jit(solution)/shard_map/ppermute | solution.py:308
  21.8 17.0 %collective-permute-start.10 = (f32[4,72,128]{2,1,0:T(8,128)S(1)}, f32[4,72,128]{2,1,0:T(8,128)S(1)}, u32[]{:S(2)}, u32[]{:S(2)}) collective-permute-start(f32[4,72,128]{2,1,0:T(8,128)S(1)} %pad_maximum_fusion.1.refs_4_), channel_id=1, source_target_pairs={{0,128},{128,0},{1,129},{129,1},{2,130},{130,2},{3,131},{131,3},{4... | collective-permute-start | bytes 442376 | tf_op jit(solution)/shard_map/ppermute | solution.py:308
  21.8 17.0 %collective-permute-start.11 = (f32[4,72,128]{2,1,0:T(8,128)S(1)}, f32[4,72,128]{2,1,0:T(8,128)S(1)}, u32[]{:S(2)}, u32[]{:S(2)}) collective-permute-start(f32[4,72,128]{2,1,0:T(8,128)S(1)} %collective-permute-done.7.refs_5_), channel_id=1, source_target_pairs={{0,128},{128,0},{1,129},{129,1},{2,130},{130,2},{3,131},{131,3},{4... | collective-permute-start | bytes 442376 | tf_op jit(solution)/shard_map/ppermute | solution.py:308
  22.3 16.5 %collective-permute-start.12 = (f32[4,72,128]{2,1,0:T(8,128)S(1)}, f32[4,72,128]{2,1,0:T(8,128)S(1)}, u32[]{:S(2)}, u32[]{:S(2)}) collective-permute-start(f32[4,72,128]{2,1,0:T(8,128)S(1)} %collective-permute-done.8.refs_6_), channel_id=1, source_target_pairs={{0,128},{128,0},{1,129},{129,1},{2,130},{130,2},{3,131},{131,3},{4... | collective-permute-start | bytes 442376 | tf_op jit(solution)/shard_map/ppermute | solution.py:308
  23.0 15.9 %collective-permute-start.13 = (f32[4,72,128]{2,1,0:T(8,128)S(1)}, f32[4,72,128]{2,1,0:T(8,128)S(1)}, u32[]{:S(2)}, u32[]{:S(2)}) collective-permute-start(f32[4,72,128]{2,1,0:T(8,128)S(1)} %collective-permute-done.9.refs_7_), channel_id=1, source_target_pairs={{0,128},{128,0},{1,129},{129,1},{2,130},{130,2},{3,131},{131,3},{4... | collective-permute-start | bytes 442376 | tf_op jit(solution)/shard_map/ppermute | solution.py:308
  24.9 3.7 %collective-permute-start.1 = (f32[2,8,256]{2,1,0:T(8,128)S(1)}, f32[2,8,256]{2,1,0:T(8,128)S(1)}, u32[]{:S(2)}, u32[]{:S(2)}) collective-permute-start(f32[2,8,256]{2,1,0:T(8,128)S(1)} %pad_maximum_fusion.2.refs_0_), channel_id=1, source_target_pairs={{0,1},{1,0},{2,3},{3,2},{4,5},{5,4},{6,7},{7,6},{8,9},{9,8},{10,11... | collective-permute-start | bytes 49160 | tf_op jit(solution)/shard_map/ppermute | solution.py:308
  28.6 5.2 %collective-permute-start.2 = (f32[2,8,256]{2,1,0:T(8,128)S(1)}, f32[2,8,256]{2,1,0:T(8,128)S(1)}, u32[]{:S(2)}, u32[]{:S(2)}) collective-permute-start(f32[2,8,256]{2,1,0:T(8,128)S(1)} %pad_maximum_fusion.2.refs_0_), channel_id=1, source_target_pairs={{0,2},{1,3},{2,0},{3,1},{4,6},{5,7},{6,4},{7,5},{8,10},{9,11},{10,... | collective-permute-start | bytes 49160 | tf_op jit(solution)/shard_map/ppermute | solution.py:308
  33.8 5.0 %collective-permute-start.3 = (f32[2,8,256]{2,1,0:T(8,128)S(1)}, f32[2,8,256]{2,1,0:T(8,128)S(1)}, u32[]{:S(2)}, u32[]{:S(2)}) collective-permute-start(f32[2,8,256]{2,1,0:T(8,128)S(1)} %pad_maximum_fusion.2.refs_0_), channel_id=1, source_target_pairs={{0,3},{1,2},{2,1},{3,0},{4,7},{5,6},{6,5},{7,4},{8,11},{9,10},{10,... | collective-permute-start | bytes 49160 | tf_op jit(solution)/shard_map/ppermute | solution.py:308
  36.9 2.0 %copy-start.8 = (f32[256,64]{0,1:T(8,128)S(1)}, f32[256,64]{0,1:T(8,128)}, u32[]{:S(2)}) copy-start(f32[256,64]{0,1:T(8,128)} %param.21) | copy-start | bytes 196612
  42.1 35.1 %copy-start = (f32[1024,128]{1,0:T(8,128)S(1)}, f32[1024,128]{1,0:T(8,128)}, u32[]{:S(2)}) copy-start(f32[1024,128]{1,0:T(8,128)} %outer_w.1) | copy-start | bytes 1572868
  56.7 20.6 %copy-start.3 = (f32[128,512]{1,0:T(8,128)S(1)}, f32[128,512]{1,0:T(8,128)}, u32[]{:S(2)}) copy-start(f32[128,512]{1,0:T(8,128)} %tri_w.1) | copy-start | bytes 786436
  56.7 20.6 %all-to-all-start.1 = ((f32[8,48,128]{2,1,0:T(8,128)}), f32[8,48,128]{2,1,0:T(8,128)S(1)}, u32[]{:S(2)}, u32[]{:S(2)}) async-start(f32[8,48,128]{2,1,0:T(8,128)} %pad_maximum_fusion), calls=%async_computation.1 | async-start | bytes 393216 | tf_op jit(solution)/shard_map/all_to_all | solution.py:341
  66.3 0.7 copy-start.11
  101.5 1.5 %collective-permute-start.14 = (f32[128,4,128]{2,1,0:T(4,128)S(1)}, f32[128,4,128]{2,1,0:T(4,128)S(1)}, u32[]{:S(2)}, u32[]{:S(2)}) collective-permute-start(f32[128,4,128]{2,1,0:T(4,128)S(1)} %all_to_all.21), channel_id=1, source_target_pairs={{0,128},{128,0},{1,129},{129,1},{2,130},{130,2},{3,131},{131,3},{4... | collective-permute-start | bytes 786440 | tf_op jit(solution)/shard_map/ppermute | solution.py:353
  103.0 10.0 %copy-start.6 = (f32[128,128]{1,0:T(8,128)S(1)}, f32[128,128]{1,0:T(8,128)}, u32[]{:S(2)}) copy-start(f32[128,128]{1,0:T(8,128)} %gate_w.1) | copy-start | bytes 196612
  104.9 19.0 %copy-start.4 = (f32[128,512]{1,0:T(8,128)S(1)}, f32[128,512]{1,0:T(8,128)}, u32[]{:S(2)}) copy-start(f32[128,512]{1,0:T(8,128)} %in_w.1) | copy-start | bytes 786436
  104.9 19.0 %copy-start.5 = (f32[512,128]{1,0:T(8,128)S(1)}, f32[512,128]{1,0:T(8,128)}, u32[]{:S(2)}) copy-start(f32[512,128]{1,0:T(8,128)} %last_w.1) | copy-start | bytes 786436
  104.9 19.0 %all-to-all-start.3 = ((f32[128,2,128]{2,1,0:T(2,128)}), f32[128,2,128]{2,1,0:T(2,128)S(1)}, u32[]{:S(2)}, u32[]{:S(2)}) async-start(f32[128,2,128]{2,1,0:T(2,128)} %bitcast.17), calls=%async_computation.3 | async-start | bytes 262144 | tf_op jit(solution)/shard_map/all_to_all | solution.py:357
  113.0 10.9 %copy-start.7 = (f32[128,128]{1,0:T(8,128)S(1)}, f32[128,128]{1,0:T(8,128)}, u32[]{:S(2)}) copy-start(f32[128,128]{1,0:T(8,128)} %out_w.3) | copy-start | bytes 196612

commit v4 on v3

--- a/solution.py
+++ b/solution.py
@@ -63,13 +63,14 @@
     return lax.broadcasted_iota(jnp.int32, shape, axis)
 
 
-def call(kernel, out_shapes, scratch=(), scalars=0, far=0, kept=()):
+def call(kernel, out_shapes, scratch=(), scalars=0, far=0, loose=0, kept=()):
     vmem = pl.BlockSpec(memory_space=pltpu.VMEM)
     smem = pl.BlockSpec(memory_space=pltpu.SMEM)
     outs = [jax.ShapeDtypeStruct(shape, f32) if n in kept else pltpu.VMEM(shape, f32) for n, shape in enumerate(out_shapes)]
 
     def run(*args):
-        arrays = [pltpu.with_memory_space_constraint(arg, pltpu.VMEM) for arg in args[scalars + far :]]
+        arrays = list(args[scalars + far : scalars + far + loose])
+        arrays += [pltpu.with_memory_space_constraint(arg, pltpu.VMEM) for arg in args[scalars + far + loose :]]
         return pl.pallas_call(
             kernel,
             out_shape=outs,
@@ -81,14 +82,19 @@
     return run
 
 
-def send_kernel(low, align, mask, x_send):
+def send_kernel(low, pair, align, mask, x_send, pair_near, align_near, mask_near, sem):
+    copy = pltpu.make_async_copy(pair, pair_near, sem)
+    copy.start()
+    align_near[...] = align[...]
     normed = layer_norm(align[...])
     lane = iota((8, 128), 1)
     spread = ((lane % 8 == iota((8, 128), 0)) & (lane // 8 == low[0])).astype(f32)
     mask_rows = jnp.concatenate([mask[...].astype(f32), jnp.zeros((4, 8), f32)], axis=0)
+    mask_near[...] = mask_rows
     x_send[0:32] = normed[:, 0:128]
     x_send[32:64] = normed[:, 128:256]
     x_send[64:72] = lax.dot_general(mask_rows, spread, NN, preferred_element_type=f32)
+    copy.wait()
 
 
 def bias_kernel(pair, bias_w, bias_send):
@@ -110,9 +116,11 @@
     gate_out[...] = jax.nn.sigmoid(dot3(normed, gate_s[...]))
 
 
-def attend_kernel(branch_of, col_of, low_of, proj, out_w, query, gate, align, mask, outer_w, *refs):
+def attend_kernel(branch_of, col_of, low_of, proj, out_w, outer_w, query, gate, align, mask, *refs):
     bias, pieces = refs[:4], refs[4:12]
-    new_align, right_send, left_mask, tiles_s, bias_s, x_s, mix_s, value_s, out_s, sems = refs[12:]
+    new_align, right_send, left_mask, tiles_s, bias_s, x_s, mix_s, value_s, out_s, outer_s, sems = refs[12:]
+    outer_copy = pltpu.make_async_copy(outer_w, outer_s, sems.at[2])
+    outer_copy.start()
     value_copy = pltpu.make_async_copy(proj.at[:, pl.ds(512, 256)], value_s, sems.at[0])
     out_copy = pltpu.make_async_copy(out_w, out_s, sems.at[1])
     value_copy.start()
@@ -145,39 +153,45 @@
         keys_other = keys_other + x_other[r, 64:72, :]
     key_bias = 1000000000.0 * (jnp.concatenate([keys_own, keys_other], axis=1) - 1.0)
     keys = (jnp.where(branch_of[0] == 0, keys_own, keys_other), jnp.where(branch_of[0] == 0, keys_other, keys_own))
-    for s in range(4):
-        x_row = jnp.concatenate(
+    x_rows = [
+        jnp.concatenate(
             [
                 jnp.concatenate([half[:, t * 32 + s * 8 : t * 32 + s * 8 + 8, :].reshape(128, 128) for t in range(2)], axis=1)
                 for half in (x_own, x_other)
             ],
             axis=0,
         )
-        scores = dot6(query[s * 64 : s * 64 + 64, :], x_row, NT)
-        scores = (scores + bias_s[...]) + key_bias[s : s + 1, :]
-        weights = jnp.exp(scores - jnp.max(scores, axis=-1, keepdims=True))
-        total = jnp.sum(weights, axis=-1, keepdims=True)
-        mix_s[s * 64 : s * 64 + 64, :] = dot3(weights, x_row) / total
+        for s in range(4)
+    ]
+    x_parts = [split3(x_row) for x_row in x_rows]
+    scores = [stacked_dot(split3(query[s * 64 : s * 64 + 64, :]), x_parts[s], NT) for s in range(4)]
+    scores = [(scores[s] + bias_s[...]) + key_bias[s : s + 1, :] for s in range(4)]
+    weights = [jnp.exp(score - jnp.max(score, axis=-1, keepdims=True)) for score in scores]
+    totals = [jnp.sum(weight, axis=-1, keepdims=True) for weight in weights]
+    for s in range(4):
+        mix_s[s * 64 : s * 64 + 64, :] = stacked_dot(split(weights[s]), x_parts[s][:2], NN) / totals[s]
     value_copy.wait()
     out_copy.wait()
+    outer_copy.wait()
     values = dot3(mix_s[...], value_s[...]).reshape(32, 8, 256)
     own_head = iota((32, 8, 256), 1) == iota((32, 8, 256), 2) // 32
     mixed = jnp.sum(jnp.where(own_head, values, 0.0), axis=1)
     updated = align[...] + dot3(mixed * gate[...], out_s[...])
     new_align[...] = updated
-    mask_rows = jnp.concatenate([mask[...].astype(f32), jnp.zeros((4, 8), f32)], axis=0)
+    mask_rows = mask[...]
     by_row = (iota((32, 8), 1) == iota((32, 8), 0) // 8).astype(f32)
     mask_wide = lax.dot_general(by_row, mask_rows, NN, preferred_element_type=f32)
     mask_col = jnp.sum(jnp.where(iota((32, 8), 1) == iota((32, 8), 0) % 8, mask_wide, 0.0), axis=1, keepdims=True)
-    factors = dot3(layer_norm(updated), outer_w[...], NT) * mask_col
+    factors = dot3(layer_norm(updated), outer_s[...], NT) * mask_col
     wide_lane = iota((64, 256), 1)
-    expand = (iota((64, 256), 0) == wide_lane % 32 + 32 * (wide_lane // 128)).astype(f32)
+    right_place = 32 + (wide_lane % 128) // 32 * 8 + wide_lane % 8
+    expand = (iota((64, 256), 0) == jnp.where(wide_lane < 128, wide_lane % 32, right_place)).astype(f32)
     wide = dot6(factors, expand)
     left = jnp.zeros((8, 128), f32)
     right = jnp.zeros((8, 128), f32)
     for s in range(4):
         left = jnp.where(chunk == s, wide[s * 8 : s * 8 + 8, 0:128], left)
-        right = jnp.where(chunk == s, wide[s * 8 : s * 8 + 8, 128:256], right)
+        right = jnp.where(lane % 32 // 8 == s, wide[s * 8 : s * 8 + 8, 128:256], right)
     for peer in range(32):
         right_send[peer] = right
     own = lax.dot_general(mask_rows, (lane == iota((8, 128), 0) + 32).astype(f32), NN, preferred_element_type=f32)
@@ -190,37 +204,46 @@
         left_mask[c, 8:16] = jnp.where(chunk == 0, tile, own)
 
 
+def merge_kernel(right_all, left_mask, merged):
+    for c in range(8):
+        merged[c, 0:32] = right_all[c * 32 : c * 32 + 32]
+        merged[c, 32:48] = left_mask[c]
+
+
 def outer_kernel(factors, pair, valid, outer_w, tri_w, pair_one, edge_send, right_s, left_s, sum_s):
     lane = iota((8, 128), 1)
-    expand_lane = iota((128, 512), 1)
-    expand = (iota((128, 512), 0) == (expand_lane // 128) * 32 + expand_lane % 32).astype(bf16)
-    rights = factors[:, 0:32, :].reshape(256, 128)
-    both = jnp.concatenate(split(rights), axis=0)
-    wide = lax.dot_general(both, expand, NN, preferred_element_type=f32)
-    wide = (wide[0:256] + wide[256:512]).reshape(8, 32, 512)
+    chunk = iota((32, 128), 1) // 32
+    for group in range(4):
+        for half in range(2):
+            tile = jnp.zeros((32, 128), f32)
+            for c in range(4):
+                source = factors[half * 4 + c, 0:32, :]
+                shift = ((c - group) * 32) % 128
+                if shift:
+                    source = pltpu.roll(source, shift, 1)
+                tile = jnp.where(chunk == c, source, tile)
+            right_s[group * 32 : group * 32 + 32, half * 128 : half * 128 + 128] = tile
     masks = []
     for c in range(8):
         left = factors[c, 32:40, :]
         masks.append(factors[c, 40:48, :])
         for s in range(4):
-            right_s[c * 4 + s] = wide[c, :, s * 128 : s * 128 + 128]
-            for group in range(8):
-                index = s * 32 + group * 4 + lane // 32
-                left_s[c * 4 + s, :, group * 128 : group * 128 + 128] = jnp.take_along_axis(left, index, axis=1)
-
-    def one_row(i, carry):
-        total = [jnp.zeros((32, 128), f32) for _ in range(8)]
-        for s in range(32):
-            right = right_s[s]
-            row = left_s[s, pl.ds(i, 1), :]
-            for group in range(8):
-                total[group] = total[group] + right * row[:, group * 128 : group * 128 + 128]
-        for group in range(8):
-            sum_s[pl.ds(i * 32, 32), group * 128 : group * 128 + 128] = total[group]
-        return carry
-
-    lax.fori_loop(0, 8, one_row, 0)
-    outer = dot3(sum_s[...], outer_w[...])
+            for half in range(2):
+                index = s * 32 + half * 16 + lane // 8
+                left_s[c * 4 + s, :, half * 128 : half * 128 + 128] = jnp.take_along_axis(left, index, axis=1)
+    right_high, right_low = split(right_s[...])
+    right_both = jnp.concatenate([right_high, right_low], axis=0)
+    diagonal = iota((32, 8, 256), 1) == iota((32, 8, 256), 2) % 8
+    for i in range(8):
+        rows = jnp.broadcast_to(left_s[:, i : i + 1, :], (32, 8, 256))
+        left_high, left_low = split(jnp.where(diagonal, rows, 0.0).reshape(256, 256))
+        product = lax.dot_general(right_both, left_high, NN, preferred_element_type=f32)
+        product = product[0:128] + (product[128:256] + lax.dot_general(right_high, left_low, NN, preferred_element_type=f32))
+        for group in range(4):
+            sum_s[i * 32 : i * 32 + 32, group * 256 : group * 256 + 256] = product[group * 32 : group * 32 + 32]
+    weights = outer_w[...].reshape(32, 4, 8, 128)
+    weights = jnp.concatenate([weights[:, group].reshape(256, 128) for group in range(4)], axis=0)
+    outer = dot3(sum_s[...], weights)
     mask_all = jnp.concatenate(masks, axis=0).astype(bf16)
     counts = lax.dot_general(mask_all.T, mask_all, NN, preferred_element_type=f32)
     count = jnp.concatenate([counts[0:32, 32 + i : 33 + i] for i in range(8)], axis=0)
@@ -235,34 +258,57 @@
     edge_send[:, 3, :] = right_edge[:, 128:256]
 
 
-def cross_kernel(place, own, other, cross_send, left_s, right_s):
+def cross_half(left_parts, edges, right_s, store):
+    chunk = iota((16, 128), 1) // 32
+    for c in range(8):
+        for h in range(2):
+            right = edges[pl.ds(c * 4 + 2 + h, 16, stride=32), :]
+            for m in range(4):
+                part = jnp.where(chunk == m, right, 0.0)
+                part = part + pltpu.roll(part, 32, 1)
+                part = part + pltpu.roll(part, 64, 1)
+                right_s[c, pl.ds(h * 4 + m, 16, stride=8), :] = part
+    right_parts = split(jnp.concatenate([right_s[c] for c in range(8)], axis=1))
+    crossed = stacked_dot(left_parts, right_parts, NT)
+    for h in range(2):
+        for c in range(4):
+            tile = jnp.zeros((16, 128), f32)
+            for m in range(4):
+                part = crossed[(m * 2 + h) * 16 : (m * 2 + h) * 16 + 16, :]
+                shift = ((m - c) * 32) % 128
+                if shift:
+                    part = pltpu.roll(part, shift, 1)
+                tile = jnp.where(chunk == m, part, tile)
+            store(c, h, tile)
+
+
+def cross_kernel(own, left_out, tiles_out, right_s):
     chunk = iota((16, 128), 1) // 32
     for c in range(8):
         for h in range(2):
             left = own[pl.ds(c * 4 + h, 16, stride=32), :]
             for m in range(4):
                 start = (m * 2 + h) * 16
-                left_s[start : start + 16, c * 128 : c * 128 + 128] = jnp.where(chunk == m, left, 0.0)
-            for half, source in enumerate((own, other)):
-                right = source[pl.ds(c * 4 + 2 + h, 16, stride=32), :]
-                for m in range(4):
-                    part = jnp.where(chunk == m, right, 0.0)
-                    part = part + pltpu.roll(part, 32, 1)
-                    part = part + pltpu.roll(part, 64, 1)
-                    right_s[half, c, pl.ds(h * 4 + m, 16, stride=8), :] = part
-    for half in range(2):
-        crossed = dot3(left_s[...], jnp.concatenate([right_s[half, c] for c in range(8)], axis=1), NT)
-        branch = place[0] if half == 0 else 1 - place[0]
-        for c in range(4):
-            for h in range(2):
-                tile = jnp.zeros((16, 128), f32)
-                for m in range(4):
-                    part = crossed[(m * 2 + h) * 16 : (m * 2 + h) * 16 + 16, :]
-                    shift = ((m - c) * 32) % 128
-                    if shift:
-                        part = pltpu.roll(part, shift, 1)
-                    tile = jnp.where(chunk == m, part, tile)
-                cross_send[pl.ds((branch * 4 + c) * 2 + h, 16, stride=16), :] = tile
+                left_out[start : start + 16, c * 128 : c * 128 + 128] = jnp.where(chunk == m, left, 0.0)
+
+    def store(c, h, tile):
+        tiles_out[(c * 2 + h) * 16 : (c * 2 + h) * 16 + 16, :] = tile
+
+    cross_half(split(left_out[...]), own, right_s, store)
+
+
+def cross_rest_kernel(branch_of, left, tiles, other, cross_send, right_s):
+    def store_at(branch):
+        def store(c, h, tile):
+            cross_send[pl.ds((branch * 4 + c) * 2 + h, 16, stride=16), :] = tile
+
+        return store
+
+    store_own = store_at(branch_of[0])
+    for c in range(4):
+        for h in range(2):
+            store_own(c, h, tiles[(c * 2 + h) * 16 : (c * 2 + h) * 16 + 16, :])
+    cross_half(split(left[...]), other, right_s, store_at(1 - branch_of[0]))
 
 
 def gate_kernel(pair_one, gate_w, gate_out):
@@ -301,8 +347,15 @@
     align = alignment.reshape(32, 256)
     low = lax.axis_index("prow").astype(jnp.int32).reshape(1)
     place = (branch, col.reshape(1), low)
-    (x_send,) = call(send_kernel, [(72, 128)], scalars=1)(low, align, row_mask)
-    (bias_send,) = call(bias_kernel, [(8, 256)])(pair, pair_bias_w.T)
+    x_send, pair_near, align_near, mask_near = call(
+        send_kernel,
+        [(72, 128), (256, 128), (32, 256), (8, 8)],
+        scratch=[pltpu.SemaphoreType.DMA],
+        scalars=1,
+        far=1,
+        loose=2,
+    )(low, pair, align, row_mask)
+    (bias_send,) = call(bias_kernel, [(8, 256)])(pair_near, pair_bias_w.T)
 
     def swap(value, axis, size, step):
         return lax.ppermute(value, axis, [(d, d ^ step) for d in range(size)])
@@ -319,7 +372,7 @@
         [(256, 256), (32, 256)],
         scratch=[pltpu.VMEM((256, 512), f32), pltpu.VMEM((256, 256), f32), pltpu.SemaphoreType.DMA((2,))],
         far=1,
-    )(attention_in, align)
+    )(attention_in, align_near)
     new_align, right_send, left_mask = call(
         attend_kernel,
         [(32, 256), (32, 8, 128), (8, 16, 128)],
@@ -330,14 +383,15 @@
             pltpu.VMEM((256, 256), f32),
             pltpu.VMEM((256, 256), f32),
             pltpu.VMEM((256, 256), f32),
-            pltpu.SemaphoreType.DMA((2,)),
+            pltpu.VMEM((64, 256), f32),
+            pltpu.SemaphoreType.DMA((3,)),
         ],
         scalars=3,
-        far=2,
+        far=3,
         kept=(0,),
-    )(*place, attention_in, attention_out, query, gate, align, row_mask, outer_in.T, *bias_own, *x_own, *x_other)
+    )(*place, attention_in, attention_out, outer_in.T, query, gate, align_near, mask_near, *bias_own, *x_own, *x_other)
     right_all = lax.all_to_all(right_send, ROWS, 0, 0, tiled=True)
-    factor_send = jnp.concatenate([right_all.reshape(8, 32, 128), left_mask], axis=1)
+    (factor_send,) = call(merge_kernel, [(8, 48, 128)], kept=(0,))(right_all.reshape(256, 128), left_mask)
     factors = lax.all_to_all(factor_send, "pcol", 0, 0, tiled=True)
     res_float = residue_mask.astype(f32)
     row_valid = lax.dynamic_slice_in_dim(res_float, row * 8, 8)
@@ -346,14 +400,17 @@
     pair_one, edge_send = call(
         outer_kernel,
         [(256, 128), (128, 4, 128)],
-        scratch=[pltpu.VMEM((32, 32, 128), f32), pltpu.VMEM((32, 8, 1024), f32), pltpu.VMEM((256, 1024), f32)],
+        scratch=[pltpu.VMEM((128, 256), f32), pltpu.VMEM((32, 8, 256), f32), pltpu.VMEM((256, 1024), f32)],
     )(factors, pair, valid, outer_out, triangle_in)
     own_edges = lax.all_to_all(edge_send, CHIPS, 0, 0, tiled=True)
     (tri_gate,) = call(gate_kernel, [(256, 128)])(pair_one, triangle_gate)
     other_edges = lax.ppermute(own_edges, "branch", [(0, 1), (1, 0)])
+    left_wide, tiles = call(
+        cross_kernel, [(128, 1024), (128, 128)], scratch=[pltpu.VMEM((8, 128, 128), f32)]
+    )(own_edges.reshape(512, 128))
     (cross_send,) = call(
-        cross_kernel, [(256, 128)], scratch=[pltpu.VMEM((128, 1024), f32), pltpu.VMEM((2, 8, 128, 128), f32)], scalars=1
-    )(branch, own_edges.reshape(512, 128), other_edges.reshape(512, 128))
+        cross_rest_kernel, [(256, 128)], scratch=[pltpu.VMEM((8, 128, 128), f32)], scalars=1
+    )(branch, left_wide, tiles, other_edges.reshape(512, 128))
     crossed = lax.all_to_all(cross_send.reshape(128, 2, 128), CHIPS, 0, 0, tiled=True)
     (new_pair,) = call(final_kernel, [(256, 128)], scratch=[pltpu.VMEM((256, 128), f32)], kept=(0,))(
         crossed.reshape(256, 128), pair_one, tri_gate, triangle_out, transit_in, transit_out

time: 127 us -> 123 us (0.969)
  local copies, waits for them, and re-layouts: 2.37 us -> 0.94 us
    unnamed x24 -> x18, local copies, waits for them, and re-layouts: 2.14 us -> 0.71 us
    pallas_call x8 -> x10, Pallas kernels: 14.9 us -> 14.1 us  [run(): pl.pallas_call(kernel, out_shape=outs, in_specs=[smem] * scalars + [pl.Bl...]
  transfers between devices with their start and end apart: 17 -> 17, of which waited for: 9 -> 9; matrix products, arithmetic and copies ran while one was open for 0% -> 0% of each run, Pallas kernels for 2% -> 3%
where the time goes in v4:
time: 123 us; the launch traced here: 122 us
  starting transfers between devices  39.5 us (32%)
  waiting for transfers between devices  33.6 us (27%)
  blocking collectives  33 us (27%)
  Pallas kernels  14.1 us (11%)
    ppermute x14, starting transfers between devices, swap(): return lax.ppermute(value, axis, [(d, d ^ step) for d in range(size)])  21.8 us
    all_to_all x1, blocking collectives, shards(): own_edges = lax.all_to_all(edge_send, CHIPS, 0, 0, tiled=True)  19.1 us
    pallas_call x10, Pallas kernels, run(): pl.pallas_call(kernel, out_shape=outs, in_specs=[smem] * scalars + [pl.Bl...  14.1 us
    all_to_all x1, blocking collectives, shards(): right_all = lax.all_to_all(right_send, ROWS, 0, 0, tiled=True)  13.8 us
    ppermute x14, waiting for transfers between devices, swap(): return lax.ppermute(value, axis, [(d, d ^ step) for d in range(size)])  12.4 us
    all_to_all x1, waiting for transfers between devices, shards(): lax.all_to_all(cross_send.reshape(128, 2, 128), CHIPS, 0, 0, tiled=True)  10.6 us
    all_to_all x1, waiting for transfers between devices, shards(): factors = lax.all_to_all(factor_send, 'pcol', 0, 0, tiled=True)  9.93 us
    all_to_all x1, starting transfers between devices, shards(): factors = lax.all_to_all(factor_send, 'pcol', 0, 0, tiled=True)  9.67 us
  transfers between devices with their start and end apart: 17, of which 9 were waited for; matrix products, arithmetic and copies ran while one was open for 0% of the time, Pallas kernels for 3%

profile of v4, /device:TPU:2, one launch (start us, length us, event | category | flops | bytes accessed | tf_op | source)
XLA Modules:
  0.0 122.1 jit_solution(2911742883355183539)
XLA Ops:
  0.6 1.7 %shard_map.149 = (f32[72,128]{1,0:T(8,128)S(1)}, f32[256,128]{1,0:T(8,128)S(1)}, f32[32,256]{1,0:T(8,128)S(1)}, f32[8,8]{1,0:T(8,128)S(1)}) custom-call(s32[1]{0:T(128)} %bitcast.2.low.low_of, f32[256,128]{1,0:T(8,128)} %bitcast.21, f32[32,256]{1,0:T(8,128)} %bitcast.34, s32[4,8]{1,0:T(4,128)} %mask.1), custom_call_target="tpu_custom_call" | custom-call | tf_op jit(solution)/shard_map/pallas_call | solution.py:74
  2.3 2.0 %collective-permute-start.4 = (f32[72,128]{1,0:T(8,128)S(1)}, f32[72,128]{1,0:T(8,128)S(1)}, u32[]{:S(2)}, u32[]{:S(2)}) collective-permute-start(f32[72,128]{1,0:T(8,128)S(1)} %get-tuple-element.20), channel_id=1, source_target_pairs={{0,8},{8,0},{16,24},{24,16},{32,40},{40,32},{48,56},{56,48},{64,72... | collective-permute-start | bytes 110600 | tf_op jit(solution)/shard_map/ppermute | solution.py:361
  4.3 3.3 %collective-permute-start.5 = (f32[72,128]{1,0:T(8,128)S(1)}, f32[72,128]{1,0:T(8,128)S(1)}, u32[]{:S(2)}, u32[]{:S(2)}) collective-permute-start(f32[72,128]{1,0:T(8,128)S(1)} %get-tuple-element.20), channel_id=1, source_target_pairs={{0,16},{8,24},{16,0},{24,8},{32,48},{40,56},{48,32},{56,40},{64,80... | collective-permute-start | bytes 110600 | tf_op jit(solution)/shard_map/ppermute | solution.py:361
  7.6 2.6 %collective-permute-done.5 = f32[72,128]{1,0:T(8,128)S(1)} collective-permute-done((f32[72,128]{1,0:T(8,128)S(1)}, f32[72,128]{1,0:T(8,128)S(1)}, u32[]{:S(2)}, u32[]{:S(2)}) %collective-permute-start.5) | collective-permute-done | bytes 36896 | tf_op jit(solution)/shard_map/ppermute | solution.py:361
  10.2 3.1 %collective-permute-done.6 = f32[72,128]{1,0:T(8,128)S(1)} collective-permute-done((f32[72,128]{1,0:T(8,128)S(1)}, f32[72,128]{1,0:T(8,128)S(1)}, u32[]{:S(2)}, u32[]{:S(2)}) %collective-permute-start.6) | collective-permute-done | bytes 36896 | tf_op jit(solution)/shard_map/ppermute | solution.py:361
  13.4 0.6 collective-permute-start.7
  14.0 2.4 %collective-permute-start.8 = (f32[4,72,128]{2,1,0:T(8,128)S(1)}, f32[4,72,128]{2,1,0:T(8,128)S(1)}, u32[]{:S(2)}, u32[]{:S(2)}) collective-permute-start(f32[4,72,128]{2,1,0:T(8,128)S(1)} %pad_maximum_fusion.refs_4_), channel_id=1, source_target_pairs={{0,64},{8,72},{16,80},{24,88},{32,96},{40,104},{48,112},{56,120},{... | collective-permute-start | bytes 442376 | tf_op jit(solution)/shard_map/ppermute | solution.py:361
  16.4 0.5 collective-permute-start.9
  17.3 4.6 %collective-permute-start = (f32[8,256]{1,0:T(8,128)S(1)}, f32[8,256]{1,0:T(8,128)S(1)}, u32[]{:S(2)}, u32[]{:S(2)}) collective-permute-start(f32[8,256]{1,0:T(8,128)S(1)} %shard_map.151), channel_id=1, source_target_pairs={{0,4},{1,5},{2,6},{3,7},{4,0},{5,1},{6,2},{7,3},{8,12},{9,13},{10,... | collective-permute-start | bytes 24584 | tf_op jit(solution)/shard_map/ppermute | solution.py:361
  21.9 0.5 collective-permute-start.11
  22.5 0.6 collective-permute-done.9.refs_7_
  23.1 1.9 %collective-permute-done = f32[8,256]{1,0:T(8,128)S(1)} collective-permute-done((f32[8,256]{1,0:T(8,128)S(1)}, f32[8,256]{1,0:T(8,128)S(1)}, u32[]{:S(2)}, u32[]{:S(2)}) %collective-permute-start) | collective-permute-done | bytes 8224 | tf_op jit(solution)/shard_map/ppermute | solution.py:361
  24.9 1.6 %collective-permute-start.1 = (f32[2,8,256]{2,1,0:T(8,128)S(1)}, f32[2,8,256]{2,1,0:T(8,128)S(1)}, u32[]{:S(2)}, u32[]{:S(2)}) collective-permute-start(f32[2,8,256]{2,1,0:T(8,128)S(1)} %pad_maximum_fusion.1.refs_0_), channel_id=1, source_target_pairs={{0,1},{1,0},{2,3},{3,2},{4,5},{5,4},{6,7},{7,6},{8,9},{9,8},{10,11... | collective-permute-start | bytes 49160 | tf_op jit(solution)/shard_map/ppermute | solution.py:361
  26.5 2.2 %collective-permute-done.1.refs_1_ = f32[2,8,256]{2,1,0:T(8,128)S(1)} collective-permute-done((f32[2,8,256]{2,1,0:T(8,128)S(1)}, f32[2,8,256]{2,1,0:T(8,128)S(1)}, u32[]{:S(2)}, u32[]{:S(2)}) %collective-permute-start.1) | collective-permute-done | bytes 16416 | tf_op jit(solution)/shard_map/ppermute | solution.py:361
  28.7 3.2 %collective-permute-start.2 = (f32[2,8,256]{2,1,0:T(8,128)S(1)}, f32[2,8,256]{2,1,0:T(8,128)S(1)}, u32[]{:S(2)}, u32[]{:S(2)}) collective-permute-start(f32[2,8,256]{2,1,0:T(8,128)S(1)} %pad_maximum_fusion.1.refs_0_), channel_id=1, source_target_pairs={{0,2},{1,3},{2,0},{3,1},{4,6},{5,7},{6,4},{7,5},{8,10},{9,11},{10,... | collective-permute-start | bytes 49160 | tf_op jit(solution)/shard_map/ppermute | solution.py:361
  31.9 2.0 %collective-permute-done.2.refs_2_ = f32[2,8,256]{2,1,0:T(8,128)S(1)} collective-permute-done((f32[2,8,256]{2,1,0:T(8,128)S(1)}, f32[2,8,256]{2,1,0:T(8,128)S(1)}, u32[]{:S(2)}, u32[]{:S(2)}) %collective-permute-start.2) | collective-permute-done | bytes 16416 | tf_op jit(solution)/shard_map/ppermute | solution.py:361
  33.9 3.0 %collective-permute-start.3 = (f32[2,8,256]{2,1,0:T(8,128)S(1)}, f32[2,8,256]{2,1,0:T(8,128)S(1)}, u32[]{:S(2)}, u32[]{:S(2)}) collective-permute-start(f32[2,8,256]{2,1,0:T(8,128)S(1)} %pad_maximum_fusion.1.refs_0_), channel_id=1, source_target_pairs={{0,3},{1,2},{2,1},{3,0},{4,7},{5,6},{6,5},{7,4},{8,11},{9,10},{10,... | collective-permute-start | bytes 49160 | tf_op jit(solution)/shard_map/ppermute | solution.py:361
  36.9 1.9 %shard_map.150 = (f32[256,256]{1,0:T(8,128)S(1)}, f32[32,256]{1,0:T(8,128)S(1)}) custom-call(f32[256,1024]{1,0:T(8,128)} %proj.3, f32[32,256]{1,0:T(8,128)S(1)} %get-tuple-element.15.align), custom_call_target="tpu_custom_call" | custom-call | tf_op jit(solution)/shard_map/pallas_call | solution.py:74
  38.9 2.8 %shard_map.152 = (f32[32,256]{1,0:T(8,128)}, f32[32,8,128]{2,1,0:T(8,128)S(1)}, f32[8,16,128]{2,1,0:T(8,128)S(1)}) custom-call(s32[1]{0:T(128)} %bitcast.branch_of, s32[1]{0:T(128)} %bitcast.1.col_of, s32[1]{0:T(128)} %bitcast.2.low.low_of, f32[256,1024]{1,0:T(8,128)} %proj.3, f32[256,256]{1,0:T(8,128)} %out_w.2, f32[64,256]{1,0:T(8,128)} %bitcast.30, ...), custom_call_target="tpu_custom_call" | custom-call | tf_op jit(solution)/shard_map/pallas_call | solution.py:74
  41.8 13.8 %all_to_all.20 = f32[32,8,128]{2,1,0:T(8,128)S(1)} all-to-all(f32[32,8,128]{2,1,0:T(8,128)S(1)} %get-tuple-element.22), channel_id=1, replica_groups=mesh['branch'=2,'prow'=16,'pcol'=8] {'branch','prow'}, dimensions={0} | all-to-all | bytes 262144 | tf_op jit(solution)/shard_map/all_to_all | solution.py:393
  55.6 0.7 shard_map.153
  56.3 9.7 %all-to-all-start.1 = ((f32[8,48,128]{2,1,0:T(8,128)}), f32[8,48,128]{2,1,0:T(8,128)S(1)}, u32[]{:S(2)}, u32[]{:S(2)}) async-start(f32[8,48,128]{2,1,0:T(8,128)} %shard_map.153), calls=%async_computation.1 | async-start | bytes 393216 | tf_op jit(solution)/shard_map/all_to_all | solution.py:395
  66.0 0.7 copy-done.8
  66.9 9.9 %all-to-all-done.1.factors = f32[8,48,128]{2,1,0:T(8,128)S(1)} async-done(((f32[8,48,128]{2,1,0:T(8,128)}), f32[8,48,128]{2,1,0:T(8,128)S(1)}, u32[]{:S(2)}, u32[]{:S(2)}) %all-to-all-start.1) | async-done | bytes 196640 | tf_op jit(solution)/shard_map/all_to_all | solution.py:395
  76.9 2.3 %shard_map.154 = (f32[256,128]{1,0:T(8,128)S(1)}, f32[128,4,128]{2,1,0:T(4,128)S(1)}) custom-call(f32[8,48,128]{2,1,0:T(8,128)S(1)} %all-to-all-done.1.factors, f32[256,128]{1,0:T(8,128)S(1)} %bitcast.22, f32[1,256]{1,0:T(1,128)S(1)} %mul.38.valid, f32[1024,128]{1,0:T(8,128)S(1)} %copy-done, f32[128,512]{1,0:T(8,128)S(1)} %copy-done.2), custom_call_target="tpu_custom_call" | custom-call | tf_op jit(solution)/shard_map/pallas_call | solution.py:74
  79.2 19.1 %all_to_all.21 = f32[128,4,128]{2,1,0:T(4,128)S(1)} all-to-all(f32[128,4,128]{2,1,0:T(4,128)S(1)} %get-tuple-element.24), channel_id=1, replica_groups=mesh['branch'=2,'prow'=16,'pcol'=8] {'prow','pcol'}, dimensions={0} | all-to-all | bytes 524288 | tf_op jit(solution)/shard_map/all_to_all | solution.py:405
  98.3 0.8 shard_map.155
  99.1 0.7 collective-permute-done.14
  99.9 1.4 %shard_map.156 = f32[256,128]{1,0:T(8,128)} custom-call(s32[1]{0:T(128)} %bitcast.branch_of, f32[128,1024]{1,0:T(8,128)S(1)} %get-tuple-element.25.left, f32[128,128]{1,0:T(8,128)S(1)} %get-tuple-element.26.tiles, f32[512,128]{1,0:T(8,128)S(1)} %bitcast.25), custom_call_target="tpu_custom_call" | custom-call | tf_op jit(solution)/shard_map/pallas_call | solution.py:74
  101.3 8.0 %all-to-all-start.3 = ((f32[128,2,128]{2,1,0:T(2,128)}), f32[128,2,128]{2,1,0:T(2,128)S(1)}, u32[]{:S(2)}, u32[]{:S(2)}) async-start(f32[128,2,128]{2,1,0:T(2,128)} %bitcast.17), calls=%async_computation.3 | async-start | bytes 262144 | tf_op jit(solution)/shard_map/all_to_all | solution.py:414
  109.7 10.6 %all-to-all-done.3 = f32[128,2,128]{2,1,0:T(2,128)S(1)} async-done(((f32[128,2,128]{2,1,0:T(2,128)}), f32[128,2,128]{2,1,0:T(2,128)S(1)}, u32[]{:S(2)}, u32[]{:S(2)}) %all-to-all-start.3) | async-done | bytes 131104 | tf_op jit(solution)/shard_map/all_to_all | solution.py:414
  120.3 1.8 %shard_map.158 = f32[256,128]{1,0:T(8,128)} custom-call(f32[256,128]{1,0:T(8,128)S(1)} %bitcast.23, f32[256,128]{1,0:T(8,128)S(1)} %get-tuple-element.27.pair_one, f32[256,128]{1,0:T(8,128)S(1)} %shard_map.157.gate, f32[128,128]{1,0:T(8,128)S(1)} %copy-done.6, f32[128,512]{1,0:T(8,128)S(1)} %copy-done.3, f32[512,128]{1,0:T(8,128)S(1)} %copy-done.4), custom_call_target="tpu_custom_call" | custom-call | tf_op jit(solution)/shard_map/pallas_call | solution.py:74
  (39 shorter events, 1.2 us)
Async XLA Ops:
  2.3 5.3 %collective-permute-start.4 = (f32[72,128]{1,0:T(8,128)S(1)}, f32[72,128]{1,0:T(8,128)S(1)}, u32[]{:S(2)}, u32[]{:S(2)}) collective-permute-start(f32[72,128]{1,0:T(8,128)S(1)} %get-tuple-element.20), channel_id=1, source_target_pairs={{0,8},{8,0},{16,24},{24,16},{32,40},{40,32},{48,56},{56,48},{64,72... | collective-permute-start | bytes 110600 | tf_op jit(solution)/shard_map/ppermute | solution.py:361
  4.3 5.9 %collective-permute-start.5 = (f32[72,128]{1,0:T(8,128)S(1)}, f32[72,128]{1,0:T(8,128)S(1)}, u32[]{:S(2)}, u32[]{:S(2)}) collective-permute-start(f32[72,128]{1,0:T(8,128)S(1)} %get-tuple-element.20), channel_id=1, source_target_pairs={{0,16},{8,24},{16,0},{24,8},{32,48},{40,56},{48,32},{56,40},{64,80... | collective-permute-start | bytes 110600 | tf_op jit(solution)/shard_map/ppermute | solution.py:361
  7.6 5.8 %collective-permute-start.6 = (f32[72,128]{1,0:T(8,128)S(1)}, f32[72,128]{1,0:T(8,128)S(1)}, u32[]{:S(2)}, u32[]{:S(2)}) collective-permute-start(f32[72,128]{1,0:T(8,128)S(1)} %get-tuple-element.20), channel_id=1, source_target_pairs={{0,24},{8,16},{16,8},{24,0},{32,56},{40,48},{48,40},{56,32},{64,88... | collective-permute-start | bytes 110600 | tf_op jit(solution)/shard_map/ppermute | solution.py:361
  13.4 3.6 %copy-start.7 = (f32[128,8]{0,1:T(8,128)S(1)}, f32[128,8]{0,1:T(8,128)}, u32[]{:S(2)}) copy-start(f32[128,8]{0,1:T(8,128)} %param.19) | copy-start | bytes 12292
  13.4 8.5 %collective-permute-start.7 = (f32[4,72,128]{2,1,0:T(8,128)S(1)}, f32[4,72,128]{2,1,0:T(8,128)S(1)}, u32[]{:S(2)}, u32[]{:S(2)}) collective-permute-start(f32[4,72,128]{2,1,0:T(8,128)S(1)} %pad_maximum_fusion.refs_4_), channel_id=1, source_target_pairs={{0,32},{8,40},{16,48},{24,56},{32,0},{40,8},{48,16},{56,24},{64,96... | collective-permute-start | bytes 442376 | tf_op jit(solution)/shard_map/ppermute | solution.py:361
  14.0 8.4 %collective-permute-start.8 = (f32[4,72,128]{2,1,0:T(8,128)S(1)}, f32[4,72,128]{2,1,0:T(8,128)S(1)}, u32[]{:S(2)}, u32[]{:S(2)}) collective-permute-start(f32[4,72,128]{2,1,0:T(8,128)S(1)} %pad_maximum_fusion.refs_4_), channel_id=1, source_target_pairs={{0,64},{8,72},{16,80},{24,88},{32,96},{40,104},{48,112},{56,120},{... | collective-permute-start | bytes 442376 | tf_op jit(solution)/shard_map/ppermute | solution.py:361
  16.4 6.6 %collective-permute-start.9 = (f32[4,72,128]{2,1,0:T(8,128)S(1)}, f32[4,72,128]{2,1,0:T(8,128)S(1)}, u32[]{:S(2)}, u32[]{:S(2)}) collective-permute-start(f32[4,72,128]{2,1,0:T(8,128)S(1)} %pad_maximum_fusion.refs_4_), channel_id=1, source_target_pairs={{0,96},{8,104},{16,112},{24,120},{32,64},{40,72},{48,80},{56,88},{... | collective-permute-start | bytes 442376 | tf_op jit(solution)/shard_map/ppermute | solution.py:361
  17.3 7.6 %collective-permute-start = (f32[8,256]{1,0:T(8,128)S(1)}, f32[8,256]{1,0:T(8,128)S(1)}, u32[]{:S(2)}, u32[]{:S(2)}) collective-permute-start(f32[8,256]{1,0:T(8,128)S(1)} %shard_map.151), channel_id=1, source_target_pairs={{0,4},{1,5},{2,6},{3,7},{4,0},{5,1},{6,2},{7,3},{8,12},{9,13},{10,... | collective-permute-start | bytes 24584 | tf_op jit(solution)/shard_map/ppermute | solution.py:361
  21.9 17.0 %collective-permute-start.10 = (f32[4,72,128]{2,1,0:T(8,128)S(1)}, f32[4,72,128]{2,1,0:T(8,128)S(1)}, u32[]{:S(2)}, u32[]{:S(2)}) collective-permute-start(f32[4,72,128]{2,1,0:T(8,128)S(1)} %pad_maximum_fusion.refs_4_), channel_id=1, source_target_pairs={{0,128},{128,0},{1,129},{129,1},{2,130},{130,2},{3,131},{131,3},{4... | collective-permute-start | bytes 442376 | tf_op jit(solution)/shard_map/ppermute | solution.py:361
  21.9 17.0 %collective-permute-start.11 = (f32[4,72,128]{2,1,0:T(8,128)S(1)}, f32[4,72,128]{2,1,0:T(8,128)S(1)}, u32[]{:S(2)}, u32[]{:S(2)}) collective-permute-start(f32[4,72,128]{2,1,0:T(8,128)S(1)} %collective-permute-done.7.refs_5_), channel_id=1, source_target_pairs={{0,128},{128,0},{1,129},{129,1},{2,130},{130,2},{3,131},{131,3},{4... | collective-permute-start | bytes 442376 | tf_op jit(solution)/shard_map/ppermute | solution.py:361
  22.4 16.5 %collective-permute-start.12 = (f32[4,72,128]{2,1,0:T(8,128)S(1)}, f32[4,72,128]{2,1,0:T(8,128)S(1)}, u32[]{:S(2)}, u32[]{:S(2)}) collective-permute-start(f32[4,72,128]{2,1,0:T(8,128)S(1)} %collective-permute-done.8.refs_6_), channel_id=1, source_target_pairs={{0,128},{128,0},{1,129},{129,1},{2,130},{130,2},{3,131},{131,3},{4... | collective-permute-start | bytes 442376 | tf_op jit(solution)/shard_map/ppermute | solution.py:361
  23.0 15.8 %collective-permute-start.13 = (f32[4,72,128]{2,1,0:T(8,128)S(1)}, f32[4,72,128]{2,1,0:T(8,128)S(1)}, u32[]{:S(2)}, u32[]{:S(2)}) collective-permute-start(f32[4,72,128]{2,1,0:T(8,128)S(1)} %collective-permute-done.9.refs_7_), channel_id=1, source_target_pairs={{0,128},{128,0},{1,129},{129,1},{2,130},{130,2},{3,131},{131,3},{4... | collective-permute-start | bytes 442376 | tf_op jit(solution)/shard_map/ppermute | solution.py:361
  24.9 3.7 %collective-permute-start.1 = (f32[2,8,256]{2,1,0:T(8,128)S(1)}, f32[2,8,256]{2,1,0:T(8,128)S(1)}, u32[]{:S(2)}, u32[]{:S(2)}) collective-permute-start(f32[2,8,256]{2,1,0:T(8,128)S(1)} %pad_maximum_fusion.1.refs_0_), channel_id=1, source_target_pairs={{0,1},{1,0},{2,3},{3,2},{4,5},{5,4},{6,7},{7,6},{8,9},{9,8},{10,11... | collective-permute-start | bytes 49160 | tf_op jit(solution)/shard_map/ppermute | solution.py:361
  28.7 5.2 %collective-permute-start.2 = (f32[2,8,256]{2,1,0:T(8,128)S(1)}, f32[2,8,256]{2,1,0:T(8,128)S(1)}, u32[]{:S(2)}, u32[]{:S(2)}) collective-permute-start(f32[2,8,256]{2,1,0:T(8,128)S(1)} %pad_maximum_fusion.1.refs_0_), channel_id=1, source_target_pairs={{0,2},{1,3},{2,0},{3,1},{4,6},{5,7},{6,4},{7,5},{8,10},{9,11},{10,... | collective-permute-start | bytes 49160 | tf_op jit(solution)/shard_map/ppermute | solution.py:361
  33.9 4.9 %collective-permute-start.3 = (f32[2,8,256]{2,1,0:T(8,128)S(1)}, f32[2,8,256]{2,1,0:T(8,128)S(1)}, u32[]{:S(2)}, u32[]{:S(2)}) collective-permute-start(f32[2,8,256]{2,1,0:T(8,128)S(1)} %pad_maximum_fusion.1.refs_0_), channel_id=1, source_target_pairs={{0,3},{1,2},{2,1},{3,0},{4,7},{5,6},{6,5},{7,4},{8,11},{9,10},{10,... | collective-permute-start | bytes 49160 | tf_op jit(solution)/shard_map/ppermute | solution.py:361
  41.7 35.1 %copy-start = (f32[1024,128]{1,0:T(8,128)S(1)}, f32[1024,128]{1,0:T(8,128)}, u32[]{:S(2)}) copy-start(f32[1024,128]{1,0:T(8,128)} %outer_w.1) | copy-start | bytes 1572868
  56.3 20.6 %copy-start.1 = (f32[8,32,128]{2,1,0:T(8,128)S(1)}, f32[8,32,128]{2,1,0:T(8,128)}, u32[]{:S(2)}) copy-start(f32[8,32,128]{2,1,0:T(8,128)} %param.14) | copy-start | bytes 393220
  56.3 20.6 %copy-start.2 = (f32[128,512]{1,0:T(8,128)S(1)}, f32[128,512]{1,0:T(8,128)}, u32[]{:S(2)}) copy-start(f32[128,512]{1,0:T(8,128)} %tri_w.1) | copy-start | bytes 786436
  56.3 20.6 %all-to-all-start.1 = ((f32[8,48,128]{2,1,0:T(8,128)}), f32[8,48,128]{2,1,0:T(8,128)S(1)}, u32[]{:S(2)}, u32[]{:S(2)}) async-start(f32[8,48,128]{2,1,0:T(8,128)} %shard_map.153), calls=%async_computation.1 | async-start | bytes 393216 | tf_op jit(solution)/shard_map/all_to_all | solution.py:395
  66.0 0.7 copy-start.8
  98.3 1.5 %collective-permute-start.14 = (f32[128,4,128]{2,1,0:T(4,128)S(1)}, f32[128,4,128]{2,1,0:T(4,128)S(1)}, u32[]{:S(2)}, u32[]{:S(2)}) collective-permute-start(f32[128,4,128]{2,1,0:T(4,128)S(1)} %all_to_all.21), channel_id=1, source_target_pairs={{0,128},{128,0},{1,129},{129,1},{2,130},{130,2},{3,131},{131,3},{4... | collective-permute-start | bytes 786440 | tf_op jit(solution)/shard_map/ppermute | solution.py:407
  99.8 9.5 %copy-start.5 = (f32[128,128]{1,0:T(8,128)S(1)}, f32[128,128]{1,0:T(8,128)}, u32[]{:S(2)}) copy-start(f32[128,128]{1,0:T(8,128)} %gate_w.1) | copy-start | bytes 196612
  101.3 19.0 %copy-start.3 = (f32[128,512]{1,0:T(8,128)S(1)}, f32[128,512]{1,0:T(8,128)}, u32[]{:S(2)}) copy-start(f32[128,512]{1,0:T(8,128)} %in_w.1) | copy-start | bytes 786436
  101.3 19.0 %copy-start.4 = (f32[512,128]{1,0:T(8,128)S(1)}, f32[512,128]{1,0:T(8,128)}, u32[]{:S(2)}) copy-start(f32[512,128]{1,0:T(8,128)} %last_w.1) | copy-start | bytes 786436
  101.3 19.0 %all-to-all-start.3 = ((f32[128,2,128]{2,1,0:T(2,128)}), f32[128,2,128]{2,1,0:T(2,128)S(1)}, u32[]{:S(2)}, u32[]{:S(2)}) async-start(f32[128,2,128]{2,1,0:T(2,128)} %bitcast.17), calls=%async_computation.3 | async-start | bytes 262144 | tf_op jit(solution)/shard_map/all_to_all | solution.py:414
  109.4 10.9 %copy-start.6 = (f32[128,128]{1,0:T(8,128)S(1)}, f32[128,128]{1,0:T(8,128)}, u32[]{:S(2)}) copy-start(f32[128,128]{1,0:T(8,128)} %out_w.3) | copy-start | bytes 196612

commit v5 on v4

--- a/solution.py
+++ b/solution.py
@@ -82,7 +82,7 @@
     return run
 
 
-def send_kernel(low, pair, align, mask, x_send, pair_near, align_near, mask_near, sem):
+def send_kernel(low, pair, align, mask, residues, x_send, pair_near, align_near, mask_near, residues_near, sem):
     copy = pltpu.make_async_copy(pair, pair_near, sem)
     copy.start()
     align_near[...] = align[...]
@@ -91,6 +91,7 @@
     spread = ((lane % 8 == iota((8, 128), 0)) & (lane // 8 == low[0])).astype(f32)
     mask_rows = jnp.concatenate([mask[...].astype(f32), jnp.zeros((4, 8), f32)], axis=0)
     mask_near[...] = mask_rows
+    residues_near[...] = residues[...].astype(f32)
     x_send[0:32] = normed[:, 0:128]
     x_send[32:64] = normed[:, 128:256]
     x_send[64:72] = lax.dot_general(mask_rows, spread, NN, preferred_element_type=f32)
@@ -210,7 +211,7 @@
         merged[c, 32:48] = left_mask[c]
 
 
-def outer_kernel(factors, pair, valid, outer_w, tri_w, pair_one, edge_send, right_s, left_s, sum_s):
+def outer_kernel(row_of, col_of, factors, pair, residues, outer_w, tri_w, gate_w, pair_one, edge_send, gate_out, right_s, left_s, sum_s):
     lane = iota((8, 128), 1)
     chunk = iota((32, 128), 1) // 32
     for group in range(4):
@@ -249,13 +250,26 @@
     count = jnp.concatenate([counts[0:32, 32 + i : 33 + i] for i in range(8)], axis=0)
     one = pair[...] + outer / (1.0 + count)
     pair_one[...] = one
-    edges = dot3(tri_w[...].T, layer_norm(one), NT)
-    left_edge = jax.nn.sigmoid(edges[0:128]) * edges[128:256] * valid[...]
-    right_edge = jax.nn.sigmoid(edges[256:384]) * edges[384:512] * valid[...]
+    normed = layer_norm(one)
+    edges = dot3(tri_w[...].T, normed, NT)
+    present = residues[...]
+    source, tile = iota((128, 256), 0), iota((128, 256), 1)
+    valid = jnp.ones((8, 256), f32)
+    for target in (row_of[0] * 8 + tile // 32, col_of[0] * 32 + tile % 32):
+        picked = jnp.zeros((8, 256), f32)
+        for half in range(2):
+            chosen = (source + half * 128 == target).astype(f32)
+            wide = jnp.broadcast_to(present[half : half + 1], (8, 128))
+            picked = picked + lax.dot_general(wide, chosen, NN, preferred_element_type=f32)
+        valid = valid * picked
+    valid = valid[0:1]
+    left_edge = jax.nn.sigmoid(edges[0:128]) * edges[128:256] * valid
+    right_edge = jax.nn.sigmoid(edges[256:384]) * edges[384:512] * valid
     edge_send[:, 0, :] = left_edge[:, 0:128]
     edge_send[:, 1, :] = left_edge[:, 128:256]
     edge_send[:, 2, :] = right_edge[:, 0:128]
     edge_send[:, 3, :] = right_edge[:, 128:256]
+    gate_out[...] = jax.nn.sigmoid(dot3(normed, gate_w[...]))
 
 
 def cross_half(left_parts, edges, right_s, store):
@@ -309,10 +323,6 @@
         for h in range(2):
             store_own(c, h, tiles[(c * 2 + h) * 16 : (c * 2 + h) * 16 + 16, :])
     cross_half(split(left[...]), other, right_s, store_at(1 - branch_of[0]))
-
-
-def gate_kernel(pair_one, gate_w, gate_out):
-    gate_out[...] = jax.nn.sigmoid(dot3(layer_norm(pair_one[...]), gate_w[...]))
 
 
 def final_kernel(crossed, pair_one, gate, out_w, in_w, last_w, new_pair, triangle_s):
@@ -347,14 +357,14 @@
     align = alignment.reshape(32, 256)
     low = lax.axis_index("prow").astype(jnp.int32).reshape(1)
     place = (branch, col.reshape(1), low)
-    x_send, pair_near, align_near, mask_near = call(
+    x_send, pair_near, align_near, mask_near, residues_near = call(
         send_kernel,
-        [(72, 128), (256, 128), (32, 256), (8, 8)],
+        [(72, 128), (256, 128), (32, 256), (8, 8), (2, 128)],
         scratch=[pltpu.SemaphoreType.DMA],
         scalars=1,
         far=1,
-        loose=2,
-    )(low, pair, align, row_mask)
+        loose=3,
+    )(low, pair, align, row_mask, residue_mask.reshape(2, 128))
     (bias_send,) = call(bias_kernel, [(8, 256)])(pair_near, pair_bias_w.T)
 
     def swap(value, axis, size, step):
@@ -391,19 +401,15 @@
         kept=(0,),
     )(*place, attention_in, attention_out, outer_in.T, query, gate, align_near, mask_near, *bias_own, *x_own, *x_other)
     right_all = lax.all_to_all(right_send, ROWS, 0, 0, tiled=True)
-    (factor_send,) = call(merge_kernel, [(8, 48, 128)], kept=(0,))(right_all.reshape(256, 128), left_mask)
+    (factor_send,) = call(merge_kernel, [(8, 48, 128)])(right_all.reshape(256, 128), left_mask)
     factors = lax.all_to_all(factor_send, "pcol", 0, 0, tiled=True)
-    res_float = residue_mask.astype(f32)
-    row_valid = lax.dynamic_slice_in_dim(res_float, row * 8, 8)
-    col_valid = lax.dynamic_slice_in_dim(res_float, col * 32, 32)
-    valid = (row_valid[:, None] * col_valid[None, :]).reshape(1, 256)
-    pair_one, edge_send = call(
+    pair_one, edge_send, tri_gate = call(
         outer_kernel,
-        [(256, 128), (128, 4, 128)],
+        [(256, 128), (128, 4, 128), (256, 128)],
         scratch=[pltpu.VMEM((128, 256), f32), pltpu.VMEM((32, 8, 256), f32), pltpu.VMEM((256, 1024), f32)],
-    )(factors, pair, valid, outer_out, triangle_in)
+        scalars=2,
+    )(row.reshape(1), col.reshape(1), factors, pair, residues_near, outer_out, triangle_in, triangle_gate)
     own_edges = lax.all_to_all(edge_send, CHIPS, 0, 0, tiled=True)
-    (tri_gate,) = call(gate_kernel, [(256, 128)])(pair_one, triangle_gate)
     other_edges = lax.ppermute(own_edges, "branch", [(0, 1), (1, 0)])
     left_wide, tiles = call(
         cross_kernel, [(128, 1024), (128, 128)], scratch=[pltpu.VMEM((8, 128, 128), f32)]

time: 123 us -> 123 us (level)
  blocking collectives: 33 us -> 51.9 us
  waiting for transfers between devices: 33.6 us -> 24.1 us
  starting transfers between devices: 39.5 us -> 31.5 us
    all_to_all x0 -> x1, blocking collectives: none -> 18.9 us  [shards(): lax.all_to_all(cross_send.reshape(128, 2, 128), CHIPS, 0, 0, tiled=True)]
    all_to_all x1 -> x0, waiting for transfers between devices: 10.6 us -> none  [shards(): lax.all_to_all(cross_send.reshape(128, 2, 128), CHIPS, 0, 0, tiled=True)]
    all_to_all x1 -> x0, starting transfers between devices: 8.03 us -> none  [shards(): lax.all_to_all(cross_send.reshape(128, 2, 128), CHIPS, 0, 0, tiled=True)]
    pallas_call x10 -> x9, Pallas kernels: 14.1 us -> 13.2 us  [run(): pl.pallas_call(kernel, out_shape=outs, in_specs=[smem] * scalars + [pl.Bl...]
  transfers between devices with their start and end apart: 17 -> 16, of which waited for: 9 -> 8; matrix products, arithmetic and copies ran while one was open for 0% -> 0% of each run, Pallas kernels for 3% -> 2%
where the time goes in v5:
time: 123 us; the launch traced here: 121 us
  blocking collectives  51.9 us (42%)
  starting transfers between devices  31.5 us (26%)
  waiting for transfers between devices  24.1 us (20%)
  Pallas kernels  13.2 us (11%)
    ppermute x14, starting transfers between devices, swap(): return lax.ppermute(value, axis, [(d, d ^ step) for d in range(size)])  21.8 us
    all_to_all x1, blocking collectives, shards(): own_edges = lax.all_to_all(edge_send, CHIPS, 0, 0, tiled=True)  19.1 us
    all_to_all x1, blocking collectives, shards(): lax.all_to_all(cross_send.reshape(128, 2, 128), CHIPS, 0, 0, tiled=True)  18.9 us
    all_to_all x1, blocking collectives, shards(): right_all = lax.all_to_all(right_send, ROWS, 0, 0, tiled=True)  13.8 us
    pallas_call x9, Pallas kernels, run(): pl.pallas_call(kernel, out_shape=outs, in_specs=[smem] * scalars + [pl.Bl...  13.2 us
    ppermute x14, waiting for transfers between devices, swap(): return lax.ppermute(value, axis, [(d, d ^ step) for d in range(size)])  12.4 us
    all_to_all x1, waiting for transfers between devices, shards(): factors = lax.all_to_all(factor_send, 'pcol', 0, 0, tiled=True)  10.9 us
    all_to_all x1, starting transfers between devices, shards(): factors = lax.all_to_all(factor_send, 'pcol', 0, 0, tiled=True)  9.67 us
  transfers between devices with their start and end apart: 16, of which 8 were waited for; matrix products, arithmetic and copies ran while one was open for 0% of the time, Pallas kernels for 2%

profile of v5, /device:TPU:2, one launch (start us, length us, event | category | flops | bytes accessed | tf_op | source)
XLA Modules:
  0.0 121.4 jit_solution(10036549629931124545)
XLA Ops:
  0.6 1.7 %shard_map.149 = (f32[72,128]{1,0:T(8,128)S(1)}, f32[256,128]{1,0:T(8,128)S(1)}, f32[32,256]{1,0:T(8,128)S(1)}, f32[8,8]{1,0:T(8,128)S(1)}, f32[2,128]{1,0:T(2,128)S(1)}) custom-call(s32[1]{0:T(128)} %bitcast.2.low.low_of, f32[256,128]{1,0:T(8,128)} %bitcast.23, f32[32,256]{1,0:T(8,128)} %bitcast.37, s32[4,8]{1,0:T(4,128)} %mask.1, s32[2,128]{1,0:T(2,128)} %bitcast.39), custom_call_target="tpu_custom_call" | custom-call | tf_op jit(solution)/shard_map/pallas_call | solution.py:74
  2.3 2.0 %collective-permute-start.4 = (f32[72,128]{1,0:T(8,128)S(1)}, f32[72,128]{1,0:T(8,128)S(1)}, u32[]{:S(2)}, u32[]{:S(2)}) collective-permute-start(f32[72,128]{1,0:T(8,128)S(1)} %get-tuple-element.22), channel_id=1, source_target_pairs={{0,8},{8,0},{16,24},{24,16},{32,40},{40,32},{48,56},{56,48},{64,72... | collective-permute-start | bytes 110600 | tf_op jit(solution)/shard_map/ppermute | solution.py:371
  4.3 3.3 %collective-permute-start.5 = (f32[72,128]{1,0:T(8,128)S(1)}, f32[72,128]{1,0:T(8,128)S(1)}, u32[]{:S(2)}, u32[]{:S(2)}) collective-permute-start(f32[72,128]{1,0:T(8,128)S(1)} %get-tuple-element.22), channel_id=1, source_target_pairs={{0,16},{8,24},{16,0},{24,8},{32,48},{40,56},{48,32},{56,40},{64,80... | collective-permute-start | bytes 110600 | tf_op jit(solution)/shard_map/ppermute | solution.py:371
  7.6 2.6 %collective-permute-done.5 = f32[72,128]{1,0:T(8,128)S(1)} collective-permute-done((f32[72,128]{1,0:T(8,128)S(1)}, f32[72,128]{1,0:T(8,128)S(1)}, u32[]{:S(2)}, u32[]{:S(2)}) %collective-permute-start.5) | collective-permute-done | bytes 36896 | tf_op jit(solution)/shard_map/ppermute | solution.py:371
  10.3 3.1 %collective-permute-done.6 = f32[72,128]{1,0:T(8,128)S(1)} collective-permute-done((f32[72,128]{1,0:T(8,128)S(1)}, f32[72,128]{1,0:T(8,128)S(1)}, u32[]{:S(2)}, u32[]{:S(2)}) %collective-permute-start.6) | collective-permute-done | bytes 36896 | tf_op jit(solution)/shard_map/ppermute | solution.py:371
  13.4 0.6 collective-permute-start.7
  14.0 2.4 %collective-permute-start.8 = (f32[4,72,128]{2,1,0:T(8,128)S(1)}, f32[4,72,128]{2,1,0:T(8,128)S(1)}, u32[]{:S(2)}, u32[]{:S(2)}) collective-permute-start(f32[4,72,128]{2,1,0:T(8,128)S(1)} %pad_maximum_fusion.refs_4_), channel_id=1, source_target_pairs={{0,64},{8,72},{16,80},{24,88},{32,96},{40,104},{48,112},{56,120},{... | collective-permute-start | bytes 442376 | tf_op jit(solution)/shard_map/ppermute | solution.py:371
  16.4 0.5 collective-permute-start.9
  17.0 0.3 shard_map.151
  17.3 4.6 %collective-permute-start = (f32[8,256]{1,0:T(8,128)S(1)}, f32[8,256]{1,0:T(8,128)S(1)}, u32[]{:S(2)}, u32[]{:S(2)}) collective-permute-start(f32[8,256]{1,0:T(8,128)S(1)} %shard_map.151), channel_id=1, source_target_pairs={{0,4},{1,5},{2,6},{3,7},{4,0},{5,1},{6,2},{7,3},{8,12},{9,13},{10,... | collective-permute-start | bytes 24584 | tf_op jit(solution)/shard_map/ppermute | solution.py:371
  21.9 0.5 collective-permute-start.11
  22.4 0.1 collective-permute-start.12
  22.5 0.6 collective-permute-done.9.refs_7_
  23.1 1.9 %collective-permute-done = f32[8,256]{1,0:T(8,128)S(1)} collective-permute-done((f32[8,256]{1,0:T(8,128)S(1)}, f32[8,256]{1,0:T(8,128)S(1)}, u32[]{:S(2)}, u32[]{:S(2)}) %collective-permute-start) | collective-permute-done | bytes 8224 | tf_op jit(solution)/shard_map/ppermute | solution.py:371
  24.9 1.6 %collective-permute-start.1 = (f32[2,8,256]{2,1,0:T(8,128)S(1)}, f32[2,8,256]{2,1,0:T(8,128)S(1)}, u32[]{:S(2)}, u32[]{:S(2)}) collective-permute-start(f32[2,8,256]{2,1,0:T(8,128)S(1)} %pad_maximum_fusion.1.refs_0_), channel_id=1, source_target_pairs={{0,1},{1,0},{2,3},{3,2},{4,5},{5,4},{6,7},{7,6},{8,9},{9,8},{10,11... | collective-permute-start | bytes 49160 | tf_op jit(solution)/shard_map/ppermute | solution.py:371
  26.5 2.2 %collective-permute-done.1.refs_1_ = f32[2,8,256]{2,1,0:T(8,128)S(1)} collective-permute-done((f32[2,8,256]{2,1,0:T(8,128)S(1)}, f32[2,8,256]{2,1,0:T(8,128)S(1)}, u32[]{:S(2)}, u32[]{:S(2)}) %collective-permute-start.1) | collective-permute-done | bytes 16416 | tf_op jit(solution)/shard_map/ppermute | solution.py:371
  28.7 3.2 %collective-permute-start.2 = (f32[2,8,256]{2,1,0:T(8,128)S(1)}, f32[2,8,256]{2,1,0:T(8,128)S(1)}, u32[]{:S(2)}, u32[]{:S(2)}) collective-permute-start(f32[2,8,256]{2,1,0:T(8,128)S(1)} %pad_maximum_fusion.1.refs_0_), channel_id=1, source_target_pairs={{0,2},{1,3},{2,0},{3,1},{4,6},{5,7},{6,4},{7,5},{8,10},{9,11},{10,... | collective-permute-start | bytes 49160 | tf_op jit(solution)/shard_map/ppermute | solution.py:371
  31.9 2.0 %collective-permute-done.2.refs_2_ = f32[2,8,256]{2,1,0:T(8,128)S(1)} collective-permute-done((f32[2,8,256]{2,1,0:T(8,128)S(1)}, f32[2,8,256]{2,1,0:T(8,128)S(1)}, u32[]{:S(2)}, u32[]{:S(2)}) %collective-permute-start.2) | collective-permute-done | bytes 16416 | tf_op jit(solution)/shard_map/ppermute | solution.py:371
  33.9 3.0 %collective-permute-start.3 = (f32[2,8,256]{2,1,0:T(8,128)S(1)}, f32[2,8,256]{2,1,0:T(8,128)S(1)}, u32[]{:S(2)}, u32[]{:S(2)}) collective-permute-start(f32[2,8,256]{2,1,0:T(8,128)S(1)} %pad_maximum_fusion.1.refs_0_), channel_id=1, source_target_pairs={{0,3},{1,2},{2,1},{3,0},{4,7},{5,6},{6,5},{7,4},{8,11},{9,10},{10,... | collective-permute-start | bytes 49160 | tf_op jit(solution)/shard_map/ppermute | solution.py:371
  36.9 1.9 %shard_map.150 = (f32[256,256]{1,0:T(8,128)S(1)}, f32[32,256]{1,0:T(8,128)S(1)}) custom-call(f32[256,1024]{1,0:T(8,128)} %proj.3, f32[32,256]{1,0:T(8,128)S(1)} %get-tuple-element.17.align), custom_call_target="tpu_custom_call" | custom-call | tf_op jit(solution)/shard_map/pallas_call | solution.py:74
  38.9 2.8 %shard_map.152 = (f32[32,256]{1,0:T(8,128)}, f32[32,8,128]{2,1,0:T(8,128)S(1)}, f32[8,16,128]{2,1,0:T(8,128)S(1)}) custom-call(s32[1]{0:T(128)} %bitcast.branch_of, s32[1]{0:T(128)} %bitcast.1.col_of, s32[1]{0:T(128)} %bitcast.2.low.low_of, f32[256,1024]{1,0:T(8,128)} %proj.3, f32[256,256]{1,0:T(8,128)} %out_w.2, f32[64,256]{1,0:T(8,128)} %bitcast.33, ...), custom_call_target="tpu_custom_call" | custom-call | tf_op jit(solution)/shard_map/pallas_call | solution.py:74
  41.8 13.8 %all_to_all.20 = f32[32,8,128]{2,1,0:T(8,128)S(1)} all-to-all(f32[32,8,128]{2,1,0:T(8,128)S(1)} %get-tuple-element.24), channel_id=1, replica_groups=mesh['branch'=2,'prow'=16,'pcol'=8] {'branch','prow'}, dimensions={0} | all-to-all | bytes 262144 | tf_op jit(solution)/shard_map/all_to_all | solution.py:403
  55.6 0.7 shard_map.153
  56.3 9.7 %all-to-all-start.1 = ((f32[8,48,128]{2,1,0:T(8,128)}), f32[8,48,128]{2,1,0:T(8,128)S(1)}, u32[]{:S(2)}, u32[]{:S(2)}) async-start(f32[8,48,128]{2,1,0:T(8,128)} %shard_map.153), calls=%async_computation.1 | async-start | bytes 393216 | tf_op jit(solution)/shard_map/all_to_all | solution.py:405
  66.0 10.9 %all-to-all-done.1.factors = f32[8,48,128]{2,1,0:T(8,128)S(1)} async-done(((f32[8,48,128]{2,1,0:T(8,128)}), f32[8,48,128]{2,1,0:T(8,128)S(1)}, u32[]{:S(2)}, u32[]{:S(2)}) %all-to-all-start.1) | async-done | bytes 196640 | tf_op jit(solution)/shard_map/all_to_all | solution.py:405
  76.9 2.3 %shard_map.154 = (f32[256,128]{1,0:T(8,128)S(1)}, f32[128,4,128]{2,1,0:T(4,128)S(1)}, f32[256,128]{1,0:T(8,128)S(1)}) custom-call(s32[1]{0:T(128)} %bitcast.15.row_of, s32[1]{0:T(128)} %bitcast.1.col_of, f32[8,48,128]{2,1,0:T(8,128)S(1)} %all-to-all-done.1.factors, f32[256,128]{1,0:T(8,128)S(1)} %bitcast.24, f32[2,128]{1,0:T(2,128)S(1)} %get-tuple-element.26.residues, ...), custom_call_target="tpu_custom_call" | custom-call | tf_op jit(solution)/shard_map/pallas_call | solution.py:74
  79.3 19.1 %all_to_all.21 = f32[128,4,128]{2,1,0:T(4,128)S(1)} all-to-all(f32[128,4,128]{2,1,0:T(4,128)S(1)} %get-tuple-element.27), channel_id=1, replica_groups=mesh['branch'=2,'prow'=16,'pcol'=8] {'prow','pcol'}, dimensions={0} | all-to-all | bytes 524288 | tf_op jit(solution)/shard_map/all_to_all | solution.py:412
  98.4 0.8 shard_map.155
  99.2 0.7 collective-permute-done.14
  99.9 0.8 shard_map.156
  100.7 18.9 %all_to_all.22 = f32[128,2,128]{2,1,0:T(2,128)S(1)} all-to-all(f32[128,2,128]{2,1,0:T(2,128)S(1)} %bitcast.25), channel_id=1, replica_groups=mesh['branch'=2,'prow'=16,'pcol'=8] {'prow','pcol'}, dimensions={0} | all-to-all | bytes 262144 | tf_op jit(solution)/shard_map/all_to_all | solution.py:420
  119.6 1.8 %shard_map.157 = f32[256,128]{1,0:T(8,128)} custom-call(f32[256,128]{1,0:T(8,128)S(1)} %bitcast.26, f32[256,128]{1,0:T(8,128)S(1)} %get-tuple-element.30.pair_one, f32[256,128]{1,0:T(8,128)S(1)} %get-tuple-element.31.gate, f32[128,128]{1,0:T(8,128)S(1)} %copy-done.6, f32[128,512]{1,0:T(8,128)S(1)} %copy-done.2, f32[512,128]{1,0:T(8,128)S(1)} %copy-done.3), custom_call_target="tpu_custom_call" | custom-call | tf_op jit(solution)/shard_map/pallas_call | solution.py:74
  (30 shorter events, 0.1 us)
Async XLA Ops:
  2.3 5.3 %collective-permute-start.4 = (f32[72,128]{1,0:T(8,128)S(1)}, f32[72,128]{1,0:T(8,128)S(1)}, u32[]{:S(2)}, u32[]{:S(2)}) collective-permute-start(f32[72,128]{1,0:T(8,128)S(1)} %get-tuple-element.22), channel_id=1, source_target_pairs={{0,8},{8,0},{16,24},{24,16},{32,40},{40,32},{48,56},{56,48},{64,72... | collective-permute-start | bytes 110600 | tf_op jit(solution)/shard_map/ppermute | solution.py:371
  4.3 5.9 %collective-permute-start.5 = (f32[72,128]{1,0:T(8,128)S(1)}, f32[72,128]{1,0:T(8,128)S(1)}, u32[]{:S(2)}, u32[]{:S(2)}) collective-permute-start(f32[72,128]{1,0:T(8,128)S(1)} %get-tuple-element.22), channel_id=1, source_target_pairs={{0,16},{8,24},{16,0},{24,8},{32,48},{40,56},{48,32},{56,40},{64,80... | collective-permute-start | bytes 110600 | tf_op jit(solution)/shard_map/ppermute | solution.py:371
  7.6 5.8 %collective-permute-start.6 = (f32[72,128]{1,0:T(8,128)S(1)}, f32[72,128]{1,0:T(8,128)S(1)}, u32[]{:S(2)}, u32[]{:S(2)}) collective-permute-start(f32[72,128]{1,0:T(8,128)S(1)} %get-tuple-element.22), channel_id=1, source_target_pairs={{0,24},{8,16},{16,8},{24,0},{32,56},{40,48},{48,40},{56,32},{64,88... | collective-permute-start | bytes 110600 | tf_op jit(solution)/shard_map/ppermute | solution.py:371
  13.4 3.6 %copy-start.7 = (f32[128,8]{0,1:T(8,128)S(1)}, f32[128,8]{0,1:T(8,128)}, u32[]{:S(2)}) copy-start(f32[128,8]{0,1:T(8,128)} %param.19) | copy-start | bytes 12292
  13.4 8.5 %collective-permute-start.7 = (f32[4,72,128]{2,1,0:T(8,128)S(1)}, f32[4,72,128]{2,1,0:T(8,128)S(1)}, u32[]{:S(2)}, u32[]{:S(2)}) collective-permute-start(f32[4,72,128]{2,1,0:T(8,128)S(1)} %pad_maximum_fusion.refs_4_), channel_id=1, source_target_pairs={{0,32},{8,40},{16,48},{24,56},{32,0},{40,8},{48,16},{56,24},{64,96... | collective-permute-start | bytes 442376 | tf_op jit(solution)/shard_map/ppermute | solution.py:371
  14.0 8.4 %collective-permute-start.8 = (f32[4,72,128]{2,1,0:T(8,128)S(1)}, f32[4,72,128]{2,1,0:T(8,128)S(1)}, u32[]{:S(2)}, u32[]{:S(2)}) collective-permute-start(f32[4,72,128]{2,1,0:T(8,128)S(1)} %pad_maximum_fusion.refs_4_), channel_id=1, source_target_pairs={{0,64},{8,72},{16,80},{24,88},{32,96},{40,104},{48,112},{56,120},{... | collective-permute-start | bytes 442376 | tf_op jit(solution)/shard_map/ppermute | solution.py:371
  16.4 6.6 %collective-permute-start.9 = (f32[4,72,128]{2,1,0:T(8,128)S(1)}, f32[4,72,128]{2,1,0:T(8,128)S(1)}, u32[]{:S(2)}, u32[]{:S(2)}) collective-permute-start(f32[4,72,128]{2,1,0:T(8,128)S(1)} %pad_maximum_fusion.refs_4_), channel_id=1, source_target_pairs={{0,96},{8,104},{16,112},{24,120},{32,64},{40,72},{48,80},{56,88},{... | collective-permute-start | bytes 442376 | tf_op jit(solution)/shard_map/ppermute | solution.py:371
  17.3 7.6 %collective-permute-start = (f32[8,256]{1,0:T(8,128)S(1)}, f32[8,256]{1,0:T(8,128)S(1)}, u32[]{:S(2)}, u32[]{:S(2)}) collective-permute-start(f32[8,256]{1,0:T(8,128)S(1)} %shard_map.151), channel_id=1, source_target_pairs={{0,4},{1,5},{2,6},{3,7},{4,0},{5,1},{6,2},{7,3},{8,12},{9,13},{10,... | collective-permute-start | bytes 24584 | tf_op jit(solution)/shard_map/ppermute | solution.py:371
  21.9 17.0 %collective-permute-start.10 = (f32[4,72,128]{2,1,0:T(8,128)S(1)}, f32[4,72,128]{2,1,0:T(8,128)S(1)}, u32[]{:S(2)}, u32[]{:S(2)}) collective-permute-start(f32[4,72,128]{2,1,0:T(8,128)S(1)} %pad_maximum_fusion.refs_4_), channel_id=1, source_target_pairs={{0,128},{128,0},{1,129},{129,1},{2,130},{130,2},{3,131},{131,3},{4... | collective-permute-start | bytes 442376 | tf_op jit(solution)/shard_map/ppermute | solution.py:371
  21.9 17.0 %collective-permute-start.11 = (f32[4,72,128]{2,1,0:T(8,128)S(1)}, f32[4,72,128]{2,1,0:T(8,128)S(1)}, u32[]{:S(2)}, u32[]{:S(2)}) collective-permute-start(f32[4,72,128]{2,1,0:T(8,128)S(1)} %collective-permute-done.7.refs_5_), channel_id=1, source_target_pairs={{0,128},{128,0},{1,129},{129,1},{2,130},{130,2},{3,131},{131,3},{4... | collective-permute-start | bytes 442376 | tf_op jit(solution)/shard_map/ppermute | solution.py:371
  22.4 16.5 %collective-permute-start.12 = (f32[4,72,128]{2,1,0:T(8,128)S(1)}, f32[4,72,128]{2,1,0:T(8,128)S(1)}, u32[]{:S(2)}, u32[]{:S(2)}) collective-permute-start(f32[4,72,128]{2,1,0:T(8,128)S(1)} %collective-permute-done.8.refs_6_), channel_id=1, source_target_pairs={{0,128},{128,0},{1,129},{129,1},{2,130},{130,2},{3,131},{131,3},{4... | collective-permute-start | bytes 442376 | tf_op jit(solution)/shard_map/ppermute | solution.py:371
  23.1 15.8 %collective-permute-start.13 = (f32[4,72,128]{2,1,0:T(8,128)S(1)}, f32[4,72,128]{2,1,0:T(8,128)S(1)}, u32[]{:S(2)}, u32[]{:S(2)}) collective-permute-start(f32[4,72,128]{2,1,0:T(8,128)S(1)} %collective-permute-done.9.refs_7_), channel_id=1, source_target_pairs={{0,128},{128,0},{1,129},{129,1},{2,130},{130,2},{3,131},{131,3},{4... | collective-permute-start | bytes 442376 | tf_op jit(solution)/shard_map/ppermute | solution.py:371
  24.9 3.7 %collective-permute-start.1 = (f32[2,8,256]{2,1,0:T(8,128)S(1)}, f32[2,8,256]{2,1,0:T(8,128)S(1)}, u32[]{:S(2)}, u32[]{:S(2)}) collective-permute-start(f32[2,8,256]{2,1,0:T(8,128)S(1)} %pad_maximum_fusion.1.refs_0_), channel_id=1, source_target_pairs={{0,1},{1,0},{2,3},{3,2},{4,5},{5,4},{6,7},{7,6},{8,9},{9,8},{10,11... | collective-permute-start | bytes 49160 | tf_op jit(solution)/shard_map/ppermute | solution.py:371
  28.7 5.2 %collective-permute-start.2 = (f32[2,8,256]{2,1,0:T(8,128)S(1)}, f32[2,8,256]{2,1,0:T(8,128)S(1)}, u32[]{:S(2)}, u32[]{:S(2)}) collective-permute-start(f32[2,8,256]{2,1,0:T(8,128)S(1)} %pad_maximum_fusion.1.refs_0_), channel_id=1, source_target_pairs={{0,2},{1,3},{2,0},{3,1},{4,6},{5,7},{6,4},{7,5},{8,10},{9,11},{10,... | collective-permute-start | bytes 49160 | tf_op jit(solution)/shard_map/ppermute | solution.py:371
  33.9 4.9 %collective-permute-start.3 = (f32[2,8,256]{2,1,0:T(8,128)S(1)}, f32[2,8,256]{2,1,0:T(8,128)S(1)}, u32[]{:S(2)}, u32[]{:S(2)}) collective-permute-start(f32[2,8,256]{2,1,0:T(8,128)S(1)} %pad_maximum_fusion.1.refs_0_), channel_id=1, source_target_pairs={{0,3},{1,2},{2,1},{3,0},{4,7},{5,6},{6,5},{7,4},{8,11},{9,10},{10,... | collective-permute-start | bytes 49160 | tf_op jit(solution)/shard_map/ppermute | solution.py:371
  41.8 35.1 %copy-start.1 = (f32[1024,128]{1,0:T(8,128)S(1)}, f32[1024,128]{1,0:T(8,128)}, u32[]{:S(2)}) copy-start(f32[1024,128]{1,0:T(8,128)} %outer_w.1) | copy-start | bytes 1572868
  55.6 21.3 %copy-start.5 = (f32[128,128]{1,0:T(8,128)S(1)}, f32[128,128]{1,0:T(8,128)}, u32[]{:S(2)}) copy-start(f32[128,128]{1,0:T(8,128)} %gate_w.1) | copy-start | bytes 196612
  56.3 20.6 %copy-start = (f32[8,32,128]{2,1,0:T(8,128)S(1)}, f32[8,32,128]{2,1,0:T(8,128)}, u32[]{:S(2)}) copy-start(f32[8,32,128]{2,1,0:T(8,128)} %param.14) | copy-start | bytes 393220
  56.3 20.6 %copy-start.4 = (f32[128,512]{1,0:T(8,128)S(1)}, f32[128,512]{1,0:T(8,128)}, u32[]{:S(2)}) copy-start(f32[128,512]{1,0:T(8,128)} %tri_w.1) | copy-start | bytes 786436
  56.3 20.6 %all-to-all-start.1 = ((f32[8,48,128]{2,1,0:T(8,128)}), f32[8,48,128]{2,1,0:T(8,128)S(1)}, u32[]{:S(2)}, u32[]{:S(2)}) async-start(f32[8,48,128]{2,1,0:T(8,128)} %shard_map.153), calls=%async_computation.1 | async-start | bytes 393216 | tf_op jit(solution)/shard_map/all_to_all | solution.py:405
  98.4 1.5 %collective-permute-start.14 = (f32[128,4,128]{2,1,0:T(4,128)S(1)}, f32[128,4,128]{2,1,0:T(4,128)S(1)}, u32[]{:S(2)}, u32[]{:S(2)}) collective-permute-start(f32[128,4,128]{2,1,0:T(4,128)S(1)} %all_to_all.21), channel_id=1, source_target_pairs={{0,128},{128,0},{1,129},{129,1},{2,130},{130,2},{3,131},{131,3},{4... | collective-permute-start | bytes 786440 | tf_op jit(solution)/shard_map/ppermute | solution.py:413
  99.9 19.7 %copy-start.3 = (f32[512,128]{1,0:T(8,128)S(1)}, f32[512,128]{1,0:T(8,128)}, u32[]{:S(2)}) copy-start(f32[512,128]{1,0:T(8,128)} %last_w.1) | copy-start | bytes 786436
  99.9 19.7 %copy-start.6 = (f32[128,128]{1,0:T(8,128)S(1)}, f32[128,128]{1,0:T(8,128)}, u32[]{:S(2)}) copy-start(f32[128,128]{1,0:T(8,128)} %out_w.3) | copy-start | bytes 196612
  100.7 18.9 %copy-start.2 = (f32[128,512]{1,0:T(8,128)S(1)}, f32[128,512]{1,0:T(8,128)}, u32[]{:S(2)}) copy-start(f32[128,512]{1,0:T(8,128)} %in_w.1) | copy-start | bytes 786436

commit v6 on v5

--- a/solution.py
+++ b/solution.py
@@ -211,7 +211,7 @@
         merged[c, 32:48] = left_mask[c]
 
 
-def outer_kernel(row_of, col_of, factors, pair, residues, outer_w, tri_w, gate_w, pair_one, edge_send, gate_out, right_s, left_s, sum_s):
+def outer_kernel(branch_of, low_of, col_of, factors, pair, residues, outer_w, tri_w, gate_w, pair_one, edge_send, gate_out, right_s, left_s, sum_s):
     lane = iota((8, 128), 1)
     chunk = iota((32, 128), 1) // 32
     for group in range(4):
@@ -255,7 +255,7 @@
     present = residues[...]
     source, tile = iota((128, 256), 0), iota((128, 256), 1)
     valid = jnp.ones((8, 256), f32)
-    for target in (row_of[0] * 8 + tile // 32, col_of[0] * 32 + tile % 32):
+    for target in ((branch_of[0] * 16 + low_of[0]) * 8 + tile // 32, col_of[0] * 32 + tile % 32):
         picked = jnp.zeros((8, 256), f32)
         for half in range(2):
             chosen = (source + half * 128 == target).astype(f32)
@@ -351,7 +351,6 @@
     transit_out,
 ):
     branch = lax.axis_index("branch").astype(jnp.int32).reshape(1)
-    row = lax.axis_index(ROWS).astype(jnp.int32)
     col = lax.axis_index("pcol").astype(jnp.int32)
     pair = pair_rep.reshape(256, 128)
     align = alignment.reshape(32, 256)
@@ -407,8 +406,8 @@
         outer_kernel,
         [(256, 128), (128, 4, 128), (256, 128)],
         scratch=[pltpu.VMEM((128, 256), f32), pltpu.VMEM((32, 8, 256), f32), pltpu.VMEM((256, 1024), f32)],
-        scalars=2,
-    )(row.reshape(1), col.reshape(1), factors, pair, residues_near, outer_out, triangle_in, triangle_gate)
+        scalars=3,
+    )(branch, low, col.reshape(1), factors, pair, residues_near, outer_out, triangle_in, triangle_gate)
     own_edges = lax.all_to_all(edge_send, CHIPS, 0, 0, tiled=True)
     other_edges = lax.ppermute(own_edges, "branch", [(0, 1), (1, 0)])
     left_wide, tiles = call(

time: 123 us -> 120 us (0.976)
  blocking collectives: 51.9 us -> 71.4 us
  starting transfers between devices: 31.5 us -> 20.6 us
  waiting for transfers between devices: 24.1 us -> 13.5 us
    all_to_all x0 -> x1, blocking collectives: none -> 19.1 us  [shards(): factors = lax.all_to_all(factor_send, 'pcol', 0, 0, tiled=True)]
    all_to_all x1 -> x0, waiting for transfers between devices: 10.9 us -> none  [shards(): factors = lax.all_to_all(factor_send, 'pcol', 0, 0, tiled=True)]
    all_to_all x1 -> x0, starting transfers between devices: 9.67 us -> none  [shards(): factors = lax.all_to_all(factor_send, 'pcol', 0, 0, tiled=True)]
  transfers between devices with their start and end apart: 16 -> 15, of which waited for: 8 -> 7; matrix products, arithmetic and copies ran while one was open for 0% -> 0% of each run, Pallas kernels for 2% -> 3%
where the time goes in v6:
time: 120 us; the launch traced here: 119 us
  blocking collectives  71.4 us (60%)
  starting transfers between devices  20.6 us (17%)
  waiting for transfers between devices  13.5 us (11%)
  Pallas kernels  12.5 us (10%)
    ppermute x14, starting transfers between devices, swap(): return lax.ppermute(value, axis, [(d, d ^ step) for d in range(size)])  20.6 us
    all_to_all x1, blocking collectives, shards(): own_edges = lax.all_to_all(edge_send, CHIPS, 0, 0, tiled=True)  19.1 us
    all_to_all x1, blocking collectives, shards(): factors = lax.all_to_all(factor_send, 'pcol', 0, 0, tiled=True)  19.1 us
    all_to_all x1, blocking collectives, shards(): lax.all_to_all(cross_send.reshape(128, 2, 128), CHIPS, 0, 0, tiled=True)  18.9 us
    all_to_all x1, blocking collectives, shards(): right_all = lax.all_to_all(right_send, ROWS, 0, 0, tiled=True)  14.4 us
    ppermute x14, waiting for transfers between devices, swap(): return lax.ppermute(value, axis, [(d, d ^ step) for d in range(size)])  12.8 us
    pallas_call x9, Pallas kernels, run(): pl.pallas_call(kernel, out_shape=outs, in_specs=[smem] * scalars + [pl.Bl...  12.5 us
  transfers between devices with their start and end apart: 15, of which 7 were waited for; matrix products, arithmetic and copies ran while one was open for 0% of the time, Pallas kernels for 3%

profile of v6, /device:TPU:2, one launch (start us, length us, event | category | flops | bytes accessed | tf_op | source)
XLA Modules:
  0.0 118.9 jit_solution(5691627198983677386)
XLA Ops:
  0.6 1.7 %shard_map.149 = (f32[72,128]{1,0:T(8,128)S(1)}, f32[256,128]{1,0:T(8,128)S(1)}, f32[32,256]{1,0:T(8,128)S(1)}, f32[8,8]{1,0:T(8,128)S(1)}, f32[2,128]{1,0:T(2,128)S(1)}) custom-call(s32[1]{0:T(128)} %bitcast.2.low.low_of, f32[256,128]{1,0:T(8,128)} %bitcast.22, f32[32,256]{1,0:T(8,128)} %bitcast.36, s32[4,8]{1,0:T(4,128)} %mask.1, s32[2,128]{1,0:T(2,128)} %bitcast.38), custom_call_target="tpu_custom_call" | custom-call | tf_op jit(solution)/shard_map/pallas_call | solution.py:74
  2.3 4.7 %collective-permute-start.6 = (f32[72,128]{1,0:T(8,128)S(1)}, f32[72,128]{1,0:T(8,128)S(1)}, u32[]{:S(2)}, u32[]{:S(2)}) collective-permute-start(f32[72,128]{1,0:T(8,128)S(1)} %get-tuple-element.22), channel_id=1, source_target_pairs={{0,24},{8,16},{16,8},{24,0},{32,56},{40,48},{48,40},{56,32},{64,88... | collective-permute-start | bytes 110600 | tf_op jit(solution)/shard_map/ppermute | solution.py:370
  7.1 0.7 collective-permute-start.4
  7.7 1.5 %collective-permute-done.6 = f32[72,128]{1,0:T(8,128)S(1)} collective-permute-done((f32[72,128]{1,0:T(8,128)S(1)}, f32[72,128]{1,0:T(8,128)S(1)}, u32[]{:S(2)}, u32[]{:S(2)}) %collective-permute-start.6) | collective-permute-done | bytes 36896 | tf_op jit(solution)/shard_map/ppermute | solution.py:370
  9.2 2.7 %collective-permute-done.5 = f32[72,128]{1,0:T(8,128)S(1)} collective-permute-done((f32[72,128]{1,0:T(8,128)S(1)}, f32[72,128]{1,0:T(8,128)S(1)}, u32[]{:S(2)}, u32[]{:S(2)}) %collective-permute-start.5) | collective-permute-done | bytes 36896 | tf_op jit(solution)/shard_map/ppermute | solution.py:370
  11.9 1.6 %collective-permute-start.9 = (f32[4,72,128]{2,1,0:T(8,128)S(1)}, f32[4,72,128]{2,1,0:T(8,128)S(1)}, u32[]{:S(2)}, u32[]{:S(2)}) collective-permute-start(f32[4,72,128]{2,1,0:T(8,128)S(1)} %pad_maximum_fusion.refs_4_), channel_id=1, source_target_pairs={{0,96},{8,104},{16,112},{24,120},{32,64},{40,72},{48,80},{56,88},{... | collective-permute-start | bytes 442376 | tf_op jit(solution)/shard_map/ppermute | solution.py:370
  13.5 1.1 collective-permute-start.8
  14.6 1.5 %collective-permute-start.7 = (f32[4,72,128]{2,1,0:T(8,128)S(1)}, f32[4,72,128]{2,1,0:T(8,128)S(1)}, u32[]{:S(2)}, u32[]{:S(2)}) collective-permute-start(f32[4,72,128]{2,1,0:T(8,128)S(1)} %pad_maximum_fusion.refs_4_), channel_id=1, source_target_pairs={{0,32},{8,40},{16,48},{24,56},{32,0},{40,8},{48,16},{56,24},{64,96... | collective-permute-start | bytes 442376 | tf_op jit(solution)/shard_map/ppermute | solution.py:370
  16.1 0.3 shard_map.151
  16.4 4.7 %collective-permute-start = (f32[8,256]{1,0:T(8,128)S(1)}, f32[8,256]{1,0:T(8,128)S(1)}, u32[]{:S(2)}, u32[]{:S(2)}) collective-permute-start(f32[8,256]{1,0:T(8,128)S(1)} %shard_map.151), channel_id=1, source_target_pairs={{0,4},{1,5},{2,6},{3,7},{4,0},{5,1},{6,2},{7,3},{8,12},{9,13},{10,... | collective-permute-start | bytes 24584 | tf_op jit(solution)/shard_map/ppermute | solution.py:370
  21.1 0.5 collective-permute-start.13
  21.6 0.1 collective-permute-start.12
  21.7 0.4 collective-permute-start.11
  22.2 1.9 %collective-permute-done = f32[8,256]{1,0:T(8,128)S(1)} collective-permute-done((f32[8,256]{1,0:T(8,128)S(1)}, f32[8,256]{1,0:T(8,128)S(1)}, u32[]{:S(2)}, u32[]{:S(2)}) %collective-permute-start) | collective-permute-done | bytes 8224 | tf_op jit(solution)/shard_map/ppermute | solution.py:370
  24.1 3.0 %collective-permute-start.3 = (f32[2,8,256]{2,1,0:T(8,128)S(1)}, f32[2,8,256]{2,1,0:T(8,128)S(1)}, u32[]{:S(2)}, u32[]{:S(2)}) collective-permute-start(f32[2,8,256]{2,1,0:T(8,128)S(1)} %pad_maximum_fusion.1.refs_0_), channel_id=1, source_target_pairs={{0,3},{1,2},{2,1},{3,0},{4,7},{5,6},{6,5},{7,4},{8,11},{9,10},{10,... | collective-permute-start | bytes 49160 | tf_op jit(solution)/shard_map/ppermute | solution.py:370
  27.1 1.9 %collective-permute-done.3.refs_3_ = f32[2,8,256]{2,1,0:T(8,128)S(1)} collective-permute-done((f32[2,8,256]{2,1,0:T(8,128)S(1)}, f32[2,8,256]{2,1,0:T(8,128)S(1)}, u32[]{:S(2)}, u32[]{:S(2)}) %collective-permute-start.3) | collective-permute-done | bytes 16416 | tf_op jit(solution)/shard_map/ppermute | solution.py:370
  29.0 2.0 %collective-permute-start.2 = (f32[2,8,256]{2,1,0:T(8,128)S(1)}, f32[2,8,256]{2,1,0:T(8,128)S(1)}, u32[]{:S(2)}, u32[]{:S(2)}) collective-permute-start(f32[2,8,256]{2,1,0:T(8,128)S(1)} %pad_maximum_fusion.1.refs_0_), channel_id=1, source_target_pairs={{0,2},{1,3},{2,0},{3,1},{4,6},{5,7},{6,4},{7,5},{8,10},{9,11},{10,... | collective-permute-start | bytes 49160 | tf_op jit(solution)/shard_map/ppermute | solution.py:370
  31.0 3.3 %collective-permute-done.2.refs_2_ = f32[2,8,256]{2,1,0:T(8,128)S(1)} collective-permute-done((f32[2,8,256]{2,1,0:T(8,128)S(1)}, f32[2,8,256]{2,1,0:T(8,128)S(1)}, u32[]{:S(2)}, u32[]{:S(2)}) %collective-permute-start.2) | collective-permute-done | bytes 16416 | tf_op jit(solution)/shard_map/ppermute | solution.py:370
  34.3 0.4 collective-permute-start.1
  34.6 1.9 %shard_map.150 = (f32[256,256]{1,0:T(8,128)S(1)}, f32[32,256]{1,0:T(8,128)S(1)}) custom-call(f32[256,1024]{1,0:T(8,128)} %proj.3, f32[32,256]{1,0:T(8,128)S(1)} %get-tuple-element.17.align), custom_call_target="tpu_custom_call" | custom-call | tf_op jit(solution)/shard_map/pallas_call | solution.py:74
  36.6 1.5 %collective-permute-done.1.refs_1_ = f32[2,8,256]{2,1,0:T(8,128)S(1)} collective-permute-done((f32[2,8,256]{2,1,0:T(8,128)S(1)}, f32[2,8,256]{2,1,0:T(8,128)S(1)}, u32[]{:S(2)}, u32[]{:S(2)}) %collective-permute-start.1) | collective-permute-done | bytes 16416 | tf_op jit(solution)/shard_map/ppermute | solution.py:370
  38.0 2.8 %shard_map.152 = (f32[32,256]{1,0:T(8,128)}, f32[32,8,128]{2,1,0:T(8,128)S(1)}, f32[8,16,128]{2,1,0:T(8,128)S(1)}) custom-call(s32[1]{0:T(128)} %bitcast.branch_of, s32[1]{0:T(128)} %bitcast.1.col_of, s32[1]{0:T(128)} %bitcast.2.low.low_of, f32[256,1024]{1,0:T(8,128)} %proj.3, f32[256,256]{1,0:T(8,128)} %out_w.2, f32[64,256]{1,0:T(8,128)} %bitcast.32, ...), custom_call_target="tpu_custom_call" | custom-call | tf_op jit(solution)/shard_map/pallas_call | solution.py:74
  40.9 14.4 %all_to_all.20 = f32[32,8,128]{2,1,0:T(8,128)S(1)} all-to-all(f32[32,8,128]{2,1,0:T(8,128)S(1)} %get-tuple-element.24), channel_id=1, replica_groups=mesh['branch'=2,'prow'=16,'pcol'=8] {'branch','prow'}, dimensions={0} | all-to-all | bytes 262144 | tf_op jit(solution)/shard_map/all_to_all | solution.py:402
  55.3 0.0 copy-start
  55.3 19.1 %all_to_all.21.factors = f32[8,48,128]{2,1,0:T(8,128)S(1)} all-to-all(f32[8,48,128]{2,1,0:T(8,128)S(1)} %shard_map.153), channel_id=1, replica_groups=mesh['branch'=2,'prow'=16,'pcol'=8] {'pcol'}, dimensions={0} | all-to-all | bytes 393216 | tf_op jit(solution)/shard_map/all_to_all | solution.py:404
  74.4 2.4 %shard_map.154 = (f32[256,128]{1,0:T(8,128)S(1)}, f32[128,4,128]{2,1,0:T(4,128)S(1)}, f32[256,128]{1,0:T(8,128)S(1)}) custom-call(s32[1]{0:T(128)} %bitcast.branch_of, s32[1]{0:T(128)} %bitcast.2.low.low_of, s32[1]{0:T(128)} %bitcast.1.col_of, f32[8,48,128]{2,1,0:T(8,128)S(1)} %all_to_all.21.factors, f32[256,128]{1,0:T(8,128)S(1)} %bitcast.23, ...), custom_call_target="tpu_custom_call" | custom-call | tf_op jit(solution)/shard_map/pallas_call | solution.py:74
  76.7 19.1 %all_to_all.22 = f32[128,4,128]{2,1,0:T(4,128)S(1)} all-to-all(f32[128,4,128]{2,1,0:T(4,128)S(1)} %get-tuple-element.27), channel_id=1, replica_groups=mesh['branch'=2,'prow'=16,'pcol'=8] {'prow','pcol'}, dimensions={0} | all-to-all | bytes 524288 | tf_op jit(solution)/shard_map/all_to_all | solution.py:411
  95.9 0.8 shard_map.155
  96.7 0.7 collective-permute-done.14
  97.4 0.8 shard_map.156
  98.2 18.9 %all_to_all.23 = f32[128,2,128]{2,1,0:T(2,128)S(1)} all-to-all(f32[128,2,128]{2,1,0:T(2,128)S(1)} %bitcast.24), channel_id=1, replica_groups=mesh['branch'=2,'prow'=16,'pcol'=8] {'prow','pcol'}, dimensions={0} | all-to-all | bytes 262144 | tf_op jit(solution)/shard_map/all_to_all | solution.py:419
  117.1 1.8 %shard_map.157 = f32[256,128]{1,0:T(8,128)} custom-call(f32[256,128]{1,0:T(8,128)S(1)} %bitcast.25, f32[256,128]{1,0:T(8,128)S(1)} %get-tuple-element.30.pair_one, f32[256,128]{1,0:T(8,128)S(1)} %get-tuple-element.31.gate, f32[128,128]{1,0:T(8,128)S(1)} %copy-done.6, f32[128,512]{1,0:T(8,128)S(1)} %copy-done.2, f32[512,128]{1,0:T(8,128)S(1)} %copy-done.3), custom_call_target="tpu_custom_call" | custom-call | tf_op jit(solution)/shard_map/pallas_call | solution.py:74
  (29 shorter events, 0.1 us)
Async XLA Ops:
  2.3 6.9 %collective-permute-start.6 = (f32[72,128]{1,0:T(8,128)S(1)}, f32[72,128]{1,0:T(8,128)S(1)}, u32[]{:S(2)}, u32[]{:S(2)}) collective-permute-start(f32[72,128]{1,0:T(8,128)S(1)} %get-tuple-element.22), channel_id=1, source_target_pairs={{0,24},{8,16},{16,8},{24,0},{32,56},{40,48},{48,40},{56,32},{64,88... | collective-permute-start | bytes 110600 | tf_op jit(solution)/shard_map/ppermute | solution.py:370
  7.0 4.9 %collective-permute-start.5 = (f32[72,128]{1,0:T(8,128)S(1)}, f32[72,128]{1,0:T(8,128)S(1)}, u32[]{:S(2)}, u32[]{:S(2)}) collective-permute-start(f32[72,128]{1,0:T(8,128)S(1)} %get-tuple-element.22), channel_id=1, source_target_pairs={{0,16},{8,24},{16,0},{24,8},{32,48},{40,56},{48,32},{56,40},{64,80... | collective-permute-start | bytes 110600 | tf_op jit(solution)/shard_map/ppermute | solution.py:370
  7.1 4.9 %collective-permute-start.4 = (f32[72,128]{1,0:T(8,128)S(1)}, f32[72,128]{1,0:T(8,128)S(1)}, u32[]{:S(2)}, u32[]{:S(2)}) collective-permute-start(f32[72,128]{1,0:T(8,128)S(1)} %get-tuple-element.22), channel_id=1, source_target_pairs={{0,8},{8,0},{16,24},{24,16},{32,40},{40,32},{48,56},{56,48},{64,72... | collective-permute-start | bytes 110600 | tf_op jit(solution)/shard_map/ppermute | solution.py:370
  11.9 4.2 %copy-start.7 = (f32[128,8]{0,1:T(8,128)S(1)}, f32[128,8]{0,1:T(8,128)}, u32[]{:S(2)}) copy-start(f32[128,8]{0,1:T(8,128)} %param.19) | copy-start | bytes 12292
  11.9 9.2 %collective-permute-start.9 = (f32[4,72,128]{2,1,0:T(8,128)S(1)}, f32[4,72,128]{2,1,0:T(8,128)S(1)}, u32[]{:S(2)}, u32[]{:S(2)}) collective-permute-start(f32[4,72,128]{2,1,0:T(8,128)S(1)} %pad_maximum_fusion.refs_4_), channel_id=1, source_target_pairs={{0,96},{8,104},{16,112},{24,120},{32,64},{40,72},{48,80},{56,88},{... | collective-permute-start | bytes 442376 | tf_op jit(solution)/shard_map/ppermute | solution.py:370
  13.5 8.1 %collective-permute-start.8 = (f32[4,72,128]{2,1,0:T(8,128)S(1)}, f32[4,72,128]{2,1,0:T(8,128)S(1)}, u32[]{:S(2)}, u32[]{:S(2)}) collective-permute-start(f32[4,72,128]{2,1,0:T(8,128)S(1)} %pad_maximum_fusion.refs_4_), channel_id=1, source_target_pairs={{0,64},{8,72},{16,80},{24,88},{32,96},{40,104},{48,112},{56,120},{... | collective-permute-start | bytes 442376 | tf_op jit(solution)/shard_map/ppermute | solution.py:370
  14.6 7.1 %collective-permute-start.7 = (f32[4,72,128]{2,1,0:T(8,128)S(1)}, f32[4,72,128]{2,1,0:T(8,128)S(1)}, u32[]{:S(2)}, u32[]{:S(2)}) collective-permute-start(f32[4,72,128]{2,1,0:T(8,128)S(1)} %pad_maximum_fusion.refs_4_), channel_id=1, source_target_pairs={{0,32},{8,40},{16,48},{24,56},{32,0},{40,8},{48,16},{56,24},{64,96... | collective-permute-start | bytes 442376 | tf_op jit(solution)/shard_map/ppermute | solution.py:370
  16.4 7.6 %collective-permute-start = (f32[8,256]{1,0:T(8,128)S(1)}, f32[8,256]{1,0:T(8,128)S(1)}, u32[]{:S(2)}, u32[]{:S(2)}) collective-permute-start(f32[8,256]{1,0:T(8,128)S(1)} %shard_map.151), channel_id=1, source_target_pairs={{0,4},{1,5},{2,6},{3,7},{4,0},{5,1},{6,2},{7,3},{8,12},{9,13},{10,... | collective-permute-start | bytes 24584 | tf_op jit(solution)/shard_map/ppermute | solution.py:370
  21.1 16.9 %collective-permute-start.10 = (f32[4,72,128]{2,1,0:T(8,128)S(1)}, f32[4,72,128]{2,1,0:T(8,128)S(1)}, u32[]{:S(2)}, u32[]{:S(2)}) collective-permute-start(f32[4,72,128]{2,1,0:T(8,128)S(1)} %pad_maximum_fusion.refs_4_), channel_id=1, source_target_pairs={{0,128},{128,0},{1,129},{129,1},{2,130},{130,2},{3,131},{131,3},{4... | collective-permute-start | bytes 442376 | tf_op jit(solution)/shard_map/ppermute | solution.py:370
  21.1 16.9 %collective-permute-start.13 = (f32[4,72,128]{2,1,0:T(8,128)S(1)}, f32[4,72,128]{2,1,0:T(8,128)S(1)}, u32[]{:S(2)}, u32[]{:S(2)}) collective-permute-start(f32[4,72,128]{2,1,0:T(8,128)S(1)} %collective-permute-done.9.refs_7_), channel_id=1, source_target_pairs={{0,128},{128,0},{1,129},{129,1},{2,130},{130,2},{3,131},{131,3},{4... | collective-permute-start | bytes 442376 | tf_op jit(solution)/shard_map/ppermute | solution.py:370
  21.6 16.4 %collective-permute-start.12 = (f32[4,72,128]{2,1,0:T(8,128)S(1)}, f32[4,72,128]{2,1,0:T(8,128)S(1)}, u32[]{:S(2)}, u32[]{:S(2)}) collective-permute-start(f32[4,72,128]{2,1,0:T(8,128)S(1)} %collective-permute-done.8.refs_6_), channel_id=1, source_target_pairs={{0,128},{128,0},{1,129},{129,1},{2,130},{130,2},{3,131},{131,3},{4... | collective-permute-start | bytes 442376 | tf_op jit(solution)/shard_map/ppermute | solution.py:370
  21.7 16.3 %collective-permute-start.11 = (f32[4,72,128]{2,1,0:T(8,128)S(1)}, f32[4,72,128]{2,1,0:T(8,128)S(1)}, u32[]{:S(2)}, u32[]{:S(2)}) collective-permute-start(f32[4,72,128]{2,1,0:T(8,128)S(1)} %collective-permute-done.7.refs_5_), channel_id=1, source_target_pairs={{0,128},{128,0},{1,129},{129,1},{2,130},{130,2},{3,131},{131,3},{4... | collective-permute-start | bytes 442376 | tf_op jit(solution)/shard_map/ppermute | solution.py:370
  24.1 4.9 %collective-permute-start.3 = (f32[2,8,256]{2,1,0:T(8,128)S(1)}, f32[2,8,256]{2,1,0:T(8,128)S(1)}, u32[]{:S(2)}, u32[]{:S(2)}) collective-permute-start(f32[2,8,256]{2,1,0:T(8,128)S(1)} %pad_maximum_fusion.1.refs_0_), channel_id=1, source_target_pairs={{0,3},{1,2},{2,1},{3,0},{4,7},{5,6},{6,5},{7,4},{8,11},{9,10},{10,... | collective-permute-start | bytes 49160 | tf_op jit(solution)/shard_map/ppermute | solution.py:370
  29.0 5.2 %collective-permute-start.2 = (f32[2,8,256]{2,1,0:T(8,128)S(1)}, f32[2,8,256]{2,1,0:T(8,128)S(1)}, u32[]{:S(2)}, u32[]{:S(2)}) collective-permute-start(f32[2,8,256]{2,1,0:T(8,128)S(1)} %pad_maximum_fusion.1.refs_0_), channel_id=1, source_target_pairs={{0,2},{1,3},{2,0},{3,1},{4,6},{5,7},{6,4},{7,5},{8,10},{9,11},{10,... | collective-permute-start | bytes 49160 | tf_op jit(solution)/shard_map/ppermute | solution.py:370
  34.3 3.7 %collective-permute-start.1 = (f32[2,8,256]{2,1,0:T(8,128)S(1)}, f32[2,8,256]{2,1,0:T(8,128)S(1)}, u32[]{:S(2)}, u32[]{:S(2)}) collective-permute-start(f32[2,8,256]{2,1,0:T(8,128)S(1)} %pad_maximum_fusion.1.refs_0_), channel_id=1, source_target_pairs={{0,1},{1,0},{2,3},{3,2},{4,5},{5,4},{6,7},{7,6},{8,9},{9,8},{10,11... | collective-permute-start | bytes 49160 | tf_op jit(solution)/shard_map/ppermute | solution.py:370
  40.9 33.5 %copy-start.1 = (f32[1024,128]{1,0:T(8,128)S(1)}, f32[1024,128]{1,0:T(8,128)}, u32[]{:S(2)}) copy-start(f32[1024,128]{1,0:T(8,128)} %outer_w.1) | copy-start | bytes 1572868
  55.3 19.1 %copy-start.5 = (f32[128,128]{1,0:T(8,128)S(1)}, f32[128,128]{1,0:T(8,128)}, u32[]{:S(2)}) copy-start(f32[128,128]{1,0:T(8,128)} %gate_w.1) | copy-start | bytes 196612
  55.3 19.1 %copy-start = (f32[8,32,128]{2,1,0:T(8,128)S(1)}, f32[8,32,128]{2,1,0:T(8,128)}, u32[]{:S(2)}) copy-start(f32[8,32,128]{2,1,0:T(8,128)} %param.14) | copy-start | bytes 393220
  55.3 19.1 %copy-start.4 = (f32[128,512]{1,0:T(8,128)S(1)}, f32[128,512]{1,0:T(8,128)}, u32[]{:S(2)}) copy-start(f32[128,512]{1,0:T(8,128)} %tri_w.1) | copy-start | bytes 786436
  95.9 1.5 %collective-permute-start.14 = (f32[128,4,128]{2,1,0:T(4,128)S(1)}, f32[128,4,128]{2,1,0:T(4,128)S(1)}, u32[]{:S(2)}, u32[]{:S(2)}) collective-permute-start(f32[128,4,128]{2,1,0:T(4,128)S(1)} %all_to_all.22), channel_id=1, source_target_pairs={{0,128},{128,0},{1,129},{129,1},{2,130},{130,2},{3,131},{131,3},{4... | collective-permute-start | bytes 786440 | tf_op jit(solution)/shard_map/ppermute | solution.py:412
  97.4 19.7 %copy-start.3 = (f32[512,128]{1,0:T(8,128)S(1)}, f32[512,128]{1,0:T(8,128)}, u32[]{:S(2)}) copy-start(f32[512,128]{1,0:T(8,128)} %last_w.1) | copy-start | bytes 786436
  97.4 19.7 %copy-start.6 = (f32[128,128]{1,0:T(8,128)S(1)}, f32[128,128]{1,0:T(8,128)}, u32[]{:S(2)}) copy-start(f32[128,128]{1,0:T(8,128)} %out_w.3) | copy-start | bytes 196612
  98.2 18.9 %copy-start.2 = (f32[128,512]{1,0:T(8,128)S(1)}, f32[128,512]{1,0:T(8,128)}, u32[]{:S(2)}) copy-start(f32[128,512]{1,0:T(8,128)} %in_w.1) | copy-start | bytes 786436
